TPU v7x, 32 devices: a whole 2x2x4 slice. The times are simulated.
32 devices in a mesh: dp: 8 (over y, x, core), mp: 4 (over z).
Axes of the slice: x: 2, y: 2, z: 4, core: 2. Of those that a mesh axis runs over, the one named last changes fastest.
Arguments:
- tokens: bfloat16 [64, 1280, 768], P(('dp', 'mp')), may hold values from -6 to 6
- image_ids: int32 [64, 1280], P(('dp', 'mp')), may hold values from -1 to 1, as said below
- selected: int32 [64, 1280], P(('dp', 'mp')), may hold values from 0 to 1, as said below
- cotangent: bfloat16 [64, 1280, 768], P(('dp', 'mp')), may hold values from -6 to 6
- qkv_weight: float32 [768, 2304], P(('dp', 'mp')), may hold values from -0.21875 to 0.21875
- qkv_first: float32 [768, 2304], P(('dp', 'mp')), may hold values from -24 to 24
- qkv_second: float32 [768, 2304], P(('dp', 'mp')), may hold values from 1.6384 to 6.5536
- proj_weight: float32 [768, 768], P(('dp', 'mp')), may hold values from -1.75 to 1.75
- proj_first: float32 [768, 768], P(('dp', 'mp')), may hold values from -24 to 24
- proj_second: float32 [768, 768], P(('dp', 'mp')), may hold values from 1.6384 to 6.5536
- up_weight: float32 [768, 3072], P('dp', 'mp'), may hold values from -0.21875 to 0.21875
- up_first: float32 [768, 3072], P('dp', 'mp'), may hold values from -24 to 24
- up_second: float32 [768, 3072], P('dp', 'mp'), may hold values from 1.6384 to 6.5536
- down_weight: float32 [3072, 768], P('mp', 'dp'), may hold values from -0.109375 to 0.109375
- down_first: float32 [3072, 768], P('mp', 'dp'), may hold values from -24 to 24
- down_second: float32 [3072, 768], P('mp', 'dp'), may hold values from 1.6384 to 6.5536
- up_bias: float32 [3072], replicated, may hold values from -3 to 3
- bias_first: float32 [3072], replicated, may hold values from -32 to 32
- bias_second: float32 [3072], replicated, may hold values from 4.096 to 16.384
- vectors: float32 [7, 768], replicated, may hold values from -4 to 4, as said below
- vector_first: float32 [7, 768], replicated, may hold values from -62.334817 to 62.334817
- vector_second: float32 [7, 768], replicated, may hold values from 2.6133333 to 80.2816, as said below
Outputs:
- block_output: bfloat16 [64, 1280, 768], P(('dp', 'mp'))
- input_grad: float32 [64, 1280, 768], P(('dp', 'mp'))
- weight_norms: float32 [2, 4], replicated
- qkv_new: float32 [768, 2304], P(('dp', 'mp'))
- qkv_first_new: float32 [768, 2304], P(('dp', 'mp'))
- qkv_second_new: float32 [768, 2304], P(('dp', 'mp'))
- proj_new: float32 [768, 768], P(('dp', 'mp'))
- proj_first_new: float32 [768, 768], P(('dp', 'mp'))
- proj_second_new: float32 [768, 768], P(('dp', 'mp'))
- up_new: float32 [768, 3072], P('dp', 'mp')
- up_first_new: float32 [768, 3072], P('dp', 'mp')
- up_second_new: float32 [768, 3072], P('dp', 'mp')
- down_new: float32 [3072, 768], P('mp', 'dp')
- down_first_new: float32 [3072, 768], P('mp', 'dp')
- down_second_new: float32 [3072, 768], P('mp', 'dp')
- bias_new: float32 [3072], replicated
- bias_first_new: float32 [3072], replicated
- bias_second_new: float32 [3072], replicated
- vectors_new: float32 [7, 768], replicated
- vector_first_new: float32 [7, 768], replicated
- vector_second_new: float32 [7, 768], replicated
Inputs may be any that keep to these rules, and one draw needn't show every extreme that they name: `image_ids`: each row holds one or two whole images of 577 patches, one after the other from some position of the row, numbered 0 and 1 in order; all other positions are padding -1; some row holds two and some row one. `selected`: each row has exactly 640 ones. `vectors`: gains lie between 0.7 and 1.3. `vector_second`: all entries are positive.
All inputs are finite; a program needn't handle non-finite values.
Results may differ from a plain program's by a relative error of at most 0.0095.
Values may be sent and summed in bfloat16 or wider, within the bound.
No kernel may reach another device: no remote copies, remote signals or barrier semaphores. Data moves between devices by JAX's collectives and lax.ppermute only.
A program may use at most 256 MiB of HBM per device.

v0:
```python
from functools import partial
import math

import jax
import jax.numpy as jnp
from jax import lax
from jax.sharding import PartitionSpec as P

D = 768
HEADS = 12
HEAD_DIM = 64
CAP = 640
STEP = 10


eps_norm = 1e-06
eps_adam = 1e-06
beta_one = 0.9
beta_two = 0.999
decay_mat = 0.01
rate_lamb = 0.3
masked_score = -1e30


def layer_norm(values, gain, shift):
    center = jnp.mean(values, -1, keepdims=True)
    offset = values - center
    spread = jnp.mean(offset * offset, -1, keepdims=True)
    return offset * lax.rsqrt(spread + eps_norm) * gain + shift


def to_heads(packed, row_count):
    shaped = packed.reshape(row_count, CAP, HEADS, HEAD_DIM)
    return shaped.transpose(0, 2, 1, 3).reshape(row_count * HEADS, CAP, HEAD_DIM)


def from_heads(split_rows, row_count):
    shaped = split_rows.reshape(row_count, HEADS, CAP, HEAD_DIM)
    return shaped.transpose(0, 2, 1, 3).reshape(row_count * CAP, HEADS * HEAD_DIM)


def head_scores(queries, key_rows, image_marks):
    scores = jnp.dot(queries, key_rows.T, preferred_element_type=jnp.float32) * (
        1.0 / math.sqrt(HEAD_DIM)
    )
    allowed = image_marks[:, None] == image_marks[None, :]
    return jnp.where(allowed, scores, masked_score)


def attend_forward(item):
    queries, key_rows, values, image_marks = item
    scores = head_scores(queries, key_rows, image_marks)
    row_max = jnp.max(scores, -1, keepdims=True)
    row_total = jnp.sum(jnp.exp(scores - row_max), -1, keepdims=True)
    log_total = row_max + jnp.log(row_total)
    probs_low = jnp.exp(scores - log_total).astype(jnp.bfloat16)
    return (jnp.dot(probs_low, values, preferred_element_type=jnp.float32), log_total)


def attend_backward(item):
    queries, key_rows, values, image_marks, log_total, context_grad = item
    scores = head_scores(queries, key_rows, image_marks)
    attn_probs = jnp.exp(scores - log_total)
    probs_low = attn_probs.astype(jnp.bfloat16)
    value_grad = jnp.dot(probs_low.T, context_grad, preferred_element_type=jnp.float32)
    probs_grad = jnp.dot(context_grad, values.T, preferred_element_type=jnp.float32)
    row_delta = jnp.sum(attn_probs * probs_grad, -1, keepdims=True)
    score_grad = (attn_probs * (probs_grad - row_delta)).astype(jnp.bfloat16)
    score_scale = 1.0 / math.sqrt(HEAD_DIM)
    query_grad = jnp.dot(score_grad, key_rows, preferred_element_type=jnp.float32) * score_scale
    key_grad = jnp.dot(score_grad.T, queries, preferred_element_type=jnp.float32) * score_scale
    return (query_grad, key_grad, value_grad)


def place_rows(base, picked, new_rows):

    def place_one(base_row, pick_row, value_row):
        return base_row.at[pick_row].set(value_row)

    return jax.vmap(place_one)(base, picked, new_rows)


def lamb_moments(weight, gradient, first_mom, second_mom, decay):
    first_new = beta_one * first_mom + (1.0 - beta_one) * gradient
    second_new = beta_two * second_mom + (1.0 - beta_two) * gradient * gradient
    update = (
        first_new
        / (1.0 - beta_one**STEP)
        / (jnp.sqrt(second_new / (1.0 - beta_two**STEP)) + eps_adam)
        + decay * weight
    )
    return (first_new, second_new, update)


def on_device(
    tokens,
    image_ids,
    selected,
    cotangent,
    qkv_weight,
    qkv_first,
    qkv_second,
    proj_weight,
    proj_first,
    proj_second,
    up_weight,
    up_first,
    up_second,
    down_weight,
    down_first,
    down_second,
    up_bias,
    bias_first,
    bias_second,
    vectors,
    vector_first,
    vector_second,
):
    qkv_mat, proj_mat = (
        lax.all_gather(qkv_weight.astype(jnp.bfloat16), ("dp", "mp"), axis=0, tiled=True),
        lax.all_gather(proj_weight.astype(jnp.bfloat16), ("dp", "mp"), axis=0, tiled=True),
    )
    up_mat, down_mat = (
        lax.all_gather(up_weight.astype(jnp.bfloat16), "dp", axis=0, tiled=True),
        lax.all_gather(down_weight.astype(jnp.bfloat16), "dp", axis=1, tiled=True),
    )
    row_count = tokens.shape[0]
    router_scale = 1.0 / math.sqrt(D)
    picked = jnp.argsort(1 - selected, axis=-1, stable=True)[:, :CAP]
    inputs = (
        jnp.take_along_axis(tokens, picked[:, :, None], axis=1)
        .astype(jnp.float32)
        .reshape(row_count * CAP, D)
    )
    image_marks = jnp.take_along_axis(image_ids, picked, axis=1)
    upstream = (
        jnp.take_along_axis(cotangent, picked[:, :, None], axis=1)
        .astype(jnp.float32)
        .reshape(row_count * CAP, D)
    )
    normed, norm_one_back = jax.vjp(layer_norm, inputs, vectors[0], vectors[1])
    normed_low = normed.astype(jnp.bfloat16)
    qkv_all = jnp.dot(normed_low, qkv_mat, preferred_element_type=jnp.float32).astype(jnp.bfloat16)
    queries = to_heads(qkv_all[:, :D], row_count)
    key_rows = to_heads(qkv_all[:, D : 2 * D], row_count)
    values = to_heads(qkv_all[:, 2 * D :], row_count)
    head_marks = jnp.repeat(image_marks, HEADS, axis=0)
    context_heads, log_totals = lax.map(attend_forward, (queries, key_rows, values, head_marks))
    context = from_heads(context_heads, row_count).astype(jnp.bfloat16)
    attended = jnp.dot(context, proj_mat, preferred_element_type=jnp.float32) + vectors[5]
    hidden_res = inputs + attended
    normed_two, norm_two_back = jax.vjp(layer_norm, hidden_res, vectors[2], vectors[3])
    normed_two_low = normed_two.astype(jnp.bfloat16)
    gelu_exact = partial(jax.nn.gelu, approximate=False)
    up_full, down_full = (
        lax.all_gather(up_mat, "mp", axis=1, tiled=True),
        lax.all_gather(down_mat, "mp", axis=0, tiled=True),
    )
    pre_act = jnp.dot(normed_two_low, up_full, preferred_element_type=jnp.float32) + up_bias
    activated, gelu_back = jax.vjp(gelu_exact, pre_act)
    activated_low = activated.astype(jnp.bfloat16)
    mlp_out = jnp.dot(activated_low, down_full, preferred_element_type=jnp.float32) + vectors[6]
    branch_sum = attended + mlp_out
    gating = jax.nn.sigmoid(jnp.sum(inputs * vectors[4], -1, keepdims=True) * router_scale)
    result = inputs + gating * branch_sum
    block_output = place_rows(
        tokens, picked, result.reshape(row_count, CAP, D).astype(jnp.bfloat16)
    )
    gate_grad = (
        jnp.sum(upstream * branch_sum, -1, keepdims=True) * gating * (1.0 - gating) * router_scale
    )
    branch_grad = upstream * gating
    input_total = upstream + gate_grad * vectors[4]
    router_grad = jnp.sum(inputs * gate_grad, 0)
    mlp_grad_low = branch_grad.astype(jnp.bfloat16)
    down_bias_grad = jnp.sum(mlp_grad_low.astype(jnp.float32), 0)
    act_grad = jnp.dot(mlp_grad_low, down_full.T, preferred_element_type=jnp.float32)
    pre_grad_low = gelu_back(act_grad)[0].astype(jnp.bfloat16)
    bias_grad = jnp.sum(pre_grad_low.astype(jnp.float32), 0)
    up_grad_full = jnp.dot(normed_two_low.T, pre_grad_low, preferred_element_type=jnp.float32)
    down_grad_full = jnp.dot(activated_low.T, mlp_grad_low, preferred_element_type=jnp.float32)
    up_grad, down_grad = (
        lax.psum_scatter(up_grad_full, "mp", scatter_dimension=1, tiled=True),
        lax.psum_scatter(down_grad_full, "mp", scatter_dimension=0, tiled=True),
    )
    normed_grad = jnp.dot(pre_grad_low, up_full.T, preferred_element_type=jnp.float32)
    hidden_grad, gain_two, shift_two = norm_two_back(normed_grad)
    input_total = input_total + hidden_grad
    attended_grad = (branch_grad + hidden_grad).astype(jnp.bfloat16)
    proj_bias_grad = jnp.sum(attended_grad.astype(jnp.float32), 0)
    proj_grad = jnp.dot(context.T, attended_grad, preferred_element_type=jnp.float32)
    context_grad = to_heads(
        jnp.dot(attended_grad, proj_mat.T, preferred_element_type=jnp.float32).astype(jnp.bfloat16),
        row_count,
    )
    query_grad, key_grad, value_grad = lax.map(
        attend_backward, (queries, key_rows, values, head_marks, log_totals, context_grad)
    )
    qkv_grad_low = jnp.concatenate(
        [
            from_heads(query_grad, row_count),
            from_heads(key_grad, row_count),
            from_heads(value_grad, row_count),
        ],
        axis=1,
    ).astype(jnp.bfloat16)
    qkv_grad = jnp.dot(normed_low.T, qkv_grad_low, preferred_element_type=jnp.float32)
    normed_grad_one = jnp.dot(qkv_grad_low, qkv_mat.T, preferred_element_type=jnp.float32)
    input_one, gain_one, shift_one = norm_one_back(normed_grad_one)
    input_total = input_total + input_one
    input_grad = place_rows(
        cotangent.astype(jnp.float32), picked, input_total.reshape(row_count, CAP, D)
    )
    qkv_sum, proj_sum = (
        lax.psum_scatter(qkv_grad, ("dp", "mp"), scatter_dimension=0, tiled=True),
        lax.psum_scatter(proj_grad, ("dp", "mp"), scatter_dimension=0, tiled=True),
    )
    up_sum, down_sum = (
        lax.psum_scatter(up_grad, "dp", scatter_dimension=0, tiled=True),
        lax.psum_scatter(down_grad, "dp", scatter_dimension=1, tiled=True),
    )
    vector_grad = jnp.stack(
        [gain_one, shift_one, gain_two, shift_two, router_grad, proj_bias_grad, down_bias_grad]
    )
    vector_sum, bias_sum = lax.psum((vector_grad, bias_grad), ("dp", "mp"))
    qkv_first_new, qkv_second_new, qkv_upd = lamb_moments(
        qkv_weight, qkv_sum, qkv_first, qkv_second, decay_mat
    )
    proj_first_new, proj_second_new, proj_upd = lamb_moments(
        proj_weight, proj_sum, proj_first, proj_second, decay_mat
    )
    up_first_new, up_second_new, up_upd = lamb_moments(
        up_weight, up_sum, up_first, up_second, decay_mat
    )
    down_first_new, down_second_new, down_upd = lamb_moments(
        down_weight, down_sum, down_first, down_second, decay_mat
    )
    squares = jnp.stack(
        [
            jnp.sum(qkv_weight * qkv_weight),
            jnp.sum(proj_weight * proj_weight),
            jnp.sum(up_weight * up_weight),
            jnp.sum(down_weight * down_weight),
            jnp.sum(qkv_upd * qkv_upd),
            jnp.sum(proj_upd * proj_upd),
            jnp.sum(up_upd * up_upd),
            jnp.sum(down_upd * down_upd),
        ]
    )
    weight_norms = jnp.sqrt(lax.psum(squares, ("dp", "mp"))).reshape(2, 4)
    ratios = weight_norms[0] / weight_norms[1]
    qkv_new = qkv_weight - rate_lamb * ratios[0] * qkv_upd
    proj_new = proj_weight - rate_lamb * ratios[1] * proj_upd
    up_new = up_weight - rate_lamb * ratios[2] * up_upd
    down_new = down_weight - rate_lamb * ratios[3] * down_upd
    bias_first_new, bias_second_new, bias_upd = lamb_moments(
        up_bias, bias_sum, bias_first, bias_second, 0.0
    )
    bias_ratio = jnp.sqrt(jnp.sum(up_bias * up_bias)) / jnp.sqrt(jnp.sum(bias_upd * bias_upd))
    bias_new = up_bias - rate_lamb * bias_ratio * bias_upd
    vector_first_new, vector_second_new, vector_upd = lamb_moments(
        vectors, vector_sum, vector_first, vector_second, 0.0
    )
    vector_ratio = jnp.sqrt(jnp.sum(vectors * vectors, -1, keepdims=True)) / jnp.sqrt(
        jnp.sum(vector_upd * vector_upd, -1, keepdims=True)
    )
    vectors_new = vectors - rate_lamb * vector_ratio * vector_upd
    return (
        block_output,
        input_grad,
        weight_norms,
        qkv_new,
        qkv_first_new,
        qkv_second_new,
        proj_new,
        proj_first_new,
        proj_second_new,
        up_new,
        up_first_new,
        up_second_new,
        down_new,
        down_first_new,
        down_second_new,
        bias_new,
        bias_first_new,
        bias_second_new,
        vectors_new,
        vector_first_new,
        vector_second_new,
    )


def solution(mesh):
    in_specs = (
        P(("dp", "mp"), None, None),
        P(("dp", "mp"), None),
        P(("dp", "mp"), None),
        P(("dp", "mp"), None, None),
        P(("dp", "mp"), None),
        P(("dp", "mp"), None),
        P(("dp", "mp"), None),
        P(("dp", "mp"), None),
        P(("dp", "mp"), None),
        P(("dp", "mp"), None),
        P("dp", "mp"),
        P("dp", "mp"),
        P("dp", "mp"),
        P("mp", "dp"),
        P("mp", "dp"),
        P("mp", "dp"),
        P(),
        P(),
        P(),
        P(),
        P(),
        P(),
    )
    out_specs = (
        P(("dp", "mp"), None, None),
        P(("dp", "mp"), None, None),
        P(),
        P(("dp", "mp"), None),
        P(("dp", "mp"), None),
        P(("dp", "mp"), None),
        P(("dp", "mp"), None),
        P(("dp", "mp"), None),
        P(("dp", "mp"), None),
        P("dp", "mp"),
        P("dp", "mp"),
        P("dp", "mp"),
        P("mp", "dp"),
        P("mp", "dp"),
        P("mp", "dp"),
        P(),
        P(),
        P(),
        P(),
        P(),
        P(),
    )
    return jax.shard_map(
        on_device, mesh=mesh, in_specs=in_specs, out_specs=out_specs, check_vma=False
    )
```

profile of v0, /device:TPU:0, one launch (start us, length us, event | category | flops | bytes accessed | tf_op | source)
XLA Modules:
  0.0 1105.5 jit_solution(3876919274548969951)
XLA Ops:
  8.2 4.4 copy.198
  17.4 22.8 %all-gather.11.cloned.1.call-done = bf16[768,768]{1,0:T(8,128)(2,1)} async-done(((bf16[96,768]{1,0:T(8,128)(2,1)}), bf16[768,768]{1,0:T(8,128)(2,1)}) %all-gather.11.cloned.1.call-update) | async-done | bytes 1179664 | tf_op jit(solution)/shard_map/all_gather | solution.py:124
  41.6 17.9 %gather_fusion.1 = bf16[1280,768]{1,0:T(8,128)(2,1)} fusion(bf16[2,1280,768]{2,1,0:T(8,128)(2,1)} %copy.198, s32[1280]{0:T(1024)S(1)} %reshape.379), kind=kCustom, calls=%fused_computation.clone | custom fusion | bytes 3942400 | tf_op jit(solution)/shard_map/jit(take_along_axis)/gather | solution.py:131
  59.5 6.3 copy.117
  65.8 2.1 convert_reduce_fusion.3
  68.0 5.9 multiply_reduce_fusion.9
  73.9 17.9 %gather_fusion.2 = bf16[1280,768]{1,0:T(8,128)(2,1)} fusion(bf16[2,1280,768]{2,1,0:T(8,128)(2,1)} %param.31, s32[1280]{0:T(1024)S(1)} %reshape.379), kind=kCustom, calls=%fused_computation.1.clone | custom fusion | bytes 3942400 | tf_op jit(solution)/shard_map/jit(take_along_axis)/gather | solution.py:137
  91.8 6.9 copy.129
  98.7 6.8 fusion.42
  105.6 2.1 copy.160
  107.7 10.8 gather_fusion
  119.1 4.3 copy.162
  123.5 6.8 all-gather.7.cloned.1.call-done
  130.3 8.3 convolution_convert_fusion
  138.5 2.3 fusion.68
  140.8 4.4 copy.118
  145.2 4.8 reshape.316
  150.0 7.2 copy.151
  157.2 4.0 copy.120
  161.2 4.8 reshape.318
  166.0 7.2 copy.152
  173.3 2.3 copy.122
  175.5 3.9 reshape.320
  179.4 5.6 copy.153
  185.3 87.1 %while.26 = (s32[]{:T(128)}, bf16[24,640,64]{1,2,0:T(8,128)(2,1)S(1)}, f32[24,640,1]{1,2,0:T(1,128)}, s32[24,640]{1,0:T(8,128)S(1)}, bf16[24,640,64]{2,1,0:T(8,1...) while((s32[]{:T(128)}, bf16[24,640,64]{1,2,0:T(8,128)(2,1)S(1)}, ...), condition=%wide.region_7.9_spmd, body=%wide.region_4.0_spmd.sunk | while | flops 108133760 | bytes 5611097 | solution.py:148
  272.5 2.0 copy.127
  274.9 7.0 fusion.66
  284.9 47.1 %multiply_convert_fusion.1 = (bf16[1280,3072]{1,0:T(8,128)(2,1)}, f32[1280,3072]{1,0:T(8,128)}, f32[1280,3072]{1,0:T(8,128)}) fusion(f32[3072]{0:T(1024)S(1)} %copy-done.52, bf16[768,3072]{1,0:T(8,128)(2,1)} %all-gather.13.cloned.1.call-done, f32[1280,768]{0,1:T(8,128)} %copy-done.4, f32[768]{0:T(1024)S(1)} %get-tuple-element.255, ...), kind=kOutput, calls=%fused_computation.60 | convolution fusion | flops 6304235520 | bytes 48001024 | tf_op jit(solution)/shard_map/dot_general | solution.py:159
  331.9 33.5 %all-gather.17.cloned.1.call-done = bf16[3072,768]{0,1:T(8,128)(2,1)} async-done(((bf16[768,768]{0,1:T(8,128)(2,1)}), bf16[3072,768]{0,1:T(8,128)(2,1)}) %all-gather.17.cloned.1.call-update) | async-done | bytes 4718608 | tf_op jit(solution)/shard_map/all_gather | solution.py:157
  365.5 13.7 %multiply_reduce_fusion.6 = (f32[1280]{0:T(1024)S(1)}, f32[1280,768]{0,1:T(8,128)}) fusion(f32[1280,768]{0,1:T(8,128)} %bitcast.210, f32[1280,768]{0,1:T(8,128)} %get-tuple-element.345, f32[768]{0:T(1024)S(1)} %copy-done.72, bf16[1280,3072]{1,0:T(8,128)(2,1)} %get-tuple-element.320, bf16[3072,768]{0,1:T(8,128)(2,1)} %all-gather.17.cloned.1.call-done), kind=kOutput, calls=%fused_computation.88 | convolution fusion | flops 6043728896 | bytes 24387584 | tf_op jit(solution)/shard_map/dot_general | solution.py:162
  379.3 12.0 %fusion.43 = f32[3072,768]{1,0:T(8,128)} fusion(bf16[1280,3072]{1,0:T(8,128)(2,1)} %get-tuple-element.320, f32[1280,768]{0,1:T(8,128)} %bitcast.211, f32[1280]{0:T(1024)S(1)} %reshape.346), kind=kOutput, calls=%fused_computation.103 | convolution fusion | flops 6041763840 | bytes 21238784 | tf_op jit(solution)/shard_map/dot_general | solution.py:181
  391.4 25.8 %convert_reduce_fusion = (f32[3072]{0:T(1024)}, bf16[1280,3072]{1,0:T(8,128)(2,1)}) fusion(f32[1280,3072]{1,0:T(8,128)} %get-tuple-element.321, bf16[3072,768]{0,1:T(8,128)(2,1)} %all-gather.17.cloned.1.call-done, f32[1280,768]{0,1:T(8,128)} %bitcast.212, f32[1280]{0:T(1024)S(1)} %reshape.346, f32[1280,3072]{1,0:T(8,128)} %get-tuple-element.346, ...), kind=kOutput, calls=%fused_computation.58 | convolution fusion | flops 6108607488 | bytes 48002048 | tf_op jit(solution)/shard_map/dot_general | solution.py:177
  417.2 12.2 %fusion.56 = f32[768,3072]{1,0:T(8,128)} fusion(bf16[1280,3072]{1,0:T(8,128)(2,1)} %get-tuple-element.350, f32[1280,768]{0,1:T(8,128)} %copy-done.4, f32[768]{0:T(1024)S(1)} %get-tuple-element.255, f32[768]{0:T(1024)S(1)} %get-tuple-element.256, f32[1280]{0:T(1024)S(1)} %fusion.50, f32[1280]{0:T(1024)S(1)} %broadcast_multiply_fusion), kind=kOutput, calls=%fused_computation.186 | convolution fusion | flops 6044712960 | bytes 21250048 | tf_op jit(solution)/shard_map/dot_general | solution.py:180
  429.5 11.8 %fusion.71 = (f32[768]{0:T(1024)S(1)}, f32[1280,768]{1,0:T(8,128)}) fusion(bf16[1280,3072]{1,0:T(8,128)(2,1)} %get-tuple-element.350, bf16[768,3072]{1,0:T(8,128)(2,1)} %all-gather.13.cloned.1.call-done), kind=kOutput, calls=%fused_computation.194 | convolution fusion | flops 6040779776 | bytes 16518144 | tf_op jit(solution)/shard_map/dot_general | solution.py:186
  441.3 5.4 copy.130
  446.8 4.6 multiply_reduce_fusion.2
  456.9 3.0 convolution_convert_fusion.1
  459.9 2.7 copy.131
  462.6 2.0 reshape.323
  464.6 7.4 copy.156
  472.1 4.7 fusion.72
  480.3 235.8 %while.27 = (s32[]{:T(128)}, bf16[24,640,64]{1,2,0:T(8,128)(2,1)S(1)}, bf16[24,640,64]{1,2,0:T(8,128)(2,1)}, bf16[24,640,64]{1,2,0:T(8,128)(2,1)}, s32[24,640]{1...) while((s32[]{:T(128)}, ...), condition=%wide.region_16.18_spmd, body=%wide.region_14.17_spmd.sunk | while | flops 266321280 | bytes 13959285 | solution.py:196
  718.5 2.0 copy.138
  720.9 3.6 copy.139
  725.3 3.0 copy-done.30
  729.2 7.2 fusion.55
  736.8 3.1 copy.158
  740.0 6.1 bitcast_convert_fusion
  747.9 9.6 convert_reduce_fusion.1
  758.1 9.6 fusion.70
  767.7 5.5 copy.140
  773.2 3.9 multiply_reduce_fusion.4
  777.3 5.0 multiply_reduce_fusion.3
  785.2 7.5 add_add_fusion.2
  792.6 5.5 copy.141
  798.2 2.4 copy.128
  800.5 16.0 %scatter_fusion.1 = f32[2560,768]{1,0:T(8,128)} fusion(f32[2560,768]{1,0:T(8,128)} %bitcast_convert_fusion, s32[1280]{0:T(1024)S(1)} %reshape.365, f32[1280,768]{1,0:T(8,128)} %copy.141), kind=kCustom, calls=%fused_computation.4 | custom fusion | bytes 11801600
  816.6 12.9 %scatter_fusion = bf16[2560,768]{1,0:T(8,128)(2,1)} fusion(bf16[2560,768]{1,0:T(8,128)(2,1)} %bitcast.201, s32[1280]{0:T(1024)S(1)} %reshape.365, bf16[1280,768]{1,0:T(8,128)(2,1)S(1)} %copy-done.15), kind=kCustom, calls=%fused_computation.3 | custom fusion | bytes 5903360
  832.1 113.5 %reduce-scatter.9.cloned.1.call-done = f32[24,2304]{1,0:T(8,128)} async-done(((f32[768,2304]{1,0:T(8,128)}), f32[24,2304]{1,0:T(8,128)}) %reduce-scatter.9.cloned.1.call-update) | async-done | bytes 221200 | tf_op jit(solution)/shard_map/reduce_scatter | solution.py:215
  945.6 2.7 multiply_reduce_fusion.14
  948.3 42.5 %reduce-scatter.19.cloned.1.call-done = f32[96,768]{1,0:T(8,128)} async-done(((f32[768,768]{1,0:T(8,128)}), f32[96,768]{1,0:T(8,128)}) %reduce-scatter.19.cloned.1.call-update) | async-done | bytes 294928
  992.9 44.0 %reduce-scatter.15.cloned.1.call-done = f32[96,768]{1,0:T(8,128)} async-done(((f32[768,768]{1,0:T(8,128)}), f32[96,768]{1,0:T(8,128)}) %reduce-scatter.15.cloned.1.call-update) | async-done | bytes 294928 | tf_op jit(solution)/shard_map/reduce_scatter | solution.py:219
  1038.9 5.3 stack.51
  1044.1 39.9 %all-reduce = (f32[8]{0:T(128)S(1)}, f32[3072]{0:T(1024)S(1)}, f32[7,768]{1,0:T(8,128)S(1)}) all-reduce(f32[8]{0:T(128)S(1)} %stack.51, f32[3072]{0:T(1024)} %get-tuple-element.349, f32[7,768]{1,0:T(8,128)S(1)} %stack.55), channel_id=1, replica_groups=mesh['dp'=8,'mp'=4] {'dp','mp'}, use_global_device_ids=true, to_apply=%region_34.36 | all-reduce | flops 8456 | bytes 67648 | tf_op jit(solution)/shard_map/psum | solution.py:250
  (602 shorter events, 367.5 us)
Async XLA Ops:
  8.0 99.7 %copy-start = (s32[2,1280]{1,0:T(2,128)S(1)}, s32[2,1280]{1,0:T(2,128)}, u32[]{:S(2)}) copy-start(s32[2,1280]{1,0:T(2,128)} %param.29) | copy-start | bytes 30724
  8.1 7.9 copy-start.18
  8.1 8.6 copy-start.28
  8.1 6.5 copy-start.22
  8.1 32.1 %copy-start.34 = (f32[7,768]{1,0:T(8,128)S(1)}, f32[7,768]{1,0:T(8,128)}, u32[]{:S(2)}) copy-start(f32[7,768]{1,0:T(8,128)} %param.47) | copy-start | bytes 64516
  8.1 32.0 %all-gather.11.cloned.1.call-start = ((), (), s32[]{:S(2)}) async-start(), calls=%async_computation.8 | async-start | bytes 1327104 | tf_op jit(solution)/shard_map/all_gather | solution.py:124
  13.2 27.6 %sort.19.cloned.1.call-start = ((), (), s32[]{:S(2)}) async-start(), calls=%async_computation.18 | async-start | bytes 61472 | tf_op jit(solution)/shard_map/jit(argsort)/sort | solution.py:129
  14.5 108.9 %all-gather.15.cloned.1.call-start = ((), (), s32[]{:S(2)}) async-start(), calls=%async_computation.10 | async-start | bytes 1327104 | tf_op jit(solution)/shard_map/all_gather | solution.py:125
  15.9 114.3 %all-gather.7.cloned.1.call-start = ((), (), s32[]{:S(2)}) async-start(), calls=%async_computation.6 | async-start | bytes 3649536 | tf_op jit(solution)/shard_map/all_gather | solution.py:120
  16.6 258.3 %all-gather.9.cloned.1.call-start = ((), (), s32[]{:S(2)}) async-start(), calls=%async_computation.7 | async-start | bytes 1216512 | tf_op jit(solution)/shard_map/all_gather | solution.py:121
  17.3 267.5 %all-gather.13.cloned.1.call-start = ((), (), s32[]{:S(2)}) async-start(), calls=%async_computation.9 | async-start | bytes 5898240 | tf_op jit(solution)/shard_map/all_gather | solution.py:156
  40.2 325.3 %all-gather.17.cloned.1.call-start = ((), (), s32[]{:S(2)}) async-start(), calls=%async_computation.11 | async-start | bytes 5898240 | tf_op jit(solution)/shard_map/all_gather | solution.py:157
  40.9 27.1 %copy-start.57 = (f32[768]{0:T(1024)}, f32[768]{0:T(1024)S(1)}, u32[]{:S(2)}) copy-start(f32[768]{0:T(1024)S(1)} %get-tuple-element.253) | copy-start | bytes 9220
  40.9 89.4 %copy-start.48 = (f32[768]{0:T(1024)}, f32[768]{0:T(1024)S(1)}, u32[]{:S(2)}) copy-start(f32[768]{0:T(1024)S(1)} %get-tuple-element.259) | copy-start | bytes 9220
  40.9 89.4 %copy-start.70 = (f32[768]{0:T(1024)}, f32[768]{0:T(1024)S(1)}, u32[]{:S(2)}) copy-start(f32[768]{0:T(1024)S(1)} %get-tuple-element.258) | copy-start | bytes 9220
  65.8 32.9 %copy-start.7 = (bf16[2,640,768]{1,0,2:T(2,128)(2,1)}, bf16[2,640,768]{1,0,2:T(2,128)(2,1)S(1)}, u32[]{:S(2)}) copy-start(bf16[2,640,768]{1,0,2:T(2,128)(2,1)S(1)} %copy.117) | copy-start | bytes 5898244
  65.8 32.9 %copy-start.50 = (pred[2,640]{1,0:T(4,128)(4,1)}, pred[2,640]{1,0:T(4,128)(4,1)S(1)}, u32[]{:S(2)}) copy-start(pred[2,640]{1,0:T(4,128)(4,1)S(1)} %and_bitcast_fusion) | copy-start | bytes 3844
  68.0 62.3 %copy-start.36 = (f32[1280]{0:T(1024)}, f32[1280]{0:T(1024)S(1)}, u32[]{:S(2)}) copy-start(f32[1280]{0:T(1024)S(1)} %div.154) | copy-start | bytes 15364
  73.9 17.9 %copy-start.46 = (f32[1280]{0:T(1024)}, f32[1280]{0:T(1024)S(1)}, u32[]{:S(2)}) copy-start(f32[1280]{0:T(1024)S(1)} %add.258) | copy-start | bytes 15364
  73.9 56.4 %copy-start.41 = (f32[1280]{0:T(1024)}, f32[1280]{0:T(1024)S(1)}, u32[]{:S(2)}) copy-start(f32[1280]{0:T(1024)S(1)} %rsqrt.27) | copy-start | bytes 15364
  123.4 613.3 %reduce-scatter.17.cloned.1.call-start = ((), (), s32[]{:S(2)}) async-start(), calls=%async_computation.16 | async-start | bytes 11796480 | tf_op jit(solution)/shard_map/reduce_scatter | solution.py:184
  274.9 7.0 copy-start.12
  284.9 80.6 %copy-start.72 = (f32[768]{0:T(1024)S(1)}, f32[768]{0:T(1024)}, u32[]{:S(2)}) copy-start(f32[768]{0:T(1024)} %get-tuple-element.254) | copy-start | bytes 9220
  365.5 13.8 %copy-start.64 = (f32[2,640]{1,0:T(2,128)S(1)}, f32[2,640]{1,0:T(2,128)}, u32[]{:S(2)}) copy-start(f32[2,640]{1,0:T(2,128)} %get-tuple-element.243) | copy-start | bytes 15364
  379.2 12.1 %copy-start.59 = (f32[1280]{0:T(1024)}, f32[1280]{0:T(1024)S(1)}, u32[]{:S(2)}) copy-start(f32[1280]{0:T(1024)S(1)} %get-tuple-element.347) | copy-start | bytes 15364
  391.4 385.8 %reduce-scatter.13.cloned.1.call-start = ((), (), s32[]{:S(2)}) async-start(), calls=%async_computation.14 | async-start | bytes 11796480 | tf_op jit(solution)/shard_map/reduce_scatter | solution.py:183
  429.5 401.0 %reduce-scatter.11.cloned.1.call-start = ((), (), s32[]{:S(2)}) async-start(), calls=%async_computation.13 | async-start | bytes 2433024 | tf_op jit(solution)/shard_map/reduce_scatter | solution.py:216
  464.6 7.4 copy-start.13
  476.8 468.8 %reduce-scatter.9.cloned.1.call-start = ((), (), s32[]{:S(2)}) async-start(), calls=%async_computation.12 | async-start | bytes 7299072 | tf_op jit(solution)/shard_map/reduce_scatter | solution.py:215
  736.5 254.3 %reduce-scatter.19.cloned.1.call-start = ((), (), s32[]{:S(2)}) async-start(), calls=%async_computation.17 | async-start | bytes 2654208
  739.9 6.4 copy-start.33
  739.9 7.8 copy-start.56
  739.9 7.8 copy-start.73
  740.0 7.8 copy-start.74
  740.0 7.9 copy-start.8
  740.0 7.9 copy-start.51
  740.0 296.9 %reduce-scatter.15.cloned.1.call-start = ((), (), s32[]{:S(2)}) async-start(), calls=%async_computation.15 | async-start | bytes 2654208 | tf_op jit(solution)/shard_map/reduce_scatter | solution.py:219
  747.9 10.2 copy-start.75
  777.2 7.9 copy-start.60
  777.2 7.9 copy-start.3
  777.3 7.9 copy-start.6
  777.3 7.9 copy-start.58
  800.5 16.0 %copy-start.15 = (bf16[1280,768]{1,0:T(8,128)(2,1)S(1)}, bf16[1280,768]{1,0:T(8,128)(2,1)}, u32[]{:S(2)}) copy-start(bf16[1280,768]{1,0:T(8,128)(2,1)} %copy.128) | copy-start | bytes 5898244
  816.6 13.0 %copy-start.66 = (f32[1,768]{1,0:T(1,128)S(1)}, f32[1,768]{1,0:T(1,128)}, u32[]{:S(2)}) copy-start(f32[1,768]{1,0:T(1,128)} %stack.54) | copy-start | bytes 9220
  816.6 13.0 %copy-start.67 = (f32[1,768]{1,0:T(1,128)S(1)}, f32[1,768]{1,0:T(1,128)}, u32[]{:S(2)}) copy-start(f32[1,768]{1,0:T(1,128)} %reshape.333) | copy-start | bytes 9220
  816.6 13.0 %copy-start.68 = (f32[1,768]{1,0:T(1,128)S(1)}, f32[1,768]{1,0:T(1,128)}, u32[]{:S(2)}) copy-start(f32[1,768]{1,0:T(1,128)} %reshape.334) | copy-start | bytes 9220
  816.6 13.8 %copy-start.29 = (f32[24,768]{1,0:T(8,128)S(1)}, f32[24,768]{1,0:T(8,128)}, u32[]{:S(2)}) copy-start(f32[24,768]{1,0:T(8,128)} %param.35) | copy-start | bytes 221188
  816.6 13.8 %copy-start.45 = (f32[24,768]{1,0:T(8,128)S(1)}, f32[24,768]{1,0:T(8,128)}, u32[]{:S(2)}) copy-start(f32[24,768]{1,0:T(8,128)} %param.36) | copy-start | bytes 221188
  816.6 129.0 %copy-start.19 = (f32[24,2304]{1,0:T(8,128)S(1)}, f32[24,2304]{1,0:T(8,128)}, u32[]{:S(2)}) copy-start(f32[24,2304]{1,0:T(8,128)} %param.32) | copy-start | bytes 663556
  829.6 207.3 %copy-start.17 = (f32[96,768]{1,0:T(8,128)S(1)}, f32[96,768]{1,0:T(8,128)}, u32[]{:S(2)}) copy-start(f32[96,768]{1,0:T(8,128)} %param.38) | copy-start | bytes 884740
  829.6 255.2 %copy-start.53 = (f32[3072]{0:T(1024)S(1)}, f32[3072]{0:T(1024)}, u32[]{:S(2)}) copy-start(f32[3072]{0:T(1024)} %param.44) | copy-start | bytes 36868
  829.6 255.2 %copy-start.65 = (f32[3072]{0:T(1024)S(1)}, f32[3072]{0:T(1024)}, u32[]{:S(2)}) copy-start(f32[3072]{0:T(1024)} %param.45) | copy-start | bytes 36868
  832.1 263.9 %copy-start.31 = (f32[24,768]{1,0:T(8,128)}, f32[24,768]{1,0:T(8,128)S(1)}, u32[]{:S(2)}) copy-start(f32[24,768]{1,0:T(8,128)S(1)} %get-tuple-element.314) | copy-start | bytes 221188
  832.1 263.9 %copy-start.32 = (f32[24,768]{1,0:T(8,128)}, f32[24,768]{1,0:T(8,128)S(1)}, u32[]{:S(2)}) copy-start(f32[24,768]{1,0:T(8,128)S(1)} %get-tuple-element.315) | copy-start | bytes 221188
  991.9 101.7 %copy-start.35 = (f32[7,768]{1,0:T(8,128)S(1)}, f32[7,768]{1,0:T(8,128)}, u32[]{:S(2)}) copy-start(f32[7,768]{1,0:T(8,128)} %param.47) | copy-start | bytes 64516
  991.9 101.7 %copy-start.61 = (f32[7,768]{1,0:T(8,128)S(1)}, f32[7,768]{1,0:T(8,128)}, u32[]{:S(2)}) copy-start(f32[7,768]{1,0:T(8,128)} %param.48) | copy-start | bytes 64516
  991.9 101.7 %copy-start.62 = (f32[7,768]{1,0:T(8,128)S(1)}, f32[7,768]{1,0:T(8,128)}, u32[]{:S(2)}) copy-start(f32[7,768]{1,0:T(8,128)} %param.49) | copy-start | bytes 64516
  991.9 105.6 %copy-start.1 = (s32[2,1280]{1,0:T(2,128)S(1)}, s32[2,1280]{1,0:T(2,128)}, u32[]{:S(2)}) copy-start(s32[2,1280]{1,0:T(2,128)} %param.29) | copy-start | bytes 30724
  992.9 103.8 %copy-start.26 = (f32[24,2304]{1,0:T(8,128)S(1)}, f32[24,2304]{1,0:T(8,128)}, u32[]{:S(2)}) copy-start(f32[24,2304]{1,0:T(8,128)} %get-tuple-element.316) | copy-start | bytes 663556
  992.9 103.8 %copy-start.27 = (f32[24,2304]{1,0:T(8,128)S(1)}, f32[24,2304]{1,0:T(8,128)}, u32[]{:S(2)}) copy-start(f32[24,2304]{1,0:T(8,128)} %get-tuple-element.317) | copy-start | bytes 663556
  1038.9 58.7 %copy-start.24 = (f32[96,768]{1,0:T(8,128)}, f32[96,768]{1,0:T(8,128)S(1)}, u32[]{:S(2)}) copy-start(f32[96,768]{1,0:T(8,128)S(1)} %get-tuple-element.312) | copy-start | bytes 884740
  1038.9 58.7 %copy-start.25 = (f32[96,768]{1,0:T(8,128)}, f32[96,768]{1,0:T(8,128)S(1)}, u32[]{:S(2)}) copy-start(f32[96,768]{1,0:T(8,128)S(1)} %get-tuple-element.313) | copy-start | bytes 884740
  1086.2 11.4 %copy-start.54 = (f32[3072]{0:T(1024)}, f32[3072]{0:T(1024)S(1)}, u32[]{:S(2)}) copy-start(f32[3072]{0:T(1024)S(1)} %get-tuple-element.303) | copy-start | bytes 36868
  1086.2 11.4 %copy-start.55 = (f32[3072]{0:T(1024)}, f32[3072]{0:T(1024)S(1)}, u32[]{:S(2)}) copy-start(f32[3072]{0:T(1024)S(1)} %get-tuple-element.304) | copy-start | bytes 36868
  (25 other events, 90.8 us)
Sparse Core Ops, SparseCore 0:
  13.4 26.7 all-gather.10
  42.6 24.0 all-gather.14
  70.1 60.1 all-gather.6
  133.5 52.9 all-gather.8
  187.8 88.3 all-gather.12
  277.6 87.8 all-gather.16
  391.5 159.7 reduce-scatter.16
  553.6 162.1 reduce-scatter.12
  721.0 99.7 reduce-scatter.10
  827.3 118.2 reduce-scatter.8
  948.9 41.7 reduce-scatter.18
  994.3 42.4 reduce-scatter.14
Sparse Core Ops, SparseCore 1:
  17.3 2.9 sort.21.cloned.1.call-done
  (1 shorter events, 0.0 us)
where the time goes:
time: 1120 us; the launch traced here: 1110 us
  matrix products  424 us (38%)
  local copies, waits for them, and re-layouts  273 us (24%)
  waiting for transfers between devices  263 us (23%)
  other arithmetic  83 us (7%)
  blocking collectives  39.9 us (4%)
  between operations  21.1 us (2%)
    reduce_scatter x1, waiting for transfers between devices, on_device(): lax.psum_scatter(qkv_grad, ('dp', 'mp'), scatter_dimension=0, tiled=True)  113 us
    dot_general x48, matrix products, head_scores(): jnp.dot(queries, key_rows.T, preferred_element_type=jnp.float32)  73.4 us
    unnamed x173, local copies, waits for them, and re-layouts  60.4 us
    dot_general x1, matrix products, on_device(): jnp.dot(normed_two_low, up_full, preferred_element_type=jnp.float32)  47.1 us
    dot_general x24, matrix products, attend_backward(): jnp.dot(probs_low.T, context_grad, preferred_element_type=jnp.float32)  47.1 us
    dot_general x24, matrix products, attend_backward(): jnp.dot(score_grad.T, queries, preferred_element_type=jnp.float32)  47 us
    reduce_scatter x1, waiting for transfers between devices, on_device(): lax.psum_scatter(up_grad, 'dp', scatter_dimension=0, tiled=True)  44 us
    unnamed x13, waiting for transfers between devices  42.7 us
  transfers between devices with their start and end apart: 12, of which 6 were waited for; matrix products, arithmetic and copies ran while one was open for 65% of the time, Pallas kernels for 0%

commit v1 on v0

v1 whole, which is shorter than its diff:
```python
from functools import partial
import math

import jax
import jax.numpy as jnp
from jax import lax
from jax.experimental import pallas as pl
from jax.experimental.pallas import tpu as pltpu
from jax.sharding import Mesh, PartitionSpec as P

D = 768
FF = 3072
HEADS = 12
HEAD_DIM = 64
CAP = 640
SEQ = 1280
STEP = 10

eps_norm = 1e-06
eps_adam = 1e-06
beta_one = 0.9
beta_two = 0.999
decay_mat = 0.01
rate_lamb = 0.3
masked_score = -1e30

f32 = jnp.float32
bf16 = jnp.bfloat16
GROUP = 256
GROUPS = D // GROUP
LOG2E = 1.0 / math.log(2.0)
SCORE_SCALE = 1.0 / math.sqrt(HEAD_DIM)
ROUTER_SCALE = 1.0 / math.sqrt(D)


def dot_ab(left, right, left_dim=1, right_dim=0):
    return lax.dot_general(
        left, right, (((left_dim,), (right_dim,)), ((), ())), preferred_element_type=f32
    )


def params(mib, **more):
    return pltpu.CompilerParams(vmem_limit_bytes=mib << 20, **more)


def cost(flops, nbytes, trans=0):
    return pl.CostEstimate(flops=int(flops), bytes_accessed=int(nbytes), transcendentals=int(trans))


def norm_parts(values):
    center = jnp.mean(values, -1, keepdims=True)
    offset = values - center
    spread = jnp.mean(offset * offset, -1, keepdims=True)
    inverse = lax.rsqrt(spread + eps_norm)
    return offset * inverse, inverse


def norm_back(grad, normalized, inverse, gain):
    scaled = grad * gain
    return inverse * (
        scaled
        - jnp.mean(scaled, -1, keepdims=True)
        - normalized * jnp.mean(scaled * normalized, -1, keepdims=True)
    )


def ranks_of(sel, ids):
    kind = jnp.where(ids < 0, 2, ids)
    sub = lax.broadcasted_iota(jnp.int32, (8, SEQ), 0)
    lane = lax.broadcasted_iota(jnp.int32, (8, SEQ), 1)
    member = jnp.where(jnp.broadcast_to(kind, (8, SEQ)) == sub, jnp.broadcast_to(sel, (8, SEQ)), 0)
    total = member
    step = 1
    while step < SEQ:
        total = total + jnp.where(lane >= step, pltpu.roll(total, step, 1), 0)
        step *= 2
    count = jnp.max(total, axis=1, keepdims=True)
    first = count[0:1]
    second = first + count[1:2]
    base = jnp.where(sub == 0, 0, jnp.where(sub == 1, first, second))
    rank = jnp.sum(member * (total + base), axis=0, keepdims=True) - 1
    return rank, first, second


def one_hot(rank):
    place = lax.broadcasted_iota(jnp.int32, (CAP, SEQ), 0)
    return jnp.where(place == rank, 1.0, 0.0).astype(bf16)


def pick_kernel(
    sel_ref, ids_ref, tok_ref, cot_ref, vec_ref,
    x_ref, dy_ref, a_ref, at_ref, dm_ref, rank_ref, bounds_ref, x_scr, dy_scr,
):
    rank, first, second = ranks_of(sel_ref[0], ids_ref[0])
    rank_ref[0] = jnp.broadcast_to(rank, (8, SEQ))
    lane = lax.broadcasted_iota(jnp.int32, (8, 128), 1)
    bounds_ref[0] = jnp.where(lane == 0, first, second)
    hot = one_hot(rank)
    x_scr[...] = dot_ab(hot, tok_ref[0])
    dy_scr[...] = dot_ab(hot, cot_ref[0])
    tile = 128

    def body(i, carry):
        rows = pl.ds(pl.multiple_of(i * tile, tile), tile)
        x = x_scr[rows, :]
        dy = dy_scr[rows, :]
        normalized, _ = norm_parts(x)
        low = (normalized * vec_ref[0:1, :] + vec_ref[1:2, :]).astype(bf16)
        gate = jax.nn.sigmoid(jnp.sum(x * vec_ref[4:5, :], -1, keepdims=True) * ROUTER_SCALE)
        x_ref[rows, :] = x.astype(bf16)
        dy_ref[rows, :] = dy.astype(bf16)
        a_ref[rows, :] = low
        dm_ref[rows, :] = (gate * dy).astype(bf16)
        return carry

    lax.fori_loop(0, CAP // tile, body, 0)
    at_ref[...] = a_ref[...].T


def pick_rows(sel, ids, tokens, cotangent, vectors):
    rows = tokens.shape[0]
    count = rows * CAP
    wide = pl.BlockSpec((CAP, D), lambda r: (r, 0))
    line = pl.BlockSpec((1, 1, SEQ), lambda r: (r, 0, 0))
    full = pl.BlockSpec((1, SEQ, D), lambda r: (r, 0, 0))
    return pl.pallas_call(
        pick_kernel,
        grid=(rows,),
        in_specs=[line, line, full, full, pl.BlockSpec((7, D), lambda r: (0, 0))],
        out_specs=[
            wide, wide, wide, pl.BlockSpec((D, CAP), lambda r: (0, r)), wide,
            pl.BlockSpec((1, 8, SEQ), lambda r: (r, 0, 0)),
            pl.BlockSpec((1, 8, 128), lambda r: (r, 0, 0)),
        ],
        out_shape=[
            jax.ShapeDtypeStruct((count, D), bf16),
            jax.ShapeDtypeStruct((count, D), bf16),
            jax.ShapeDtypeStruct((count, D), bf16),
            jax.ShapeDtypeStruct((D, count), bf16),
            jax.ShapeDtypeStruct((count, D), bf16),
            jax.ShapeDtypeStruct((rows, 8, SEQ), jnp.int32),
            jax.ShapeDtypeStruct((rows, 8, 128), jnp.int32),
        ],
        scratch_shapes=[pltpu.VMEM((CAP, D), f32), pltpu.VMEM((CAP, D), f32)],
        compiler_params=params(48),
        cost_estimate=cost(4 * count * SEQ * D, 4 * rows * SEQ * D * 2),
        name="pick_rows",
    )(sel[:, None, :], ids[:, None, :], tokens, cotangent, vectors)


def fill_bias(bias_scr, bounds_ref):
    first = bounds_ref[0, 0:1, 0:1]
    second = bounds_ref[0, 0:1, 1:2]
    tile = 128
    key = lax.broadcasted_iota(jnp.int32, (tile, CAP), 1)
    key_kind = jnp.where(key >= first, 1, 0) + jnp.where(key >= second, 1, 0)
    for i in range(CAP // tile):
        row = lax.broadcasted_iota(jnp.int32, (tile, CAP), 0) + i * tile
        row_kind = jnp.where(row >= first, 1, 0) + jnp.where(row >= second, 1, 0)
        bias_scr[i * tile : (i + 1) * tile, :] = jnp.where(row_kind == key_kind, 0.0, masked_score)


def half_masks():
    lane = lax.broadcasted_iota(jnp.int32, (1, 128), 1)
    low = jnp.where(lane < HEAD_DIM, 1.0, 0.0)
    return low, 1.0 - low


def attend_kernel(
    a_ref, wq_ref, wk_ref, wv_ref, bounds_ref,
    q_ref, k_ref, v_ref, ctx_ref, lse_ref, bias_scr,
):
    group = pl.program_id(1)

    @pl.when(group == 0)
    def _():
        fill_bias(bias_scr, bounds_ref)
        lse_ref[...] = jnp.zeros_like(lse_ref)

    a = a_ref[...]
    q_ref[...] = dot_ab(a, wq_ref[...]).astype(bf16)
    k_ref[...] = dot_ab(a, wk_ref[...]).astype(bf16)
    v_ref[...] = dot_ab(a, wv_ref[...]).astype(bf16)
    masks = half_masks()
    lane = lax.broadcasted_iota(jnp.int32, (1, 128), 1)
    for pair in range(GROUP // 128):
        cols = slice(pair * 128, pair * 128 + 128)
        queries, key_rows, values = q_ref[:, cols], k_ref[:, cols], v_ref[:, cols]
        halves = []
        for half in range(2):
            scores = dot_ab(queries * masks[half].astype(bf16), key_rows, 1, 1)
            scores = scores * (SCORE_SCALE * LOG2E) + bias_scr[...]
            row_max = jnp.max(scores, -1, keepdims=True)
            probs = jnp.exp2(scores - row_max)
            row_total = jnp.sum(probs, -1, keepdims=True)
            out = dot_ab(probs.astype(bf16), values)
            halves.append(out * (1.0 / row_total))
            head = group * (GROUP // HEAD_DIM) + pair * 2 + half
            lse_ref[...] = jnp.where(lane == head, row_max + jnp.log2(row_total), lse_ref[...])
        ctx_ref[:, cols] = jnp.where(lane < HEAD_DIM, halves[0], halves[1]).astype(bf16)


def attend_forward(a, weights, bounds):
    count = a.shape[0]
    rows = count // CAP
    piece = pl.BlockSpec((CAP, GROUP), lambda r, g: (r, g))
    narrow = jax.ShapeDtypeStruct((count, D), bf16)
    return pl.pallas_call(
        attend_kernel,
        grid=(rows, GROUPS),
        in_specs=[
            pl.BlockSpec((CAP, D), lambda r, g: (r, 0)),
            pl.BlockSpec((D, GROUP), lambda r, g: (0, g)),
            pl.BlockSpec((D, GROUP), lambda r, g: (0, g + GROUPS)),
            pl.BlockSpec((D, GROUP), lambda r, g: (0, g + 2 * GROUPS)),
            pl.BlockSpec((1, 8, 128), lambda r, g: (r, 0, 0)),
        ],
        out_specs=[piece, piece, piece, piece, pl.BlockSpec((CAP, 128), lambda r, g: (r, 0))],
        out_shape=[narrow, narrow, narrow, narrow, jax.ShapeDtypeStruct((count, 128), f32)],
        scratch_shapes=[pltpu.VMEM((CAP, CAP), f32)],
        compiler_params=params(48),
        cost_estimate=cost(
            2 * count * D * 3 * D + rows * HEADS * 16 * CAP * CAP * HEAD_DIM, 12 * count * D,
            rows * HEADS * CAP * CAP,
        ),
        name="attend_forward",
    )(a, weights, weights, weights, bounds)


def attend_back_kernel(
    me_ref, at_ref, q_ref, k_ref, v_ref, ctx_ref, dctx_ref, lse_ref, bounds_ref, gwo_ref,
    dq_ref, dk_ref, dv_ref, keep_ref, send_ref, bias_scr, acc_scr, *, plan,
):
    group, row = pl.program_id(0), pl.program_id(1)
    fill_bias(bias_scr, bounds_ref)
    masks = half_masks()
    lane = lax.broadcasted_iota(jnp.int32, (1, 128), 1)
    for pair in range(GROUP // 128):
        cols = slice(pair * 128, pair * 128 + 128)
        queries, key_rows, values = q_ref[:, cols], k_ref[:, cols], v_ref[:, cols]
        grads = dctx_ref[:, cols]
        product = ctx_ref[:, cols].astype(f32) * grads.astype(f32)
        queries_t, grads_t = queries.T, grads.T
        dq, dk_t, dv_t = [], [], []
        for half in range(2):
            mask_low = masks[half].astype(bf16)
            span = slice(half * HEAD_DIM, half * HEAD_DIM + HEAD_DIM)
            head = group * (GROUP // HEAD_DIM) + pair * 2 + half
            log_total = jnp.sum(jnp.where(lane == head, lse_ref[...], 0.0), -1, keepdims=True)
            delta = jnp.sum(product * masks[half], -1, keepdims=True)
            scores = dot_ab(queries * mask_low, key_rows, 1, 1)
            scores = scores * (SCORE_SCALE * LOG2E) + bias_scr[...]
            probs = jnp.exp2(scores - log_total)
            probs_grad = dot_ab(grads * mask_low, values, 1, 1)
            score_grad = (probs * (probs_grad - delta)).astype(bf16)
            dq.append(dot_ab(score_grad, key_rows))
            dk_t.append(dot_ab(queries_t[span], score_grad))
            dv_t.append(dot_ab(grads_t[span], probs.astype(bf16)))
        dq_ref[:, cols] = (jnp.where(lane < HEAD_DIM, dq[0], dq[1]) * SCORE_SCALE).astype(bf16)
        dk_ref[:, cols] = (jnp.concatenate(dk_t, 0) * SCORE_SCALE).astype(bf16).T
        dv_ref[:, cols] = jnp.concatenate(dv_t, 0).astype(bf16).T
    at = at_ref[...]
    for part, ref in enumerate((dq_ref, dk_ref, dv_ref)):
        span = slice(part * GROUP, part * GROUP + GROUP)
        product = dot_ab(at, ref[...])

        @pl.when(row == 0)
        def _():
            acc_scr[:, span] = product

        @pl.when(row > 0)
        def _():
            acc_scr[:, span] = acc_scr[:, span] + product

    @pl.when(row == pl.num_programs(1) - 1)
    def _():
        acc_scr[:, 3 * GROUP :] = gwo_ref[...]
        split_blocks(me_ref, acc_scr, keep_ref, send_ref, plan)


def split_blocks(me_ref, acc_scr, keep_ref, send_ref, plan):
    if plan is None:
        keep_ref[0] = acc_scr[...].astype(bf16)
        send_ref[0] = jnp.zeros_like(send_ref[0])
        return
    blocks, core_bit = plan
    size = D // blocks
    me = me_ref[0]
    on_high = (me & core_bit) != 0
    for block in range(blocks):
        if block & core_bit:
            continue
        low = acc_scr[block * size : (block + 1) * size, :]
        other = block | core_bit
        high = acc_scr[other * size : (other + 1) * size, :]
        place = me ^ block
        slot = (place // (2 * core_bit)) * core_bit + place % core_bit
        keep_ref[slot] = jnp.where(on_high, high, low).astype(bf16)
        send_ref[slot] = jnp.where(on_high, low, high).astype(bf16)


def attend_backward(me, at, q, k, v, ctx, dctx, lse, bounds, gwo, plan):
    count = q.shape[0]
    rows = count // CAP
    piece = pl.BlockSpec((CAP, GROUP), lambda g, r, me: (r, g))
    narrow = jax.ShapeDtypeStruct((count, D), bf16)
    if plan is None:
        half, size, sent = 1, D, 8
    else:
        half, size = plan[0] // 2, D // plan[0]
        sent = size
    width = 4 * GROUP
    return pl.pallas_call(
        partial(attend_back_kernel, plan=plan),
        grid_spec=pltpu.PrefetchScalarGridSpec(
            num_scalar_prefetch=1,
            grid=(GROUPS, rows),
            in_specs=[
                pl.BlockSpec((D, CAP), lambda g, r, me: (0, r)),
                piece, piece, piece, piece, piece,
                pl.BlockSpec((CAP, 128), lambda g, r, me: (r, 0)),
                pl.BlockSpec((1, 8, 128), lambda g, r, me: (r, 0, 0)),
                pl.BlockSpec((D, GROUP), lambda g, r, me: (0, g)),
            ],
            out_specs=[
                piece, piece, piece,
                pl.BlockSpec((half, size, width), lambda g, r, me: (0, 0, g)),
                pl.BlockSpec((half, sent, width), lambda g, r, me: (0, 0, g)),
            ],
            scratch_shapes=[pltpu.VMEM((CAP, CAP), f32), pltpu.VMEM((D, width), f32)],
        ),
        out_shape=[
            narrow, narrow, narrow,
            jax.ShapeDtypeStruct((half, size, 4 * D), bf16),
            jax.ShapeDtypeStruct((half, sent, 4 * D), bf16),
        ],
        compiler_params=params(56),
        cost_estimate=cost(
            2 * count * D * 3 * D + rows * HEADS * 40 * CAP * CAP * HEAD_DIM, 20 * count * D,
            rows * HEADS * CAP * CAP,
        ),
        name="attend_backward",
    )(me, at, q, k, v, ctx, dctx, lse, bounds, gwo)


def middle_kernel(ctx_ref, wo_ref, x_ref, vec_ref, att_ref, c_ref):
    att = dot_ab(ctx_ref[...], wo_ref[...]) + vec_ref[5:6, :]
    att_ref[...] = att
    normalized, _ = norm_parts(x_ref[...].astype(f32) + att)
    c_ref[...] = (normalized * vec_ref[2:3, :] + vec_ref[3:4, :]).astype(bf16)


def middle(ctx, weights, x, vectors):
    count = ctx.shape[0]
    tile = 320
    wide = pl.BlockSpec((tile, D), lambda t: (t, 0))
    return pl.pallas_call(
        middle_kernel,
        grid=(count // tile,),
        in_specs=[
            wide, pl.BlockSpec((D, D), lambda t: (0, 3)), wide,
            pl.BlockSpec((7, D), lambda t: (0, 0)),
        ],
        out_specs=[wide, wide],
        out_shape=[
            jax.ShapeDtypeStruct((count, D), f32),
            jax.ShapeDtypeStruct((count, D), bf16),
        ],
        compiler_params=params(32),
        cost_estimate=cost(2 * count * D * D, 10 * count * D),
        name="middle",
    )(ctx, weights, x, vectors)


ERF_P = 0.3275911 / math.sqrt(2.0)
ERF_COEF = (0.254829592, -0.284496736, 1.421413741, -1.453152027, 1.061405429)


def gelu_parts(u):
    bell = jnp.exp2(u * u * (-0.5 * LOG2E))
    t = 1.0 / (1.0 + ERF_P * jnp.abs(u))
    poly = ERF_COEF[4]
    for coef in ERF_COEF[3::-1]:
        poly = poly * t + coef
    tail = (0.5 * poly * t) * bell
    phi = jnp.where(u >= 0, 1.0 - tail, tail)
    return u * phi, phi + u * (bell * (1.0 / math.sqrt(2.0 * math.pi)))


def mlp_kernel(
    me_ref, c_ref, dm_ref, wu_ref, wd_ref, bias_ref,
    mlp_ref, dc_ref, keep_ref, send_ref, gbias_ref, ct_scr, dmt_scr, *, blocks, split,
):
    first = (pl.program_id(0) == 0) & (pl.program_id(1) == 0)

    @pl.when(first)
    def _():
        ct_scr[...] = c_ref[...].T
        dmt_scr[...] = dm_ref[...].T
        mlp_ref[...] = jnp.zeros_like(mlp_ref)
        dc_ref[...] = jnp.zeros_like(dc_ref)

    width = wu_ref.shape[-1]
    wu = wu_ref[...].reshape(D, width)
    wd = wd_ref[...].reshape(D, width)
    u = dot_ab(c_ref[...], wu) + bias_ref[0]
    act, slope = gelu_parts(u)
    act = act.astype(bf16)
    du = slope * dot_ab(dm_ref[...], wd)
    du = du.astype(bf16)
    gbias_ref[0] = jnp.broadcast_to(jnp.sum(du.astype(f32), 0, keepdims=True), (8, width))
    mlp_ref[...] += dot_ab(act, wd, 1, 1)
    dc_ref[...] += dot_ab(du, wu, 1, 1)
    size = D // blocks
    for which, grad in enumerate((dot_ab(ct_scr[...], du), dot_ab(dmt_scr[...], act))):
        if not split:
            keep_ref[0, 0, which] = grad.astype(bf16)
            continue
        on_high = (me_ref[2] & 1) != 0
        for block in range(0, blocks, 2):
            low = grad[block * size : (block + 1) * size]
            high = grad[(block + 1) * size : (block + 2) * size]
            keep_ref[block // 2, 0, which] = jnp.where(on_high, high, low).astype(bf16)
            send_ref[block // 2, 0, which] = jnp.where(on_high, low, high).astype(bf16)
    if not split:
        send_ref[...] = jnp.zeros_like(send_ref)


def mlp_all(me, c, dm, weights, bias, split):
    count = c.shape[0]
    blocks, mp, _, size, units = weights.shape
    width = 384
    subs = units // width
    half = blocks // 2 if split else 1
    sent = size if split else 8
    rows_out = size if split else D
    all_rows = pl.BlockSpec((count, D), lambda j, s, me: (0, 0))

    def weight_spec(which):
        return pl.BlockSpec(
            (blocks, 1, 1, size, width), lambda j, s, me, which=which: (0, me[1] ^ j, which, 0, s)
        )

    return pl.pallas_call(
        partial(mlp_kernel, blocks=blocks, split=split),
        grid_spec=pltpu.PrefetchScalarGridSpec(
            num_scalar_prefetch=1,
            grid=(mp, subs),
            in_specs=[
                all_rows, all_rows, weight_spec(0), weight_spec(1),
                pl.BlockSpec((1, 1, width), lambda j, s, me: ((me[1] ^ j) * subs + s, 0, 0)),
            ],
            out_specs=[
                all_rows, all_rows,
                pl.BlockSpec((half, 1, 2, rows_out, width), lambda j, s, me: (0, j, 0, 0, s)),
                pl.BlockSpec((half, 1, 2, sent, width), lambda j, s, me: (0, j, 0, 0, s)),
                pl.BlockSpec((1, 8, width), lambda j, s, me: ((me[1] ^ j) * subs + s, 0, 0)),
            ],
            scratch_shapes=[pltpu.VMEM((D, count), bf16), pltpu.VMEM((D, count), bf16)],
        ),
        out_shape=[
            jax.ShapeDtypeStruct((count, D), f32),
            jax.ShapeDtypeStruct((count, D), f32),
            jax.ShapeDtypeStruct((half, mp, 2, rows_out, units), bf16),
            jax.ShapeDtypeStruct((half, mp, 2, sent, units), bf16),
            jax.ShapeDtypeStruct((mp * subs, 8, width), f32),
        ],
        compiler_params=params(58),
        cost_estimate=cost(
            12 * count * D * mp * units, 12 * count * D + 8 * mp * units * D, 2 * count * mp * units
        ),
        name="mlp_all",
    )(me, c, dm, weights, weights, bias.reshape(mp * subs, 1, width))


def turn_kernel(
    x_ref, dy_ref, att_ref, mlp_ref, dc_ref, ctx_ref, wo_ref, vec_ref,
    y_ref, part_ref, dctx_ref, gwo_ref, gvec_ref, datt_scr,
):
    step = pl.program_id(0)

    @pl.when(step == 0)
    def _():
        gvec_ref[...] = jnp.zeros_like(gvec_ref)
        gwo_ref[...] = jnp.zeros_like(gwo_ref)

    tile = 64
    router = vec_ref[4:5, :]

    def body(i, carry):
        rows = pl.ds(pl.multiple_of(i * tile, tile), tile)
        x = x_ref[rows, :].astype(f32)
        dy = dy_ref[rows, :].astype(f32)
        att = att_ref[rows, :]
        branch = att + mlp_ref[rows, :] + vec_ref[6:7, :]
        gate = jax.nn.sigmoid(jnp.sum(x * router, -1, keepdims=True) * ROUTER_SCALE)
        y_ref[rows, :] = (x + gate * branch).astype(bf16)
        dr = jnp.sum(dy * branch, -1, keepdims=True) * gate * (1.0 - gate) * ROUTER_SCALE
        e = gate * dy
        normalized, inverse = norm_parts(x + att)
        dc = dc_ref[rows, :]
        dh = norm_back(dc, normalized, inverse, vec_ref[2:3, :])
        datt = (e + dh).astype(bf16)
        datt_scr[rows, :] = datt
        part_ref[rows, :] = dy + dr * router + dh
        for place, term in enumerate(
            (dc * normalized, dc, dr * x, datt.astype(f32), e.astype(bf16).astype(f32))
        ):
            gvec_ref[place : place + 1, :] += jnp.sum(term, 0, keepdims=True)
        return carry

    lax.fori_loop(0, x_ref.shape[0] // tile, body, 0)
    datt = datt_scr[...]
    dctx_ref[...] = dot_ab(datt, wo_ref[...], 1, 1).astype(bf16)
    gwo_ref[...] += dot_ab(ctx_ref[...], datt, 0, 0)


def turn(x, dy, att, mlp, dc, ctx, weights, vectors):
    count = x.shape[0]
    tile = 320
    wide = pl.BlockSpec((tile, D), lambda t: (t, 0))
    return pl.pallas_call(
        turn_kernel,
        grid=(count // tile,),
        in_specs=[
            wide, wide, wide, wide, wide, wide, pl.BlockSpec((D, D), lambda t: (0, 3)),
            pl.BlockSpec((7, D), lambda t: (0, 0)),
        ],
        out_specs=[
            wide, wide, wide, pl.BlockSpec((D, D), lambda t: (0, 0)),
            pl.BlockSpec((8, D), lambda t: (0, 0)),
        ],
        out_shape=[
            jax.ShapeDtypeStruct((count, D), bf16),
            jax.ShapeDtypeStruct((count, D), f32),
            jax.ShapeDtypeStruct((count, D), bf16),
            jax.ShapeDtypeStruct((D, D), f32),
            jax.ShapeDtypeStruct((8, D), f32),
        ],
        scratch_shapes=[pltpu.VMEM((tile, D), bf16)],
        compiler_params=params(48),
        cost_estimate=cost(4 * count * D * D, 26 * count * D),
        name="turn",
    )(x, dy, att, mlp, dc, ctx, weights, vectors)


def finish_kernel(
    dq_ref, dk_ref, dv_ref, wq_ref, wk_ref, wv_ref, x_ref, part_ref, vec_ref, rank_ref, cot_ref,
    out_ref, gvec_ref, da_scr, hi_scr,
):
    @pl.when(pl.program_id(0) == 0)
    def _():
        gvec_ref[...] = jnp.zeros_like(gvec_ref)

    da = dot_ab(dq_ref[...], wq_ref[...], 1, 1)
    da += dot_ab(dk_ref[...], wk_ref[...], 1, 1)
    da_scr[...] = da + dot_ab(dv_ref[...], wv_ref[...], 1, 1)
    tile = 64

    def body(i, carry):
        rows = pl.ds(pl.multiple_of(i * tile, tile), tile)
        normalized, inverse = norm_parts(x_ref[rows, :].astype(f32))
        da = da_scr[rows, :]
        for place, term in enumerate((da * normalized, da)):
            gvec_ref[place : place + 1, :] += jnp.sum(term, 0, keepdims=True)
        grad = part_ref[rows, :] + norm_back(da, normalized, inverse, vec_ref[0:1, :])
        high = grad.astype(bf16)
        hi_scr[rows, 0:D] = high
        hi_scr[rows, D : 2 * D] = (grad - high.astype(f32)).astype(bf16)
        hi_scr[rows, 2 * D :] = jnp.ones((tile, 128), bf16)
        return carry

    lax.fori_loop(0, CAP // tile, body, 0)
    hot = one_hot(rank_ref[0, 0:1, :])
    placed = dot_ab(hot, hi_scr[...], 0, 0)
    kept = 1.0 - placed[:, 2 * D : 2 * D + 1]
    out_ref[0] = placed[:, 0:D] + placed[:, D : 2 * D] + kept * cot_ref[0].astype(f32)


def finish(dq, dk, dv, weights, x, part, vectors, rank, cotangent):
    count = x.shape[0]
    rows = count // CAP
    wide = pl.BlockSpec((CAP, D), lambda r: (r, 0))

    def weight_spec(which):
        return pl.BlockSpec((D, D), lambda r, which=which: (0, which))

    return pl.pallas_call(
        finish_kernel,
        grid=(rows,),
        in_specs=[
            wide, wide, wide, weight_spec(0), weight_spec(1), weight_spec(2), wide, wide,
            pl.BlockSpec((7, D), lambda r: (0, 0)),
            pl.BlockSpec((1, 8, SEQ), lambda r: (r, 0, 0)),
            pl.BlockSpec((1, SEQ, D), lambda r: (r, 0, 0)),
        ],
        out_specs=[
            pl.BlockSpec((1, SEQ, D), lambda r: (r, 0, 0)),
            pl.BlockSpec((8, D), lambda r: (0, 0)),
        ],
        out_shape=[
            jax.ShapeDtypeStruct((rows, SEQ, D), f32),
            jax.ShapeDtypeStruct((8, D), f32),
        ],
        scratch_shapes=[pltpu.VMEM((CAP, D), f32), pltpu.VMEM((CAP, 2 * D + 128), bf16)],
        compiler_params=params(60),
        cost_estimate=cost(2 * count * D * 3 * D + 6 * count * SEQ * D, 24 * count * D),
        name="finish",
    )(dq, dk, dv, weights, weights, weights, x, part, vectors, rank, cotangent)


def place_kernel(y_ref, rank_ref, tok_ref, out_ref, ext_scr):
    ext_scr[:, 0:D] = y_ref[...]
    ext_scr[:, D:] = jnp.ones((CAP, 128), bf16)
    placed = dot_ab(one_hot(rank_ref[0, 0:1, :]), ext_scr[...], 0, 0)
    kept = 1.0 - placed[:, D : D + 1]
    out_ref[0] = (placed[:, 0:D] + kept * tok_ref[0].astype(f32)).astype(bf16)


def place(y, rank, tokens):
    rows = tokens.shape[0]
    return pl.pallas_call(
        place_kernel,
        grid=(rows,),
        in_specs=[
            pl.BlockSpec((CAP, D), lambda r: (r, 0)),
            pl.BlockSpec((1, 8, SEQ), lambda r: (r, 0, 0)),
            pl.BlockSpec((1, SEQ, D), lambda r: (r, 0, 0)),
        ],
        out_specs=pl.BlockSpec((1, SEQ, D), lambda r: (r, 0, 0)),
        out_shape=jax.ShapeDtypeStruct((rows, SEQ, D), bf16),
        scratch_shapes=[pltpu.VMEM((CAP, D + 128), bf16)],
        compiler_params=params(48),
        cost_estimate=cost(2 * rows * CAP * SEQ * D, 10 * rows * CAP * D),
        name="place",
    )(y, rank, tokens)


def order_kernel(me_ref, *refs, plan):
    blocks, core_bit, mp, bit_orders = plan
    *sources, out_ref, sem = refs
    size = D // blocks
    me = me_ref[0]
    copies = []
    for half, bits in enumerate(bit_orders):
        for side in range(2):
            source = sources[half * 2 + side]
            for slot in range(blocks // 2):
                place, rest = slot % mp, slot // mp
                for bit in bits:
                    place |= mp * bit * (rest & 1)
                    rest >>= 1
                place |= core_bit * side
                start = pl.multiple_of((me ^ place) * size, 8)
                copies.append(
                    pltpu.make_async_copy(
                        source.at[slot],
                        out_ref.at[pl.ds(start, size), pl.ds(half * 2 * D, 2 * D)],
                        sem,
                    )
                )
    for copy in copies:
        copy.start()
    for copy in copies:
        copy.wait()


def in_order(me, pieces, plan):
    anywhere = pl.BlockSpec(memory_space=pl.ANY)
    return pl.pallas_call(
        partial(order_kernel, plan=plan),
        grid_spec=pltpu.PrefetchScalarGridSpec(
            num_scalar_prefetch=1,
            grid=(1,),
            in_specs=[anywhere] * len(pieces),
            out_specs=anywhere,
            scratch_shapes=[pltpu.SemaphoreType.DMA],
        ),
        out_shape=jax.ShapeDtypeStruct((D, 4 * D), bf16),
        cost_estimate=cost(0, 16 * D * D),
        name="in_order",
    )(me, *pieces)


def lamb_moments(weight, gradient, first_mom, second_mom, decay):
    first_new = beta_one * first_mom + (1.0 - beta_one) * gradient
    second_new = beta_two * second_mom + (1.0 - beta_two) * gradient * gradient
    update = (
        first_new
        / (1.0 - beta_one**STEP)
        / (jnp.sqrt(second_new / (1.0 - beta_two**STEP)) + eps_adam)
        + decay * weight
    )
    return (first_new, second_new, update)


def swap(value, axis, size, bit):
    return lax.ppermute(value, axis, [(i, i ^ bit) for i in range(size)])


def on_device(
    tokens, image_ids, selected, cotangent,
    qkv_weight, qkv_first, qkv_second, proj_weight, proj_first, proj_second,
    up_weight, up_first, up_second, down_weight, down_first, down_second,
    up_bias, bias_first, bias_second, vectors, vector_first, vector_second,
    *, dp, mp,
):
    world = dp * mp
    dq_at, dc_at, mp_at = (lax.axis_index(name) for name in ("dq", "dc", "mp"))
    dp_at = dq_at * 2 + dc_at
    me = jnp.stack([dp_at * mp + mp_at, mp_at, dp_at]).astype(jnp.int32)
    everyone = ("dq", "dc", "mp")
    fast = (D // world) % 8 == 0 and dp >= 4 and (D // dp) % 16 == 0

    def swap_dp(value, bit):
        if bit == 1:
            return swap(value, "dc", 2, 1)
        return swap(value, "dq", dp // 2, bit // 2)

    def swap_mp(value, bit):
        return swap(value, "mp", mp, bit)

    bits = []
    bit = 2
    while bit < dp:
        bits.append(bit)
        bit *= 2
    bit_orders = (tuple(bits), tuple(reversed(bits)))

    attn_low = jnp.concatenate([qkv_weight, proj_weight], 1).astype(bf16)
    mlp_low = jnp.stack([up_weight.astype(bf16), down_weight.astype(bf16).T])
    if fast:
        rel = [attn_low[None]] + [swap_mp(attn_low[None], k) for k in range(1, mp)]
        rel = jnp.concatenate(rel, 0)
        pieces = []
        for half, order in enumerate(bit_orders):
            held = rel[:, :, half * 2 * D : (half + 1) * 2 * D]
            for bit in order:
                held = jnp.concatenate([held, swap_dp(held, bit)], 0)
            pieces += [held, swap_dp(held, 1)]
        attn_mat = in_order(me, pieces, (world, mp, mp, bit_orders))
    else:
        attn_mat = lax.all_gather(attn_low, everyone, axis=0, tiled=True)
    mlp_mat = lax.all_gather(mlp_low[None], everyone, axis=0, tiled=True)
    mlp_mat = mlp_mat.reshape(dp, mp, 2, D // dp, FF // mp)
    if not fast:
        mlp_mat = mlp_mat.transpose(1, 2, 0, 3, 4).reshape(1, mp, 2, D, FF // mp)

    x, dy, a, at, dm, rank, bounds = pick_rows(selected, image_ids, tokens, cotangent, vectors)
    q, k, v, ctx, lse = attend_forward(a, attn_mat, bounds)
    att, c = middle(ctx, attn_mat, x, vectors)
    mlp, dc, mlp_keep, mlp_send, bias_rows = mlp_all(me, c, dm, mlp_mat, up_bias, fast)
    y, part, dctx, gwo, gvec_two = turn(x, dy, att, mlp, dc, ctx, attn_mat, vectors)
    plan = (world, mp) if fast else None
    dq, dk, dv, attn_keep, attn_send = attend_backward(
        me, at, q, k, v, ctx, dctx, lse, bounds, gwo, plan
    )
    input_grad, gvec_one = finish(dq, dk, dv, attn_mat, x, part, vectors, rank, cotangent)
    block_output = place(y, rank, tokens)

    def add(kept, came):
        return (kept.astype(f32) + came.astype(f32)).astype(bf16)

    if fast:
        both = add(mlp_keep, swap_dp(mlp_send, 1))
        mine = lax.psum_scatter(both, "dq", scatter_dimension=0, tiled=True)[0]
        mlp_sum = mine[0].astype(f32)
        for k_at in range(1, mp):
            mlp_sum = mlp_sum + swap_mp(mine[k_at], k_at).astype(f32)
        both = add(attn_keep, swap_dp(attn_send, 1))
        parts = []
        for half, order in enumerate(bit_orders):
            held = both[:, :, half * 2 * D : (half + 1) * 2 * D]
            held = held.reshape((2,) * len(bits) + (mp, D // world, 2 * D))
            left = list(reversed(bits))
            for bit in reversed(order):
                axis = left.index(bit)
                left.remove(bit)
                low = lax.index_in_dim(held, 0, axis, False)
                high = lax.index_in_dim(held, 1, axis, False)
                held = add(low, swap_dp(high, bit))
            total = held[0].astype(f32)
            for k_at in range(1, mp):
                total = total + swap_mp(held[k_at], k_at).astype(f32)
            parts.append(total)
        attn_sum = jnp.concatenate(parts, 1)
    else:
        shaped = mlp_keep[0].reshape(mp, 2, dp, D // dp, FF // mp)
        shaped = jnp.take(shaped, mp_at ^ jnp.arange(mp), axis=0)
        shaped = shaped.transpose(2, 0, 1, 3, 4).reshape(world, 2, D // dp, FF // mp)
        mlp_sum = lax.psum_scatter(shaped, everyone, scatter_dimension=0, tiled=True)[0]
        mlp_sum = mlp_sum.astype(f32)
        attn_sum = lax.psum_scatter(attn_keep[0], everyone, scatter_dimension=0, tiled=True)
        attn_sum = attn_sum.astype(f32)
    attn_sum = attn_sum.reshape(D // world, GROUPS, 4, GROUP).transpose(0, 2, 1, 3)
    attn_sum = attn_sum.reshape(D // world, 4 * D)
    qkv_sum, proj_sum = attn_sum[:, : 3 * D], attn_sum[:, 3 * D :]
    up_sum, down_sum = mlp_sum[0], mlp_sum[1].T

    qkv_first_new, qkv_second_new, qkv_upd = lamb_moments(
        qkv_weight, qkv_sum, qkv_first, qkv_second, decay_mat
    )
    proj_first_new, proj_second_new, proj_upd = lamb_moments(
        proj_weight, proj_sum, proj_first, proj_second, decay_mat
    )
    up_first_new, up_second_new, up_upd = lamb_moments(
        up_weight, up_sum, up_first, up_second, decay_mat
    )
    down_first_new, down_second_new, down_upd = lamb_moments(
        down_weight, down_sum, down_first, down_second, decay_mat
    )
    squares = jnp.stack(
        [
            jnp.sum(value * value)
            for value in (
                qkv_weight, proj_weight, up_weight, down_weight,
                qkv_upd, proj_upd, up_upd, down_upd,
            )
        ]
    )
    small = jnp.concatenate(
        [
            gvec_one[0:2].reshape(-1),
            gvec_two[0:5].reshape(-1),
            bias_rows[:, 0, :].reshape(-1),
            jnp.pad(squares, (0, 120)),
        ]
    ).reshape(-1, 128)
    if fast:
        bit = 1
        while bit < dp:
            small = small + swap_dp(small, bit)
            bit *= 2
        bit = 1
        while bit < mp:
            small = small + swap_mp(small, bit)
            bit *= 2
    else:
        small = lax.psum(small, everyone)
    small = small.reshape(-1)
    vector_sum = small[: 7 * D].reshape(7, D)
    bias_sum = small[7 * D : 7 * D + FF]
    weight_norms = jnp.sqrt(small[7 * D + FF : 7 * D + FF + 8]).reshape(2, 4)
    ratios = weight_norms[0] / weight_norms[1]
    qkv_new = qkv_weight - rate_lamb * ratios[0] * qkv_upd
    proj_new = proj_weight - rate_lamb * ratios[1] * proj_upd
    up_new = up_weight - rate_lamb * ratios[2] * up_upd
    down_new = down_weight - rate_lamb * ratios[3] * down_upd
    bias_first_new, bias_second_new, bias_upd = lamb_moments(
        up_bias, bias_sum, bias_first, bias_second, 0.0
    )
    bias_ratio = jnp.sqrt(jnp.sum(up_bias * up_bias)) / jnp.sqrt(jnp.sum(bias_upd * bias_upd))
    bias_new = up_bias - rate_lamb * bias_ratio * bias_upd
    vector_first_new, vector_second_new, vector_upd = lamb_moments(
        vectors, vector_sum, vector_first, vector_second, 0.0
    )
    vector_ratio = jnp.sqrt(jnp.sum(vectors * vectors, -1, keepdims=True)) / jnp.sqrt(
        jnp.sum(vector_upd * vector_upd, -1, keepdims=True)
    )
    vectors_new = vectors - rate_lamb * vector_ratio * vector_upd
    return (
        block_output, input_grad, weight_norms,
        qkv_new, qkv_first_new, qkv_second_new,
        proj_new, proj_first_new, proj_second_new,
        up_new, up_first_new, up_second_new,
        down_new, down_first_new, down_second_new,
        bias_new, bias_first_new, bias_second_new,
        vectors_new, vector_first_new, vector_second_new,
    )


def solution(mesh):
    dp, mp = mesh.shape["dp"], mesh.shape["mp"]
    split = Mesh(mesh.devices.reshape(dp // 2, 2, mp), ("dq", "dc", "mp"))
    rows = ("dq", "dc", "mp")
    by_rows = (P(rows, None),) * 3
    shared = (P(),) * 3
    up_spec = (P(("dq", "dc"), "mp"),) * 3
    down_spec = (P("mp", ("dq", "dc")),) * 3
    in_specs = (
        (P(rows, None, None), P(rows, None), P(rows, None), P(rows, None, None))
        + by_rows + by_rows + up_spec + down_spec + shared + shared
    )
    out_specs = (
        (P(rows, None, None), P(rows, None, None), P())
        + by_rows + by_rows + up_spec + down_spec + shared + shared
    )
    return jax.shard_map(
        partial(on_device, dp=dp, mp=mp),
        mesh=split, in_specs=in_specs, out_specs=out_specs, check_vma=False,
    )
```

time: 1120 us -> 656 us (0.59)
  matrix products: 424 us -> 0 us
  Pallas kernels: 0 us -> 353 us
  local copies, waits for them, and re-layouts: 273 us -> 31.5 us
  waiting for transfers between devices: 263 us -> 177 us
  other arithmetic: 83 us -> 33.4 us
  blocking collectives: 39.9 us -> 0 us
  starting transfers between devices: 0.72 us -> 34.5 us
    dot_general x180 -> x0, matrix products: 424 us -> none  [the longest x48 73.4 us: head_scores(): jnp.dot(queries, key_rows.T, preferred_element_type=jnp.float32)]
    pallas_call x0 -> x9, Pallas kernels: none -> 353 us  [the longest x1 145 us: in_order(): pl.pallas_call(partial(order_kernel, plan=plan), grid_spec=pltpu.Prefetch...]
    reduce_scatter x5 -> x0, waiting for transfers between devices: 158 us -> none  [the longest x1 113 us: on_device(): lax.psum_scatter(qkv_grad, ('dp', 'mp'), scatter_dimension=0, tiled=True)]
    ppermute x0 -> x29, waiting for transfers between devices: none -> 96.4 us  [swap(): return lax.ppermute(value, axis, [(i, i ^ bit) for i in range(size)])]
    all_gather x6 -> x1, waiting for transfers between devices: 63.1 us -> 0.01 us  [on_device(): mlp_mat = lax.all_gather(mlp_low[None], everyone, axis=0, tiled=True)]
    gather x7 -> x0, local copies, waits for them, and re-layouts: 59.8 us -> none  [the longest x2 24.8 us: on_device(): jnp.take_along_axis(cotangent, picked[:, :, None], axis=1)]
    reshape x17 -> x5, local copies, waits for them, and re-layouts: 53.7 us -> 0.97 us  [the longest x1 0.61 us: on_device(): gvec_two[0:5].reshape(-1)]
    unnamed x173 -> x103, local copies, waits for them, and re-layouts: 60.4 us -> 16.8 us
  transfers between devices with their start and end apart: 12 -> 31, of which waited for: 6 -> 18; matrix products, arithmetic and copies ran while one was open for 65% -> 3% of each run, Pallas kernels for 0% -> 45%
where the time goes in v1:
time: 656 us; the launch traced here: 649 us
  Pallas kernels  353 us (54%)
  waiting for transfers between devices  177 us (27%)
  starting transfers between devices  34.5 us (5%)
  other arithmetic  33.4 us (5%)
  local copies, waits for them, and re-layouts  31.5 us (5%)
  between operations  19.2 us (3%)
    pallas_call x1, Pallas kernels, in_order(): pl.pallas_call(partial(order_kernel, plan=plan), grid_spec=pltpu.Prefetch...  145 us
    ppermute x29, waiting for transfers between devices, swap(): return lax.ppermute(value, axis, [(i, i ^ bit) for i in range(size)])  96.4 us
    unnamed x3, waiting for transfers between devices  80.9 us
    pallas_call x1, Pallas kernels, mlp_all(): pl.pallas_call(partial(mlp_kernel, blocks=blocks, split=split), grid_spec...  62.9 us
    pallas_call x1, Pallas kernels, attend_backward(): pl.pallas_call(partial(attend_back_kernel, plan=plan), grid_spec=pltpu.Pr...  45.5 us
    ppermute x29, starting transfers between devices, swap(): return lax.ppermute(value, axis, [(i, i ^ bit) for i in range(size)])  34.4 us
    pallas_call x1, Pallas kernels, finish(): pl.pallas_call(finish_kernel, grid=(rows,), in_specs=[wide, wide, wide, w...  29.5 us
    pallas_call x1, Pallas kernels, attend_forward(): pl.pallas_call(attend_kernel, grid=(rows, GROUPS), in_specs=[pl.BlockSpec...  29.4 us
  transfers between devices with their start and end apart: 31, of which 18 were waited for; matrix products, arithmetic and copies ran while one was open for 3% of the time, Pallas kernels for 45%

profile of v1, /device:TPU:0, one launch (start us, length us, event | category | flops | bytes accessed | tf_op | source)
XLA Modules:
  0.0 648.8 jit_solution(6162842361625025475)
XLA Ops:
  11.0 5.1 collective-permute-start.2
  16.8 4.1 collective-permute-done.2
  20.9 11.5 %collective-permute-done.1 = bf16[1,24,3072]{2,1,0:T(8,128)(2,1)S(1)} collective-permute-done((bf16[1,24,3072]{2,1,0:T(8,128)(2,1)S(1)}, bf16[1,24,3072]{2,1,0:T(8,128)(2,1)S(1)}, u32[]{:S(2)}, u32[]{:S(2)}) %collective-permute-start.1) | collective-permute-done | bytes 147488 | tf_op jit(solution)/shard_map/ppermute | solution.py:698
  32.5 1.6 collective-permute-start.3
  34.1 2.3 collective-permute-start.6
  36.4 2.9 collective-permute-done.3
  39.4 2.3 collective-permute-start.4
  41.7 3.4 collective-permute-done.6
  45.3 12.7 %collective-permute-done.4 = bf16[8,24,1536]{2,1,0:T(8,128)(2,1)S(1)} collective-permute-done((bf16[8,24,1536]{2,1,0:T(8,128)(2,1)S(1)}, bf16[8,24,1536]{2,1,0:T(8,128)(2,1)S(1)}, u32[]{:S(2)}, u32[]{:S(2)}) %collective-permute-start.4) | collective-permute-done | bytes 589856 | tf_op jit(solution)/shard_map/ppermute | solution.py:698
  58.2 3.0 collective-permute-done.7
  63.0 13.0 %pick_rows.1 = (bf16[1280,768]{1,0:T(8,128)(2,1)S(1)}, bf16[1280,768]{1,0:T(8,128)(2,1)S(1)}, bf16[1280,768]{1,0:T(8,128)(2,1)S(1)}, bf16[768,1280]{1,0:T(8,128)...) custom-call(s32[2,1,1280]{2,1,0:T(1,128)S(1)} %broadcast_in_dim.6.sel_ref, ...), custom_call_target="tpu_custom_call" | custom-call | flops 5033164800 | bytes 15728640 | tf_op jit(solution)/shard_map/pick_rows/pallas_call | solution.py:126
  76.0 1.3 copy-done.6
  78.0 1.3 copy-done.13
  79.3 144.7 %in_order.1.wq_ref.wk_ref.wv_ref.wo_ref = bf16[768,3072]{1,0:T(8,128)(2,1)} custom-call(s32[3]{0:T(128)} %pad_add_fusion.me_ref, bf16[16,24,1536]{2,1,0:T(8,128)(2,1)} %copy-done.18, bf16[16,24,1536]{2,1,0:T(8,128)(2,1)} %collective-permute-done.5.refs_1_, bf16[16,24,1536]{2,1,0:T(8,128)(2,1)} %pad_maximum_fusion.1.refs_2_, ...), custom_call_target="tpu_custom_call" | custom-call | bytes 9437184 | tf_op jit(solution)/shard_map/in_order/pallas_call | solution.py:670
  224.0 29.4 %attend_forward.1 = (bf16[1280,768]{1,0:T(8,128)(2,1)S(1)}, bf16[1280,768]{1,0:T(8,128)(2,1)S(1)}, bf16[1280,768]{1,0:T(8,128)(2,1)}, bf16[1280,768]{1,0:T(8,128)(2,1)}, f32[1280,128]{1,0:T(8,128)S(1)}) custom-call(bf16[1280,768]{1,0:T(8,128)(2,1)} %copy-done.13, bf16[768,3072]{1,0:T(8,128)(2,1)} %in_order.1.wq_ref.wk_ref.wv_ref.wo_ref, ...), custom_call_target="tpu_custom_call" | custom-call | flops 14596177920 | bytes 11796480 | tf_op jit(solution)/shard_map/attend_forward/pallas_call | solution.py:208
  253.5 1.3 copy-done.14
  254.8 1.3 copy-done.15
  256.9 1.5 copy-done.1
  258.4 3.4 middle.1
  261.8 1.9 copy-done.3
  263.7 1.3 copy-done.12
  265.0 62.9 %mlp_all.1 = (f32[1280,768]{1,0:T(8,128)}, f32[1280,768]{1,0:T(8,128)}, bf16[4,4,2,96,768]{4,3,2,1,0:T(8,128)(2,1)}, bf16[4,4,2,96,768]{4,3,2,1,0:T(8,128)(2,1)}, f32[8,8,384]{2,1,0:T(8,128)}) custom-call(s32[3]{0:T(128)} %pad_add_fusion.me_ref, bf16[1280,768]{1,0:T(8,128)(2,1)} %copy-done.12, bf16[1280,768]{1,0:T(8,128)(2,1)} %get-tuple-element.59.dm_ref, ...), custom_call_target="tpu_custom_call" | custom-call | flops 36238786560 | bytes 30670848 | tf_op jit(solution)/shard_map/mlp_all/pallas_call | solution.py:444
  328.4 17.8 %turn.1 = (bf16[1280,768]{1,0:T(8,128)(2,1)S(1)}, f32[1280,768]{1,0:T(8,128)}, bf16[1280,768]{1,0:T(8,128)(2,1)S(1)}, f32[768,768]{1,0:T(8,128)}, f32[8,768]{1,0:T(8,128)S(1)}) custom-call(bf16[1280,768]{1,0:T(8,128)(2,1)S(1)} %get-tuple-element.52.x_ref, bf16[1280,768]{1,0:T(8,128)(2,1)} %copy-done.6, f32[1280,768]{1,0:T(8,128)} %copy-done.3, ...), custom_call_target="tpu_custom_call" | custom-call | flops 3019898880 | bytes 25559040 | tf_op jit(solution)/shard_map/turn/pallas_call | solution.py:522
  346.2 1.3 copy-done.4
  347.5 1.3 copy-done.11
  348.8 45.5 %attend_backward.1 = (bf16[1280,768]{1,0:T(8,128)(2,1)}, bf16[1280,768]{1,0:T(8,128)(2,1)}, bf16[1280,768]{1,0:T(8,128)(2,1)}, bf16[16,24,3072]{2,1,0:T(8,128)(2,1)}, bf16[16,24,3072]{2,1,0:T(8,128)(2,1)}) custom-call(s32[3]{0:T(128)} %pad_add_fusion.me_ref, bf16[768,1280]{1,0:T(8,128)(2,1)} %get-tuple-element.64.at_ref, bf16[1280,768]{1,0:T(8,128)(2,1)} %copy-done.14, ...), custom_call_target="tpu_custom_call" | custom-call | flops 29695672320 | bytes 19660800 | tf_op jit(solution)/shard_map/attend_backward/pallas_call | solution.py:313
  395.0 1.5 slice.141
  397.1 29.5 %finish.1 = (f32[2,1280,768]{2,1,0:T(8,128)}, f32[8,768]{1,0:T(8,128)}) custom-call(bf16[1280,768]{1,0:T(8,128)(2,1)} %get-tuple-element.71.dq_ref, bf16[1280,768]{1,0:T(8,128)(2,1)} %get-tuple-element.72.dk_ref, bf16[1280,768]{1,0:T(8,128)(2,1)} %get-tuple-element.73.dv_ref, bf16[768,3072]{1,0:T(8,128)(2,1)} %in_order.1.wq_ref.wk_ref.wv_ref.wo_ref, ...), custom_call_target="tpu_custom_call" | custom-call | flops 12079595520 | bytes 23592960 | tf_op jit(solution)/shard_map/finish/pallas_call | solution.py:588
  427.5 2.7 add_convert_fusion.1
  431.1 1.6 collective-permute-start.15
  433.7 1.4 collective-permute-start.10
  435.0 5.8 add_convert_fusion
  440.9 7.0 %collective-permute-done.15 = bf16[2,4,24,1536]{3,2,1,0:T(8,128)(2,1)S(1)} collective-permute-done((bf16[2,4,24,1536]{3,2,1,0:T(8,128)(2,1)}, bf16[2,4,24,1536]{3,2,1,0:T(8,128)(2,1)S(1)}, u32[]{:S(2)}, u32[]{:S(2)}) %collective-permute-start.15) | collective-permute-done | bytes 589856 | tf_op jit(solution)/shard_map/ppermute | solution.py:698
  449.2 3.8 collective-permute-done.10
  453.2 11.6 %collective-permute-done.16 = bf16[4,24,1536]{2,1,0:T(8,128)(2,1)S(1)} collective-permute-done((bf16[4,24,1536]{2,1,0:T(8,128)(2,1)S(1)}, bf16[4,24,1536]{2,1,0:T(8,128)(2,1)S(1)}, u32[]{:S(2)}, u32[]{:S(2)}) %collective-permute-start.16) | collective-permute-done | bytes 294944 | tf_op jit(solution)/shard_map/ppermute | solution.py:698
  465.0 2.0 collective-permute-start.19
  466.9 2.5 collective-permute-start.17
  469.5 2.0 collective-permute-start.14
  471.5 2.5 collective-permute-start.12
  474.0 2.9 collective-permute-done.18
  477.0 1.6 collective-permute-done.13
  479.1 80.9 %all-reduce.4.cloned.1.call-done = bf16[4,4,2,96,768]{4,3,2,1,0:T(8,128)(2,1)} async-done(((bf16[4,4,2,96,768]{4,3,2,1,0:T(8,128)(2,1)}), bf16[4,4,2,96,768]{4,3,2,1,0:T(8,128)(2,1)}) %all-reduce.4.cloned.1.call-update) | async-done | bytes 4718608
  560.0 1.8 dynamic-slice_bitcast_fusion.2
  561.9 3.4 collective-permute-start.23
  566.3 1.3 multiply_reduce_fusion.6
  567.6 1.5 multiply_reduce_fusion.4
  569.1 4.6 collective-permute-done.23
  573.7 16.8 %collective-permute-done.22 = bf16[2,96,768]{2,1,0:T(8,128)(2,1)S(1)} collective-permute-done((bf16[2,96,768]{2,1,0:T(8,128)(2,1)S(1)}, bf16[2,96,768]{2,1,0:T(8,128)(2,1)S(1)}, u32[]{:S(2)}, u32[]{:S(2)}) %collective-permute-start.22) | collective-permute-done | bytes 294944 | tf_op jit(solution)/shard_map/ppermute | solution.py:698
  590.6 1.8 fusion.3
  592.4 1.6 multiply_reduce_fusion.1
  594.0 1.7 multiply_reduce_fusion
  595.6 5.3 stack.63
  601.6 1.2 collective-permute-done.24
  603.6 1.5 collective-permute-start.25
  605.1 2.5 collective-permute-done.25
  608.3 1.4 collective-permute-start.26
  609.7 2.7 collective-permute-done.26
  612.3 3.9 collective-permute-done.27
  616.3 1.3 collective-permute-start.28
  617.6 2.1 copy-done.2
  619.7 6.5 %place.1 = bf16[2,1280,768]{2,1,0:T(8,128)(2,1)} custom-call(bf16[1280,768]{1,0:T(8,128)(2,1)S(1)} %copy-done.5, s32[2,8,1280]{2,1,0:T(8,128)S(1)} %copy-done.10, bf16[2,1280,768]{2,1,0:T(8,128)(2,1)S(1)} %copy-done.2), custom_call_target="tpu_custom_call" | custom-call | flops 2516582400 | bytes 9830400 | tf_op jit(solution)/shard_map/place/pallas_call | solution.py:622
  631.3 1.4 multiply_reduce_fusion.10
  635.1 1.8 multiply_subtract_fusion.2
  636.8 1.6 multiply_subtract_fusion.3
  (181 shorter events, 24.6 us)
Async XLA Ops:
  7.2 257.8 %all-gather.3.cloned.1.call-start = ((), (), s32[]{:S(2)}) async-start(), calls=%async_computation | async-start | bytes 9732096 | tf_op jit(solution)/shard_map/all_gather | solution.py:744
  10.0 550.0 %all-reduce.4.cloned.1.call-start = ((), (), s32[]{:S(2)}) async-start(), calls=%async_computation.1 | async-start | bytes 9437184
  11.0 9.9 %collective-permute-start.2 = (bf16[1,24,3072]{2,1,0:T(8,128)(2,1)S(1)}, bf16[1,24,3072]{2,1,0:T(8,128)(2,1)S(1)}, u32[]{:S(2)}, u32[]{:S(2)}) collective-permute-start(bf16[1,24,3072]{2,1,0:T(8,128)(2,1)S(1)} %pad_maximum_fusion.7), channel_id=1, source_target_pairs={{0,3},{1,2},{2,1},{3,0},{4,7},{5,6},{6,5},{7,4},{8,11},{9,10},{10,... | collective-permute-start | bytes 442376 | tf_op jit(solution)/shard_map/ppermute | solution.py:698
  16.1 16.3 %collective-permute-start.1 = (bf16[1,24,3072]{2,1,0:T(8,128)(2,1)S(1)}, bf16[1,24,3072]{2,1,0:T(8,128)(2,1)S(1)}, u32[]{:S(2)}, u32[]{:S(2)}) collective-permute-start(bf16[1,24,3072]{2,1,0:T(8,128)(2,1)S(1)} %pad_maximum_fusion.7), channel_id=1, source_target_pairs={{0,2},{1,3},{2,0},{3,1},{4,6},{5,7},{6,4},{7,5},{8,10},{9,11},{10,... | collective-permute-start | bytes 442376 | tf_op jit(solution)/shard_map/ppermute | solution.py:698
  16.1 16.3 %collective-permute-start = (bf16[1,24,3072]{2,1,0:T(8,128)(2,1)S(1)}, bf16[1,24,3072]{2,1,0:T(8,128)(2,1)S(1)}, u32[]{:S(2)}, u32[]{:S(2)}) collective-permute-start(bf16[1,24,3072]{2,1,0:T(8,128)(2,1)S(1)} %pad_maximum_fusion.7), channel_id=1, source_target_pairs={{0,1},{1,0},{2,3},{3,2},{4,5},{5,4},{6,7},{7,6},{8,9},{9,8},{10,11... | collective-permute-start | bytes 442376 | tf_op jit(solution)/shard_map/ppermute | solution.py:698
  32.5 6.8 %collective-permute-start.3 = (bf16[4,24,1536]{2,1,0:T(8,128)(2,1)S(1)}, bf16[4,24,1536]{2,1,0:T(8,128)(2,1)S(1)}, u32[]{:S(2)}, u32[]{:S(2)}) collective-permute-start(bf16[4,24,1536]{2,1,0:T(8,128)(2,1)S(1)} %get-tuple-element.113), channel_id=1, source_target_pairs={{0,8},{8,0},{16,24},{24,16},{1,9},{9,1},{17,25},{25,17},{2,10},{10... | collective-permute-start | bytes 884744 | tf_op jit(solution)/shard_map/ppermute | solution.py:698
  34.1 11.0 %collective-permute-start.6 = (bf16[4,24,1536]{2,1,0:T(8,128)(2,1)S(1)}, bf16[4,24,1536]{2,1,0:T(8,128)(2,1)S(1)}, u32[]{:S(2)}, u32[]{:S(2)}) collective-permute-start(bf16[4,24,1536]{2,1,0:T(8,128)(2,1)S(1)} %get-tuple-element.112), channel_id=1, source_target_pairs={{0,16},{8,24},{16,0},{24,8},{1,17},{9,25},{17,1},{25,9},{2,18},{10... | collective-permute-start | bytes 884744 | tf_op jit(solution)/shard_map/ppermute | solution.py:698
  39.4 18.6 %collective-permute-start.4 = (bf16[8,24,1536]{2,1,0:T(8,128)(2,1)S(1)}, bf16[8,24,1536]{2,1,0:T(8,128)(2,1)S(1)}, u32[]{:S(2)}, u32[]{:S(2)}) collective-permute-start(bf16[8,24,1536]{2,1,0:T(8,128)(2,1)S(1)} %pad_maximum_fusion.3), channel_id=1, source_target_pairs={{0,16},{8,24},{16,0},{24,8},{1,17},{9,25},{17,1},{25,9},{2,18},{10... | collective-permute-start | bytes 1769480 | tf_op jit(solution)/shard_map/ppermute | solution.py:698
  45.2 17.2 %copy-start.44 = (s32[2,1280]{1,0:T(2,128)S(1)}, s32[2,1280]{1,0:T(2,128)}, u32[]{:S(2)}) copy-start(s32[2,1280]{1,0:T(2,128)} %param.24) | copy-start | bytes 30724
  45.2 17.2 %copy-start.45 = (s32[2,1280]{1,0:T(2,128)S(1)}, s32[2,1280]{1,0:T(2,128)}, u32[]{:S(2)}) copy-start(s32[2,1280]{1,0:T(2,128)} %param.23) | copy-start | bytes 30724
  45.2 17.8 %copy-start.7 = (f32[7,768]{1,0:T(8,128)S(1)}, f32[7,768]{1,0:T(8,128)}, u32[]{:S(2)}) copy-start(f32[7,768]{1,0:T(8,128)} %vec_ref.7) | copy-start | bytes 64516
  45.2 16.0 %collective-permute-start.7 = (bf16[8,24,1536]{2,1,0:T(8,128)(2,1)S(1)}, bf16[8,24,1536]{2,1,0:T(8,128)(2,1)S(1)}, u32[]{:S(2)}, u32[]{:S(2)}) collective-permute-start(bf16[8,24,1536]{2,1,0:T(8,128)(2,1)S(1)} %pad_maximum_fusion.4), channel_id=1, source_target_pairs={{0,8},{8,0},{16,24},{24,16},{1,9},{9,1},{17,25},{25,17},{2,10},{10... | collective-permute-start | bytes 1769480 | tf_op jit(solution)/shard_map/ppermute | solution.py:698
  58.1 17.9 %copy-start.18 = (bf16[16,24,1536]{2,1,0:T(8,128)(2,1)}, bf16[16,24,1536]{2,1,0:T(8,128)(2,1)S(1)}, u32[]{:S(2)}) copy-start(bf16[16,24,1536]{2,1,0:T(8,128)(2,1)S(1)} %pad_maximum_fusion.refs_0_) | copy-start | bytes 3538948
  58.1 21.1 %collective-permute-start.5 = (bf16[16,24,1536]{2,1,0:T(8,128)(2,1)S(1)}, bf16[16,24,1536]{2,1,0:T(8,128)(2,1)}, u32[]{:S(2)}, u32[]{:S(2)}) collective-permute-start(bf16[16,24,1536]{2,1,0:T(8,128)(2,1)S(1)} %pad_maximum_fusion.refs_0_), channel_id=1, source_target_pairs={{0,4},{4,0},{1,5},{5,1},{2,6},{6,2},{3,7},{7,3},{8,12},{12,8},{9,1... | collective-permute-start | bytes 3538952 | tf_op jit(solution)/shard_map/ppermute | solution.py:698
  62.4 16.9 %collective-permute-start.8 = (bf16[16,24,1536]{2,1,0:T(8,128)(2,1)}, bf16[16,24,1536]{2,1,0:T(8,128)(2,1)}, u32[]{:S(2)}, u32[]{:S(2)}) collective-permute-start(bf16[16,24,1536]{2,1,0:T(8,128)(2,1)} %pad_maximum_fusion.1.refs_2_), channel_id=1, source_target_pairs={{0,4},{4,0},{1,5},{5,1},{2,6},{6,2},{3,7},{7,3},{8,12},{12,8},{9,1... | collective-permute-start | bytes 3538952 | tf_op jit(solution)/shard_map/ppermute | solution.py:698
  79.2 144.8 %copy-start.17 = (s32[2,8,128]{2,1,0:T(8,128)}, s32[2,8,128]{2,1,0:T(8,128)S(1)}, u32[]{:S(2)}) copy-start(s32[2,8,128]{2,1,0:T(8,128)S(1)} %get-tuple-element.55.bounds_ref) | copy-start | bytes 24580
  79.2 249.2 %copy-start = (bf16[1280,768]{1,0:T(8,128)(2,1)}, bf16[1280,768]{1,0:T(8,128)(2,1)S(1)}, u32[]{:S(2)}) copy-start(bf16[1280,768]{1,0:T(8,128)(2,1)S(1)} %get-tuple-element.52.x_ref) | copy-start | bytes 5898244
  224.0 32.9 %slice-start = ((s8[4718592]{0:T(1024)(128)(4,1)}), s8[4194304]{0:T(1024)(128)(4,1)S(1)}, s32[]{:S(2)}) async-start(s8[4718592]{0:T(1024)(128)(4,1)} %bitcast.126), calls=%async_computation.2 | async-start | bytes 8388608
  224.0 32.8 %slice-start.1 = ((s8[4718592]{0:T(1024)(128)(4,1)}), s8[524288]{0:T(1024)(128)(4,1)S(1)}, s32[]{:S(2)}) async-start(s8[4718592]{0:T(1024)(128)(4,1)} %bitcast.126), calls=%async_computation.3 | async-start | bytes 1048576
  327.9 107.1 %collective-permute-start.20 = (bf16[4,4,2,96,768]{4,3,2,1,0:T(8,128)(2,1)}, bf16[4,4,2,96,768]{4,3,2,1,0:T(8,128)(2,1)}, u32[]{:S(2)}, u32[]{:S(2)}) collective-permute-start(bf16[4,4,2,96,768]{4,3,2,1,0:T(8,128)(2,1)} %get-tuple-element.82), channel_id=1, source_target_pairs={{0,4},{4,0},{1,5},{5,1},{2,6},{6,2},{3,7},{7,3},{8,12},{12,8},{9,1... | collective-permute-start | bytes 14155784 | tf_op jit(solution)/shard_map/ppermute | solution.py:698
  348.8 45.6 %copy-start.46 = (u32[32]{0:T(128)S(1)}, u32[32]{0:T(128)}, u32[]{:S(2)}) copy-start(u32[32]{0:T(128)} %constant.52) | copy-start | bytes 388
  394.3 33.1 %collective-permute-start.9 = (bf16[16,24,3072]{2,1,0:T(8,128)(2,1)}, bf16[16,24,3072]{2,1,0:T(8,128)(2,1)}, u32[]{:S(2)}, u32[]{:S(2)}) collective-permute-start(bf16[16,24,3072]{2,1,0:T(8,128)(2,1)} %get-tuple-element.80), channel_id=1, source_target_pairs={{0,4},{4,0},{1,5},{5,1},{2,6},{6,2},{3,7},{7,3},{8,12},{12,8},{9,1... | collective-permute-start | bytes 7077896 | tf_op jit(solution)/shard_map/ppermute | solution.py:698
  397.1 30.3 %copy-start.21 = (bf16[16,24,3072]{2,1,0:T(8,128)(2,1)S(1)}, bf16[16,24,3072]{2,1,0:T(8,128)(2,1)}, u32[]{:S(2)}) copy-start(bf16[16,24,3072]{2,1,0:T(8,128)(2,1)} %get-tuple-element.79) | copy-start | bytes 7077892
  431.1 16.8 %collective-permute-start.15 = (bf16[2,4,24,1536]{3,2,1,0:T(8,128)(2,1)}, bf16[2,4,24,1536]{3,2,1,0:T(8,128)(2,1)S(1)}, u32[]{:S(2)}, u32[]{:S(2)}) collective-permute-start(bf16[2,4,24,1536]{3,2,1,0:T(8,128)(2,1)} %slice_bitcast_fusion), channel_id=1, source_target_pairs={{0,8},{8,0},{16,24},{24,16},{1,9},{9,1},{17,25},{25,17},{2,10},{10... | collective-permute-start | bytes 1769480 | tf_op jit(solution)/shard_map/ppermute | solution.py:698
  433.7 19.3 %collective-permute-start.10 = (bf16[2,4,24,1536]{3,2,1,0:T(8,128)(2,1)}, bf16[2,4,24,1536]{3,2,1,0:T(8,128)(2,1)S(1)}, u32[]{:S(2)}, u32[]{:S(2)}) collective-permute-start(bf16[2,4,24,1536]{3,2,1,0:T(8,128)(2,1)} %bitcast.16), channel_id=1, source_target_pairs={{0,16},{8,24},{16,0},{24,8},{1,17},{9,25},{17,1},{25,9},{2,18},{10... | collective-permute-start | bytes 1769480 | tf_op jit(solution)/shard_map/ppermute | solution.py:698
  448.1 16.8 %collective-permute-start.16 = (bf16[4,24,1536]{2,1,0:T(8,128)(2,1)S(1)}, bf16[4,24,1536]{2,1,0:T(8,128)(2,1)S(1)}, u32[]{:S(2)}, u32[]{:S(2)}) collective-permute-start(bf16[4,24,1536]{2,1,0:T(8,128)(2,1)S(1)} %slice_bitcast_fusion.4), channel_id=1, source_target_pairs={{0,16},{8,24},{16,0},{24,8},{1,17},{9,25},{17,1},{25,9},{2,18},{10... | collective-permute-start | bytes 884744 | tf_op jit(solution)/shard_map/ppermute | solution.py:698
  453.2 16.3 %collective-permute-start.11 = (bf16[4,24,1536]{2,1,0:T(8,128)(2,1)S(1)}, bf16[4,24,1536]{2,1,0:T(8,128)(2,1)S(1)}, u32[]{:S(2)}, u32[]{:S(2)}) collective-permute-start(bf16[4,24,1536]{2,1,0:T(8,128)(2,1)S(1)} %slice_bitcast_fusion.6), channel_id=1, source_target_pairs={{0,8},{8,0},{16,24},{24,16},{1,9},{9,1},{17,25},{25,17},{2,10},{10... | collective-permute-start | bytes 884744 | tf_op jit(solution)/shard_map/ppermute | solution.py:698
  465.0 6.5 %collective-permute-start.19 = (bf16[24,1536]{1,0:T(8,128)(2,1)S(1)}, bf16[24,1536]{1,0:T(8,128)(2,1)S(1)}, u32[]{:S(2)}, u32[]{:S(2)}) collective-permute-start(bf16[24,1536]{1,0:T(8,128)(2,1)S(1)} %get-tuple-element.118), channel_id=1, source_target_pairs={{0,3},{1,2},{2,1},{3,0},{4,7},{5,6},{6,5},{7,4},{8,11},{9,10},{10,... | collective-permute-start | bytes 221192 | tf_op jit(solution)/shard_map/ppermute | solution.py:698
  466.9 10.0 %collective-permute-start.18 = (bf16[24,1536]{1,0:T(8,128)(2,1)S(1)}, bf16[24,1536]{1,0:T(8,128)(2,1)S(1)}, u32[]{:S(2)}, u32[]{:S(2)}) collective-permute-start(bf16[24,1536]{1,0:T(8,128)(2,1)S(1)} %get-tuple-element.119), channel_id=1, source_target_pairs={{0,2},{1,3},{2,0},{3,1},{4,6},{5,7},{6,4},{7,5},{8,10},{9,11},{10,... | collective-permute-start | bytes 221192 | tf_op jit(solution)/shard_map/ppermute | solution.py:698
  466.9 10.0 %collective-permute-start.17 = (bf16[24,1536]{1,0:T(8,128)(2,1)S(1)}, bf16[24,1536]{1,0:T(8,128)(2,1)S(1)}, u32[]{:S(2)}, u32[]{:S(2)}) collective-permute-start(bf16[24,1536]{1,0:T(8,128)(2,1)S(1)} %get-tuple-element.117), channel_id=1, source_target_pairs={{0,1},{1,0},{2,3},{3,2},{4,5},{5,4},{6,7},{7,6},{8,9},{9,8},{10,11... | collective-permute-start | bytes 221192 | tf_op jit(solution)/shard_map/ppermute | solution.py:698
  469.5 7.4 %collective-permute-start.14 = (bf16[24,1536]{1,0:T(8,128)(2,1)S(1)}, bf16[24,1536]{1,0:T(8,128)(2,1)S(1)}, u32[]{:S(2)}, u32[]{:S(2)}) collective-permute-start(bf16[24,1536]{1,0:T(8,128)(2,1)S(1)} %get-tuple-element.115), channel_id=1, source_target_pairs={{0,3},{1,2},{2,1},{3,0},{4,7},{5,6},{6,5},{7,4},{8,11},{9,10},{10,... | collective-permute-start | bytes 221192 | tf_op jit(solution)/shard_map/ppermute | solution.py:698
  471.5 7.0 %collective-permute-start.13 = (bf16[24,1536]{1,0:T(8,128)(2,1)S(1)}, bf16[24,1536]{1,0:T(8,128)(2,1)S(1)}, u32[]{:S(2)}, u32[]{:S(2)}) collective-permute-start(bf16[24,1536]{1,0:T(8,128)(2,1)S(1)} %get-tuple-element.116), channel_id=1, source_target_pairs={{0,2},{1,3},{2,0},{3,1},{4,6},{5,7},{6,4},{7,5},{8,10},{9,11},{10,... | collective-permute-start | bytes 221192 | tf_op jit(solution)/shard_map/ppermute | solution.py:698
  471.5 7.0 %collective-permute-start.12 = (bf16[24,1536]{1,0:T(8,128)(2,1)S(1)}, bf16[24,1536]{1,0:T(8,128)(2,1)S(1)}, u32[]{:S(2)}, u32[]{:S(2)}) collective-permute-start(bf16[24,1536]{1,0:T(8,128)(2,1)S(1)} %get-tuple-element.114), channel_id=1, source_target_pairs={{0,1},{1,0},{2,3},{3,2},{4,5},{5,4},{6,7},{7,6},{8,9},{9,8},{10,11... | collective-permute-start | bytes 221192 | tf_op jit(solution)/shard_map/ppermute | solution.py:698
  478.6 87.7 %copy-start.28 = (f32[24,768]{1,0:T(8,128)S(1)}, f32[24,768]{1,0:T(8,128)}, u32[]{:S(2)}) copy-start(f32[24,768]{1,0:T(8,128)} %param.29) | copy-start | bytes 221188
  478.6 87.7 %copy-start.39 = (f32[24,768]{1,0:T(8,128)S(1)}, f32[24,768]{1,0:T(8,128)}, u32[]{:S(2)}) copy-start(f32[24,768]{1,0:T(8,128)} %param.30) | copy-start | bytes 221188
  478.6 87.7 %copy-start.40 = (f32[24,768]{1,0:T(8,128)S(1)}, f32[24,768]{1,0:T(8,128)}, u32[]{:S(2)}) copy-start(f32[24,768]{1,0:T(8,128)} %param.31) | copy-start | bytes 221188
  478.6 89.0 %copy-start.35 = (f32[24,2304]{1,0:T(8,128)S(1)}, f32[24,2304]{1,0:T(8,128)}, u32[]{:S(2)}) copy-start(f32[24,2304]{1,0:T(8,128)} %param.27) | copy-start | bytes 663556
  478.6 89.0 %copy-start.36 = (f32[24,2304]{1,0:T(8,128)S(1)}, f32[24,2304]{1,0:T(8,128)}, u32[]{:S(2)}) copy-start(f32[24,2304]{1,0:T(8,128)} %param.28) | copy-start | bytes 663556
  561.8 30.5 %copy-start.19 = (f32[96,768]{1,0:T(8,128)S(1)}, f32[96,768]{1,0:T(8,128)}, u32[]{:S(2)}) copy-start(f32[96,768]{1,0:T(8,128)} %param.32) | copy-start | bytes 884740
  561.8 30.5 %copy-start.30 = (f32[96,768]{1,0:T(8,128)S(1)}, f32[96,768]{1,0:T(8,128)}, u32[]{:S(2)}) copy-start(f32[96,768]{1,0:T(8,128)} %param.33) | copy-start | bytes 884740
  561.9 30.5 %copy-start.31 = (f32[96,768]{1,0:T(8,128)S(1)}, f32[96,768]{1,0:T(8,128)}, u32[]{:S(2)}) copy-start(f32[96,768]{1,0:T(8,128)} %param.34) | copy-start | bytes 884740
  561.9 11.9 %collective-permute-start.23 = (bf16[2,96,768]{2,1,0:T(8,128)(2,1)S(1)}, bf16[2,96,768]{2,1,0:T(8,128)(2,1)S(1)}, u32[]{:S(2)}, u32[]{:S(2)}) collective-permute-start(bf16[2,96,768]{2,1,0:T(8,128)(2,1)S(1)} %get-tuple-element.109), channel_id=1, source_target_pairs={{0,3},{1,2},{2,1},{3,0},{4,7},{5,6},{6,5},{7,4},{8,11},{9,10},{10,... | collective-permute-start | bytes 884744 | tf_op jit(solution)/shard_map/ppermute | solution.py:698
  565.3 25.3 %collective-permute-start.22 = (bf16[2,96,768]{2,1,0:T(8,128)(2,1)S(1)}, bf16[2,96,768]{2,1,0:T(8,128)(2,1)S(1)}, u32[]{:S(2)}, u32[]{:S(2)}) collective-permute-start(bf16[2,96,768]{2,1,0:T(8,128)(2,1)S(1)} %get-tuple-element.108), channel_id=1, source_target_pairs={{0,2},{1,3},{2,0},{3,1},{4,6},{5,7},{6,4},{7,5},{8,10},{9,11},{10,... | collective-permute-start | bytes 884744 | tf_op jit(solution)/shard_map/ppermute | solution.py:698
  565.3 25.3 %collective-permute-start.21 = (bf16[2,96,768]{2,1,0:T(8,128)(2,1)S(1)}, bf16[2,96,768]{2,1,0:T(8,128)(2,1)S(1)}, u32[]{:S(2)}, u32[]{:S(2)}) collective-permute-start(bf16[2,96,768]{2,1,0:T(8,128)(2,1)S(1)} %get-tuple-element.107), channel_id=1, source_target_pairs={{0,1},{1,0},{2,3},{3,2},{4,5},{5,4},{6,7},{7,6},{8,9},{9,8},{10,11... | collective-permute-start | bytes 884744 | tf_op jit(solution)/shard_map/ppermute | solution.py:698
  567.6 69.2 %copy-start.29 = (f32[24,768]{1,0:T(8,128)}, f32[24,768]{1,0:T(8,128)S(1)}, u32[]{:S(2)}) copy-start(f32[24,768]{1,0:T(8,128)S(1)} %get-tuple-element.103) | copy-start | bytes 221188
  569.1 66.0 %copy-start.27 = (f32[24,2304]{1,0:T(8,128)}, f32[24,2304]{1,0:T(8,128)S(1)}, u32[]{:S(2)}) copy-start(f32[24,2304]{1,0:T(8,128)S(1)} %get-tuple-element.105) | copy-start | bytes 663556
  569.1 24.9 %copy-start.20 = (f32[768,96]{0,1:T(8,128)S(1)}, f32[768,96]{0,1:T(8,128)}, u32[]{:S(2)}) copy-start(f32[768,96]{0,1:T(8,128)} %param.35) | copy-start | bytes 884740
  569.1 24.9 %copy-start.32 = (f32[768,96]{0,1:T(8,128)S(1)}, f32[768,96]{0,1:T(8,128)}, u32[]{:S(2)}) copy-start(f32[768,96]{0,1:T(8,128)} %param.36) | copy-start | bytes 884740
  569.1 24.9 %copy-start.33 = (f32[768,96]{0,1:T(8,128)S(1)}, f32[768,96]{0,1:T(8,128)}, u32[]{:S(2)}) copy-start(f32[768,96]{0,1:T(8,128)} %param.37) | copy-start | bytes 884740
  592.4 25.2 %copy-start.5 = (bf16[1280,768]{1,0:T(8,128)(2,1)S(1)}, bf16[1280,768]{1,0:T(8,128)(2,1)}, u32[]{:S(2)}) copy-start(bf16[1280,768]{1,0:T(8,128)(2,1)} %copy-done.4) | copy-start | bytes 5898244
  592.4 25.2 %copy-start.10 = (s32[2,8,1280]{2,1,0:T(8,128)S(1)}, s32[2,8,1280]{2,1,0:T(8,128)}, u32[]{:S(2)}) copy-start(s32[2,8,1280]{2,1,0:T(8,128)} %copy-done.9) | copy-start | bytes 245764
  594.0 44.4 %copy-start.23 = (f32[96,768]{1,0:T(8,128)}, f32[96,768]{1,0:T(8,128)S(1)}, u32[]{:S(2)}) copy-start(f32[96,768]{1,0:T(8,128)S(1)} %get-tuple-element.101) | copy-start | bytes 884740
  601.6 1.2 collective-permute-start.24
  603.6 4.0 collective-permute-start.25
  608.3 4.0 collective-permute-start.26
  612.3 4.0 collective-permute-start.27
  616.3 9.9 %collective-permute-start.28 = (f32[67,128]{1,0:T(8,128)S(1)}, f32[67,128]{1,0:T(8,128)S(1)}, u32[]{:S(2)}, u32[]{:S(2)}) collective-permute-start(f32[67,128]{1,0:T(8,128)S(1)} %add.200), channel_id=1, source_target_pairs={{0,2},{1,3},{2,0},{3,1},{4,6},{5,7},{6,4},{7,5},{8,10},{9,11},{10,... | collective-permute-start | bytes 102920 | tf_op jit(solution)/shard_map/ppermute | solution.py:698
  619.7 14.3 %copy-start.8 = (f32[7,768]{1,0:T(8,128)S(1)}, f32[7,768]{1,0:T(8,128)}, u32[]{:S(2)}) copy-start(f32[7,768]{1,0:T(8,128)} %vec_ref.7) | copy-start | bytes 64516
  626.2 12.2 %copy-start.24 = (f32[96,768]{1,0:T(8,128)S(1)}, f32[96,768]{1,0:T(8,128)}, u32[]{:S(2)}) copy-start(f32[96,768]{1,0:T(8,128)} %get-tuple-element.102) | copy-start | bytes 884740
  626.2 13.1 %copy-start.25 = (f32[768,96]{0,1:T(8,128)S(1)}, f32[768,96]{0,1:T(8,128)}, u32[]{:S(2)}) copy-start(f32[768,96]{0,1:T(8,128)} %get-tuple-element.99) | copy-start | bytes 884740
  626.3 13.0 %copy-start.26 = (f32[768,96]{0,1:T(8,128)S(1)}, f32[768,96]{0,1:T(8,128)}, u32[]{:S(2)}) copy-start(f32[768,96]{0,1:T(8,128)} %get-tuple-element.100) | copy-start | bytes 884740
  627.4 12.8 %copy-start.41 = (f32[3072]{0:T(1024)S(1)}, f32[3072]{0:T(1024)}, u32[]{:S(2)}) copy-start(f32[3072]{0:T(1024)} %param.38) | copy-start | bytes 36868
  632.7 8.8 %copy-start.42 = (f32[3072]{0:T(1024)}, f32[3072]{0:T(1024)S(1)}, u32[]{:S(2)}) copy-start(f32[3072]{0:T(1024)S(1)} %get-tuple-element.97) | copy-start | bytes 36868
  632.7 8.8 %copy-start.43 = (f32[3072]{0:T(1024)}, f32[3072]{0:T(1024)S(1)}, u32[]{:S(2)}) copy-start(f32[3072]{0:T(1024)S(1)} %get-tuple-element.98) | copy-start | bytes 36868
  (18 other events, 56.5 us)
Sparse Core Ops, SparseCore 0:
  11.4 91.4 all-gather.2
  441.0 118.9 all-reduce.3

commit v2 on v1

--- a/solution.py
+++ b/solution.py
@@ -142,7 +142,7 @@
             jax.ShapeDtypeStruct((rows, 8, 128), jnp.int32),
         ],
         scratch_shapes=[pltpu.VMEM((CAP, D), f32), pltpu.VMEM((CAP, D), f32)],
-        compiler_params=params(48),
+        compiler_params=params(40),
         cost_estimate=cost(4 * count * SEQ * D, 4 * rows * SEQ * D * 2),
         name="pick_rows",
     )(sel[:, None, :], ids[:, None, :], tokens, cotangent, vectors)
@@ -167,7 +167,7 @@
 
 
 def attend_kernel(
-    a_ref, wq_ref, wk_ref, wv_ref, bounds_ref,
+    a_ref, wqk_ref, wv_ref, bounds_ref,
     q_ref, k_ref, v_ref, ctx_ref, lse_ref, bias_scr,
 ):
     group = pl.program_id(1)
@@ -178,8 +178,8 @@
         lse_ref[...] = jnp.zeros_like(lse_ref)
 
     a = a_ref[...]
-    q_ref[...] = dot_ab(a, wq_ref[...]).astype(bf16)
-    k_ref[...] = dot_ab(a, wk_ref[...]).astype(bf16)
+    q_ref[...] = dot_ab(a, wqk_ref[:, :GROUP]).astype(bf16)
+    k_ref[...] = dot_ab(a, wqk_ref[:, GROUP:]).astype(bf16)
     v_ref[...] = dot_ab(a, wv_ref[...]).astype(bf16)
     masks = half_masks()
     lane = lax.broadcasted_iota(jnp.int32, (1, 128), 1)
@@ -200,7 +200,7 @@
         ctx_ref[:, cols] = jnp.where(lane < HEAD_DIM, halves[0], halves[1]).astype(bf16)
 
 
-def attend_forward(a, weights, bounds):
+def attend_forward(a, w_qk, w_vo, bounds):
     count = a.shape[0]
     rows = count // CAP
     piece = pl.BlockSpec((CAP, GROUP), lambda r, g: (r, g))
@@ -210,9 +210,8 @@
         grid=(rows, GROUPS),
         in_specs=[
             pl.BlockSpec((CAP, D), lambda r, g: (r, 0)),
+            pl.BlockSpec((D, 2 * GROUP), lambda r, g: (0, g)),
             pl.BlockSpec((D, GROUP), lambda r, g: (0, g)),
-            pl.BlockSpec((D, GROUP), lambda r, g: (0, g + GROUPS)),
-            pl.BlockSpec((D, GROUP), lambda r, g: (0, g + 2 * GROUPS)),
             pl.BlockSpec((1, 8, 128), lambda r, g: (r, 0, 0)),
         ],
         out_specs=[piece, piece, piece, piece, pl.BlockSpec((CAP, 128), lambda r, g: (r, 0))],
@@ -224,14 +223,14 @@
             rows * HEADS * CAP * CAP,
         ),
         name="attend_forward",
-    )(a, weights, weights, weights, bounds)
+    )(a, w_qk, w_vo, bounds)
 
 
 def attend_back_kernel(
     me_ref, at_ref, q_ref, k_ref, v_ref, ctx_ref, dctx_ref, lse_ref, bounds_ref, gwo_ref,
-    dq_ref, dk_ref, dv_ref, keep_ref, send_ref, bias_scr, acc_scr, *, plan,
+    d_ref, keep_ref, send_ref, bias_scr, acc_scr, *, plan, start,
 ):
-    group, row = pl.program_id(0), pl.program_id(1)
+    group, row = pl.program_id(0) + start, pl.program_id(1)
     fill_bias(bias_scr, bounds_ref)
     masks = half_masks()
     lane = lax.broadcasted_iota(jnp.int32, (1, 128), 1)
@@ -256,13 +255,16 @@
             dq.append(dot_ab(score_grad, key_rows))
             dk_t.append(dot_ab(queries_t[span], score_grad))
             dv_t.append(dot_ab(grads_t[span], probs.astype(bf16)))
-        dq_ref[:, cols] = (jnp.where(lane < HEAD_DIM, dq[0], dq[1]) * SCORE_SCALE).astype(bf16)
-        dk_ref[:, cols] = (jnp.concatenate(dk_t, 0) * SCORE_SCALE).astype(bf16).T
-        dv_ref[:, cols] = jnp.concatenate(dv_t, 0).astype(bf16).T
+        place = pair * 128
+        d_ref[:, place : place + 128] = (jnp.where(lane < HEAD_DIM, dq[0], dq[1]) * SCORE_SCALE).astype(bf16)
+        place += GROUP
+        d_ref[:, place : place + 128] = (jnp.concatenate(dk_t, 0) * SCORE_SCALE).astype(bf16).T
+        place += GROUP
+        d_ref[:, place : place + 128] = jnp.concatenate(dv_t, 0).astype(bf16).T
     at = at_ref[...]
-    for part, ref in enumerate((dq_ref, dk_ref, dv_ref)):
+    for part in range(3):
         span = slice(part * GROUP, part * GROUP + GROUP)
-        product = dot_ab(at, ref[...])
+        product = dot_ab(at, d_ref[:, span])
 
         @pl.when(row == 0)
         def _():
@@ -299,11 +301,10 @@
         send_ref[slot] = jnp.where(on_high, low, high).astype(bf16)
 
 
-def attend_backward(me, at, q, k, v, ctx, dctx, lse, bounds, gwo, plan):
+def attend_backward(me, at, q, k, v, ctx, dctx, lse, bounds, gwo, plan, start, groups):
     count = q.shape[0]
     rows = count // CAP
-    piece = pl.BlockSpec((CAP, GROUP), lambda g, r, me: (r, g))
-    narrow = jax.ShapeDtypeStruct((count, D), bf16)
+    piece = pl.BlockSpec((CAP, GROUP), lambda g, r, me: (r, g + start))
     if plan is None:
         half, size, sent = 1, D, 8
     else:
@@ -311,33 +312,34 @@
         sent = size
     width = 4 * GROUP
     return pl.pallas_call(
-        partial(attend_back_kernel, plan=plan),
+        partial(attend_back_kernel, plan=plan, start=start),
         grid_spec=pltpu.PrefetchScalarGridSpec(
             num_scalar_prefetch=1,
-            grid=(GROUPS, rows),
+            grid=(groups, rows),
             in_specs=[
                 pl.BlockSpec((D, CAP), lambda g, r, me: (0, r)),
                 piece, piece, piece, piece, piece,
                 pl.BlockSpec((CAP, 128), lambda g, r, me: (r, 0)),
                 pl.BlockSpec((1, 8, 128), lambda g, r, me: (r, 0, 0)),
-                pl.BlockSpec((D, GROUP), lambda g, r, me: (0, g)),
+                pl.BlockSpec((D, GROUP), lambda g, r, me: (0, g + start)),
             ],
             out_specs=[
-                piece, piece, piece,
+                pl.BlockSpec((CAP, 3 * GROUP), lambda g, r, me: (r, g)),
                 pl.BlockSpec((half, size, width), lambda g, r, me: (0, 0, g)),
                 pl.BlockSpec((half, sent, width), lambda g, r, me: (0, 0, g)),
             ],
             scratch_shapes=[pltpu.VMEM((CAP, CAP), f32), pltpu.VMEM((D, width), f32)],
         ),
         out_shape=[
-            narrow, narrow, narrow,
-            jax.ShapeDtypeStruct((half, size, 4 * D), bf16),
-            jax.ShapeDtypeStruct((half, sent, 4 * D), bf16),
-        ],
-        compiler_params=params(56),
+            jax.ShapeDtypeStruct((count, groups * 3 * GROUP), bf16),
+            jax.ShapeDtypeStruct((half, size, groups * width), bf16),
+            jax.ShapeDtypeStruct((half, sent, groups * width), bf16),
+        ],
+        compiler_params=params(40),
         cost_estimate=cost(
-            2 * count * D * 3 * D + rows * HEADS * 40 * CAP * CAP * HEAD_DIM, 20 * count * D,
-            rows * HEADS * CAP * CAP,
+            groups * GROUP * (6 * count * D + 40 * count * CAP),
+            groups * GROUP * 20 * count,
+            groups * (GROUP // HEAD_DIM) * count * CAP,
         ),
         name="attend_backward",
     )(me, at, q, k, v, ctx, dctx, lse, bounds, gwo)
@@ -350,7 +352,7 @@
     c_ref[...] = (normalized * vec_ref[2:3, :] + vec_ref[3:4, :]).astype(bf16)
 
 
-def middle(ctx, weights, x, vectors):
+def middle(ctx, w_vo, x, vectors):
     count = ctx.shape[0]
     tile = 320
     wide = pl.BlockSpec((tile, D), lambda t: (t, 0))
@@ -358,7 +360,7 @@
         middle_kernel,
         grid=(count // tile,),
         in_specs=[
-            wide, pl.BlockSpec((D, D), lambda t: (0, 3)), wide,
+            wide, pl.BlockSpec((D, D), lambda t: (0, 1)), wide,
             pl.BlockSpec((7, D), lambda t: (0, 0)),
         ],
         out_specs=[wide, wide],
@@ -369,7 +371,7 @@
         compiler_params=params(32),
         cost_estimate=cost(2 * count * D * D, 10 * count * D),
         name="middle",
-    )(ctx, weights, x, vectors)
+    )(ctx, w_vo, x, vectors)
 
 
 ERF_P = 0.3275911 / math.sqrt(2.0)
@@ -414,14 +416,15 @@
     size = D // blocks
     for which, grad in enumerate((dot_ab(ct_scr[...], du), dot_ab(dmt_scr[...], act))):
         if not split:
-            keep_ref[0, 0, which] = grad.astype(bf16)
+            keep_ref[which, 0, 0] = grad.astype(bf16)
             continue
         on_high = (me_ref[2] & 1) != 0
         for block in range(0, blocks, 2):
             low = grad[block * size : (block + 1) * size]
             high = grad[(block + 1) * size : (block + 2) * size]
-            keep_ref[block // 2, 0, which] = jnp.where(on_high, high, low).astype(bf16)
-            send_ref[block // 2, 0, which] = jnp.where(on_high, low, high).astype(bf16)
+            slot = (me_ref[2] ^ block) >> 1
+            keep_ref[which, slot, 0] = jnp.where(on_high, high, low).astype(bf16)
+            send_ref[which, slot, 0] = jnp.where(on_high, low, high).astype(bf16)
     if not split:
         send_ref[...] = jnp.zeros_like(send_ref)
 
@@ -452,8 +455,8 @@
             ],
             out_specs=[
                 all_rows, all_rows,
-                pl.BlockSpec((half, 1, 2, rows_out, width), lambda j, s, me: (0, j, 0, 0, s)),
-                pl.BlockSpec((half, 1, 2, sent, width), lambda j, s, me: (0, j, 0, 0, s)),
+                pl.BlockSpec((2, half, 1, rows_out, width), lambda j, s, me: (0, 0, j, 0, s)),
+                pl.BlockSpec((2, half, 1, sent, width), lambda j, s, me: (0, 0, j, 0, s)),
                 pl.BlockSpec((1, 8, width), lambda j, s, me: ((me[1] ^ j) * subs + s, 0, 0)),
             ],
             scratch_shapes=[pltpu.VMEM((D, count), bf16), pltpu.VMEM((D, count), bf16)],
@@ -461,8 +464,8 @@
         out_shape=[
             jax.ShapeDtypeStruct((count, D), f32),
             jax.ShapeDtypeStruct((count, D), f32),
-            jax.ShapeDtypeStruct((half, mp, 2, rows_out, units), bf16),
-            jax.ShapeDtypeStruct((half, mp, 2, sent, units), bf16),
+            jax.ShapeDtypeStruct((2, half, mp, rows_out, units), bf16),
+            jax.ShapeDtypeStruct((2, half, mp, sent, units), bf16),
             jax.ShapeDtypeStruct((mp * subs, 8, width), f32),
         ],
         compiler_params=params(58),
@@ -515,7 +518,7 @@
     gwo_ref[...] += dot_ab(ctx_ref[...], datt, 0, 0)
 
 
-def turn(x, dy, att, mlp, dc, ctx, weights, vectors):
+def turn(x, dy, att, mlp, dc, ctx, w_vo, vectors):
     count = x.shape[0]
     tile = 320
     wide = pl.BlockSpec((tile, D), lambda t: (t, 0))
@@ -523,7 +526,7 @@
         turn_kernel,
         grid=(count // tile,),
         in_specs=[
-            wide, wide, wide, wide, wide, wide, pl.BlockSpec((D, D), lambda t: (0, 3)),
+            wide, wide, wide, wide, wide, wide, pl.BlockSpec((D, D), lambda t: (0, 1)),
             pl.BlockSpec((7, D), lambda t: (0, 0)),
         ],
         out_specs=[
@@ -541,20 +544,33 @@
         compiler_params=params(48),
         cost_estimate=cost(4 * count * D * D, 26 * count * D),
         name="turn",
-    )(x, dy, att, mlp, dc, ctx, weights, vectors)
-
-
-def finish_kernel(
-    dq_ref, dk_ref, dv_ref, wq_ref, wk_ref, wv_ref, x_ref, part_ref, vec_ref, rank_ref, cot_ref,
-    out_ref, gvec_ref, da_scr, hi_scr,
+    )(x, dy, att, mlp, dc, ctx, w_vo, vectors)
+
+
+def entry_kernel(
+    *refs, spans,
 ):
+    count = len(spans)
+    grads = refs[:count]
+    wqk_ref, wv_ref, x_ref, part_ref, vec_ref, out_ref, gvec_ref, da_scr = refs[count:]
+
     @pl.when(pl.program_id(0) == 0)
     def _():
         gvec_ref[...] = jnp.zeros_like(gvec_ref)
 
-    da = dot_ab(dq_ref[...], wq_ref[...], 1, 1)
-    da += dot_ab(dk_ref[...], wk_ref[...], 1, 1)
-    da_scr[...] = da + dot_ab(dv_ref[...], wv_ref[...], 1, 1)
+    da = None
+    for ref, (start, groups) in zip(grads, spans):
+        for at in range(groups):
+            group, left = start + at, at * 3 * GROUP
+            term = dot_ab(
+                ref[:, left : left + 2 * GROUP],
+                wqk_ref[:, group * 2 * GROUP : (group + 1) * 2 * GROUP], 1, 1,
+            ) + dot_ab(
+                ref[:, left + 2 * GROUP : left + 3 * GROUP],
+                wv_ref[:, group * GROUP : (group + 1) * GROUP], 1, 1,
+            )
+            da = term if da is None else da + term
+    da_scr[...] = da
     tile = 64
 
     def body(i, carry):
@@ -565,48 +581,65 @@
             gvec_ref[place : place + 1, :] += jnp.sum(term, 0, keepdims=True)
         grad = part_ref[rows, :] + norm_back(da, normalized, inverse, vec_ref[0:1, :])
         high = grad.astype(bf16)
-        hi_scr[rows, 0:D] = high
-        hi_scr[rows, D : 2 * D] = (grad - high.astype(f32)).astype(bf16)
-        hi_scr[rows, 2 * D :] = jnp.ones((tile, 128), bf16)
+        out_ref[rows, 0:D] = high
+        out_ref[rows, D:] = (grad - high.astype(f32)).astype(bf16)
         return carry
 
-    lax.fori_loop(0, CAP // tile, body, 0)
-    hot = one_hot(rank_ref[0, 0:1, :])
-    placed = dot_ab(hot, hi_scr[...], 0, 0)
+    lax.fori_loop(0, x_ref.shape[0] // tile, body, 0)
+
+
+def entry(grads, spans, w_qk, w_vo, x, part, vectors):
+    count = x.shape[0]
+    tile = 320
+    wide = pl.BlockSpec((tile, D), lambda r: (r, 0))
+    return pl.pallas_call(
+        partial(entry_kernel, spans=spans),
+        grid=(count // tile,),
+        in_specs=[pl.BlockSpec((tile, g.shape[1]), lambda r: (r, 0)) for g in grads]
+        + [
+            pl.BlockSpec((D, 2 * D), lambda r: (0, 0)), pl.BlockSpec((D, D), lambda r: (0, 0)),
+            wide, wide, pl.BlockSpec((7, D), lambda r: (0, 0)),
+        ],
+        out_specs=[
+            pl.BlockSpec((tile, 2 * D), lambda r: (r, 0)),
+            pl.BlockSpec((8, D), lambda r: (0, 0)),
+        ],
+        out_shape=[
+            jax.ShapeDtypeStruct((count, 2 * D), bf16),
+            jax.ShapeDtypeStruct((8, D), f32),
+        ],
+        scratch_shapes=[pltpu.VMEM((tile, D), f32)],
+        compiler_params=params(32),
+        cost_estimate=cost(2 * count * D * 3 * D, 24 * count * D),
+        name="entry",
+    )(*grads, w_qk, w_vo, x, part, vectors)
+
+
+def finish_kernel(grad_ref, rank_ref, cot_ref, out_ref, ext_scr):
+    ext_scr[:, 0 : 2 * D] = grad_ref[...]
+    ext_scr[:, 2 * D :] = jnp.ones((CAP, 128), bf16)
+    placed = dot_ab(one_hot(rank_ref[0, 0:1, :]), ext_scr[...], 0, 0)
     kept = 1.0 - placed[:, 2 * D : 2 * D + 1]
     out_ref[0] = placed[:, 0:D] + placed[:, D : 2 * D] + kept * cot_ref[0].astype(f32)
 
 
-def finish(dq, dk, dv, weights, x, part, vectors, rank, cotangent):
-    count = x.shape[0]
-    rows = count // CAP
-    wide = pl.BlockSpec((CAP, D), lambda r: (r, 0))
-
-    def weight_spec(which):
-        return pl.BlockSpec((D, D), lambda r, which=which: (0, which))
-
+def finish(grad, rank, cotangent):
+    rows = cotangent.shape[0]
     return pl.pallas_call(
         finish_kernel,
         grid=(rows,),
         in_specs=[
-            wide, wide, wide, weight_spec(0), weight_spec(1), weight_spec(2), wide, wide,
-            pl.BlockSpec((7, D), lambda r: (0, 0)),
+            pl.BlockSpec((CAP, 2 * D), lambda r: (r, 0)),
             pl.BlockSpec((1, 8, SEQ), lambda r: (r, 0, 0)),
             pl.BlockSpec((1, SEQ, D), lambda r: (r, 0, 0)),
         ],
-        out_specs=[
-            pl.BlockSpec((1, SEQ, D), lambda r: (r, 0, 0)),
-            pl.BlockSpec((8, D), lambda r: (0, 0)),
-        ],
-        out_shape=[
-            jax.ShapeDtypeStruct((rows, SEQ, D), f32),
-            jax.ShapeDtypeStruct((8, D), f32),
-        ],
-        scratch_shapes=[pltpu.VMEM((CAP, D), f32), pltpu.VMEM((CAP, 2 * D + 128), bf16)],
-        compiler_params=params(60),
-        cost_estimate=cost(2 * count * D * 3 * D + 6 * count * SEQ * D, 24 * count * D),
+        out_specs=pl.BlockSpec((1, SEQ, D), lambda r: (r, 0, 0)),
+        out_shape=jax.ShapeDtypeStruct((rows, SEQ, D), f32),
+        scratch_shapes=[pltpu.VMEM((CAP, 2 * D + 128), bf16)],
+        compiler_params=params(48),
+        cost_estimate=cost(4 * rows * CAP * SEQ * D, 18 * rows * CAP * D),
         name="finish",
-    )(dq, dk, dv, weights, weights, weights, x, part, vectors, rank, cotangent)
+    )(grad, rank, cotangent)
 
 
 def place_kernel(y_ref, rank_ref, tok_ref, out_ref, ext_scr):
@@ -634,52 +667,6 @@
         cost_estimate=cost(2 * rows * CAP * SEQ * D, 10 * rows * CAP * D),
         name="place",
     )(y, rank, tokens)
-
-
-def order_kernel(me_ref, *refs, plan):
-    blocks, core_bit, mp, bit_orders = plan
-    *sources, out_ref, sem = refs
-    size = D // blocks
-    me = me_ref[0]
-    copies = []
-    for half, bits in enumerate(bit_orders):
-        for side in range(2):
-            source = sources[half * 2 + side]
-            for slot in range(blocks // 2):
-                place, rest = slot % mp, slot // mp
-                for bit in bits:
-                    place |= mp * bit * (rest & 1)
-                    rest >>= 1
-                place |= core_bit * side
-                start = pl.multiple_of((me ^ place) * size, 8)
-                copies.append(
-                    pltpu.make_async_copy(
-                        source.at[slot],
-                        out_ref.at[pl.ds(start, size), pl.ds(half * 2 * D, 2 * D)],
-                        sem,
-                    )
-                )
-    for copy in copies:
-        copy.start()
-    for copy in copies:
-        copy.wait()
-
-
-def in_order(me, pieces, plan):
-    anywhere = pl.BlockSpec(memory_space=pl.ANY)
-    return pl.pallas_call(
-        partial(order_kernel, plan=plan),
-        grid_spec=pltpu.PrefetchScalarGridSpec(
-            num_scalar_prefetch=1,
-            grid=(1,),
-            in_specs=[anywhere] * len(pieces),
-            out_specs=anywhere,
-            scratch_shapes=[pltpu.SemaphoreType.DMA],
-        ),
-        out_shape=jax.ShapeDtypeStruct((D, 4 * D), bf16),
-        cost_estimate=cost(0, 16 * D * D),
-        name="in_order",
-    )(me, *pieces)
 
 
 def lamb_moments(weight, gradient, first_mom, second_mom, decay):
@@ -725,75 +712,138 @@
     while bit < dp:
         bits.append(bit)
         bit *= 2
-    bit_orders = (tuple(bits), tuple(reversed(bits)))
-
-    attn_low = jnp.concatenate([qkv_weight, proj_weight], 1).astype(bf16)
+    ups, downs = tuple(bits), tuple(reversed(bits))
+
+    def tie(*values):
+        return lax.optimization_barrier(values)
+
+    def total(terms):
+        result = terms[0].astype(f32)
+        for term in terms[1:]:
+            result = result + term.astype(f32)
+        return result
+
+    def merge(held, came, high, axis):
+        return jnp.where(high, jnp.stack([came, held], axis), jnp.stack([held, came], axis))
+
+    narrow = qkv_weight.astype(bf16)
+    size = D // world
+    low_qk = narrow[:, : 2 * D].reshape(size, 2, GROUPS, GROUP).transpose(0, 2, 1, 3)
+    low_qk = low_qk.reshape(size, 2 * D)
+    low_vo = jnp.concatenate([narrow[:, 2 * D :], proj_weight.astype(bf16)], 1)
     mlp_low = jnp.stack([up_weight.astype(bf16), down_weight.astype(bf16).T])
+    picked = pick_rows(selected, image_ids, tokens, cotangent, vectors)
     if fast:
-        rel = [attn_low[None]] + [swap_mp(attn_low[None], k) for k in range(1, mp)]
-        rel = jnp.concatenate(rel, 0)
-        pieces = []
-        for half, order in enumerate(bit_orders):
-            held = rel[:, :, half * 2 * D : (half + 1) * 2 * D]
-            for bit in order:
-                held = jnp.concatenate([held, swap_dp(held, bit)], 0)
-            pieces += [held, swap_dp(held, 1)]
-        attn_mat = in_order(me, pieces, (world, mp, mp, bit_orders))
+        low_both = jnp.concatenate([low_qk, low_vo], 1)
+        held = [low_both] + [swap_mp(low_both, k) for k in range(1, mp)]
+        held, picked = tie(held, picked)
+        held = jnp.stack(held).reshape((2,) * (mp.bit_length() - 1) + (size, 4 * D))
+        for axis in range(mp.bit_length() - 1):
+            flip = ((mp_at >> (mp.bit_length() - 2 - axis)) & 1) != 0
+            held = jnp.where(flip, jnp.flip(held, axis), held)
+        held = held.reshape(mp, size, 4 * D)
+        halves = []
+        for half, order in enumerate((ups, downs)):
+            value = held[:, :, half * 2 * D : (half + 1) * 2 * D]
+            done = []
+            for bit in order + (1,):
+                axis = sum(other > bit for other in done)
+                done.append(bit)
+                value = merge(value, swap_dp(value, bit), (dp_at & bit) != 0, axis)
+            halves.append(value.reshape(D, 2 * D))
+        w_qk, w_vo = halves
     else:
-        attn_mat = lax.all_gather(attn_low, everyone, axis=0, tiled=True)
+        w_qk = lax.all_gather(low_qk, everyone, axis=0, tiled=True)
+        w_vo = lax.all_gather(low_vo, everyone, axis=0, tiled=True)
     mlp_mat = lax.all_gather(mlp_low[None], everyone, axis=0, tiled=True)
     mlp_mat = mlp_mat.reshape(dp, mp, 2, D // dp, FF // mp)
     if not fast:
         mlp_mat = mlp_mat.transpose(1, 2, 0, 3, 4).reshape(1, mp, 2, D, FF // mp)
 
-    x, dy, a, at, dm, rank, bounds = pick_rows(selected, image_ids, tokens, cotangent, vectors)
-    q, k, v, ctx, lse = attend_forward(a, attn_mat, bounds)
-    att, c = middle(ctx, attn_mat, x, vectors)
+    def stage(terms, left, bit):
+        axis = left.index(bit)
+        give = total([lax.index_in_dim(t, 1, axis, False) for t in terms]).astype(bf16)
+        terms = [lax.index_in_dim(t, 0, axis, False) for t in terms]
+        return terms + [swap_dp(give, bit)], [b for b in left if b != bit]
+
+    def as_bits(value):
+        return value.reshape((2,) * len(bits) + (mp,) + value.shape[-2:])
+
+    x, dy, a, at, dm, rank, bounds = picked
+    q, k, v, ctx, lse = attend_forward(a, w_qk, w_vo, bounds)
+    att, c = middle(ctx, w_vo, x, vectors)
     mlp, dc, mlp_keep, mlp_send, bias_rows = mlp_all(me, c, dm, mlp_mat, up_bias, fast)
-    y, part, dctx, gwo, gvec_two = turn(x, dy, att, mlp, dc, ctx, attn_mat, vectors)
     plan = (world, mp) if fast else None
-    dq, dk, dv, attn_keep, attn_send = attend_backward(
-        me, at, q, k, v, ctx, dctx, lse, bounds, gwo, plan
-    )
-    input_grad, gvec_one = finish(dq, dk, dv, attn_mat, x, part, vectors, rank, cotangent)
-    block_output = place(y, rank, tokens)
-
-    def add(kept, came):
-        return (kept.astype(f32) + came.astype(f32)).astype(bf16)
-
+    spans = ((0, GROUPS - 1), (GROUPS - 1, 1))
+    back = partial(attend_backward, me, at, q, k, v, ctx)
     if fast:
-        both = add(mlp_keep, swap_dp(mlp_send, 1))
-        mine = lax.psum_scatter(both, "dq", scatter_dimension=0, tiled=True)[0]
-        mlp_sum = mine[0].astype(f32)
+        mlp_came = swap_dp(mlp_send, 1)
+    y, part, dctx, gwo, gvec_two = turn(x, dy, att, mlp, dc, ctx, w_vo, vectors)
+    if fast:
+        mlp_came, dctx = tie(mlp_came, dctx)
+        chains = []
+        for which, order in enumerate((ups, downs)):
+            terms = [as_bits(mlp_keep[which]), as_bits(mlp_came[which])]
+            chains.append([terms, list(reversed(bits)), list(order)])
+
+        def step(chains):
+            for chain in chains:
+                chain[0], chain[1] = stage(chain[0], chain[1], chain[2].pop(0))
+
+        step(chains)
+        d_one, keep_one, send_one = back(dctx, lse, bounds, gwo, plan, *spans[0])
+        (chains[0][0][-1], chains[1][0][-1]), d_one, send_one, dctx = tie(
+            (chains[0][0][-1], chains[1][0][-1]), d_one, send_one, dctx
+        )
+        while chains[0][2]:
+            step(chains)
+        came_one = swap_dp(send_one, 1)
+        d_two, keep_two, send_two = back(dctx, lse, bounds, gwo, plan, *spans[1])
+        (chains[0][0][-1], chains[1][0][-1]), came_one, send_two, d_two, y = tie(
+            (chains[0][0][-1], chains[1][0][-1]), came_one, send_two, d_two, y
+        )
+        mlp_sent = []
         for k_at in range(1, mp):
-            mlp_sum = mlp_sum + swap_mp(mine[k_at], k_at).astype(f32)
-        both = add(attn_keep, swap_dp(attn_send, 1))
-        parts = []
-        for half, order in enumerate(bit_orders):
-            held = both[:, :, half * 2 * D : (half + 1) * 2 * D]
-            held = held.reshape((2,) * len(bits) + (mp, D // world, 2 * D))
-            left = list(reversed(bits))
-            for bit in reversed(order):
-                axis = left.index(bit)
-                left.remove(bit)
-                low = lax.index_in_dim(held, 0, axis, False)
-                high = lax.index_in_dim(held, 1, axis, False)
-                held = add(low, swap_dp(high, bit))
-            total = held[0].astype(f32)
-            for k_at in range(1, mp):
-                total = total + swap_mp(held[k_at], k_at).astype(f32)
-            parts.append(total)
-        attn_sum = jnp.concatenate(parts, 1)
+            give = jnp.stack([total([t[k_at] for t in chain[0]]) for chain in chains])
+            mlp_sent.append(swap_mp(give.astype(bf16), k_at))
+        mlp_mine = jnp.stack([total([t[0] for t in chain[0]]) for chain in chains])
+        one = [[as_bits(keep_one), as_bits(came_one)], list(reversed(bits)), list(ups)]
+        came_two = swap_dp(send_two, 1)
+        step([one])
+        block_output = place(y, rank, tokens)
+        came_two, block_output, d_one = tie(came_two, block_output, d_one)
+        two = [[as_bits(keep_two), as_bits(came_two)], list(reversed(bits)), list(downs)]
+        step([two])
+        grad, gvec_one = entry((d_one, d_two), spans, w_qk, w_vo, x, part, vectors)
+        one[0][-1], two[0][-1], grad, gvec_one = tie(one[0][-1], two[0][-1], grad, gvec_one)
+        while one[2]:
+            step([one, two])
+        input_grad = finish(grad, rank, cotangent)
+        one[0][-1], two[0][-1], input_grad, mlp_sent = tie(
+            one[0][-1], two[0][-1], input_grad, mlp_sent
+        )
+        attn_sent = []
+        for k_at in range(1, mp):
+            give = [total([t[k_at] for t in chain[0]]).astype(bf16) for chain in (one, two)]
+            attn_sent.append(swap_mp(jnp.concatenate(give, 1), k_at))
+        mlp_sum = mlp_mine + total(mlp_sent)
+        attn_sum = jnp.concatenate(
+            [total([t[0] for t in chain[0]]) for chain in (one, two)], 1
+        ) + total(attn_sent)
     else:
-        shaped = mlp_keep[0].reshape(mp, 2, dp, D // dp, FF // mp)
-        shaped = jnp.take(shaped, mp_at ^ jnp.arange(mp), axis=0)
-        shaped = shaped.transpose(2, 0, 1, 3, 4).reshape(world, 2, D // dp, FF // mp)
+        d_all, attn_keep, _ = back(dctx, lse, bounds, gwo, plan, 0, GROUPS)
+        block_output = place(y, rank, tokens)
+        grad, gvec_one = entry((d_all,), ((0, GROUPS),), w_qk, w_vo, x, part, vectors)
+        input_grad = finish(grad, rank, cotangent)
+        shaped = mlp_keep[:, 0].reshape(2, mp, dp, D // dp, FF // mp)
+        shaped = jnp.take(shaped, mp_at ^ jnp.arange(mp), axis=1)
+        shaped = shaped.transpose(2, 1, 0, 3, 4).reshape(world, 2, D // dp, FF // mp)
         mlp_sum = lax.psum_scatter(shaped, everyone, scatter_dimension=0, tiled=True)[0]
         mlp_sum = mlp_sum.astype(f32)
         attn_sum = lax.psum_scatter(attn_keep[0], everyone, scatter_dimension=0, tiled=True)
         attn_sum = attn_sum.astype(f32)
-    attn_sum = attn_sum.reshape(D // world, GROUPS, 4, GROUP).transpose(0, 2, 1, 3)
-    attn_sum = attn_sum.reshape(D // world, 4 * D)
+    attn_sum = attn_sum.reshape(size, GROUPS, 4, GROUP).transpose(0, 2, 1, 3)
+    attn_sum = attn_sum.reshape(size, 4 * D)
     qkv_sum, proj_sum = attn_sum[:, : 3 * D], attn_sum[:, 3 * D :]
     up_sum, down_sum = mlp_sum[0], mlp_sum[1].T
 

time: 656 us -> 409 us (0.62)
  waiting for transfers between devices: 177 us -> 40.6 us
  Pallas kernels: 353 us -> 217 us
  local copies, waits for them, and re-layouts: 31.5 us -> 53 us
    pallas_call x3 -> x4, Pallas kernels: 220 us -> 70.5 us  [the longest x2 47 us: attend_backward(): pl.pallas_call(partial(attend_back_kernel, plan=plan, start=start), grid_...]
    unnamed x3 -> x1, waiting for transfers between devices: 80.9 us -> 0.02 us
    ppermute x29 -> x31, waiting for transfers between devices: 96.4 us -> 40.5 us  [swap(): return lax.ppermute(value, axis, [(i, i ^ bit) for i in range(size)])]
    unnamed x103 -> x176, local copies, waits for them, and re-layouts: 16.8 us -> 34.2 us
    pallas_call x1, Pallas kernels: 62.9 us -> 76.8 us  [mlp_all(): pl.pallas_call(partial(mlp_kernel, blocks=blocks, split=split), grid_spec...]
    convert_element_type x6 -> x12, other arithmetic: 8.94 us -> 14 us  [the longest x8 11.3 us: stage(): total([lax.index_in_dim(t, 1, axis, False) for t in terms]).astype(bf16)]
    ppermute x29 -> x31, starting transfers between devices: 34.4 us -> 37.2 us  [swap(): return lax.ppermute(value, axis, [(i, i ^ bit) for i in range(size)])]
  transfers between devices with their start and end apart: 31 -> 32, of which waited for: 18 -> 12; matrix products, arithmetic and copies ran while one was open for 3% -> 6% of each run, Pallas kernels for 45% -> 34%
where the time goes in v2:
time: 409 us; the launch traced here: 406 us
  Pallas kernels  217 us (53%)
  local copies, waits for them, and re-layouts  53 us (13%)
  waiting for transfers between devices  40.6 us (10%)
  other arithmetic  39 us (10%)
  starting transfers between devices  37.3 us (9%)
  between operations  19.2 us (5%)
    pallas_call x1, Pallas kernels, mlp_all(): pl.pallas_call(partial(mlp_kernel, blocks=blocks, split=split), grid_spec...  76.8 us
    pallas_call x2, Pallas kernels, attend_backward(): pl.pallas_call(partial(attend_back_kernel, plan=plan, start=start), grid_...  47 us
    ppermute x31, waiting for transfers between devices, swap(): return lax.ppermute(value, axis, [(i, i ^ bit) for i in range(size)])  40.5 us
    ppermute x31, starting transfers between devices, swap(): return lax.ppermute(value, axis, [(i, i ^ bit) for i in range(size)])  37.2 us
    unnamed x176, local copies, waits for them, and re-layouts  34.2 us
    pallas_call x1, Pallas kernels, attend_forward(): pl.pallas_call(attend_kernel, grid=(rows, GROUPS), in_specs=[pl.BlockSpec...  29.8 us
    pallas_call x1, Pallas kernels, turn(): pl.pallas_call(turn_kernel, grid=(count // tile,), in_specs=[wide, wide,...  18.2 us
    pallas_call x1, Pallas kernels, entry(): pl.pallas_call(partial(entry_kernel, spans=spans), grid=(count // tile,),...  11.9 us
  transfers between devices with their start and end apart: 32, of which 12 were waited for; matrix products, arithmetic and copies ran while one was open for 6% of the time, Pallas kernels for 34%

profile of v2, /device:TPU:0, one launch (start us, length us, event | category | flops | bytes accessed | tf_op | source)
XLA Modules:
  0.0 405.6 jit_solution(14319408386325859641)
XLA Ops:
  10.4 5.1 %collective-permute-start.2 = (bf16[24,3072]{1,0:T(8,128)(2,1)S(1)}, bf16[24,3072]{1,0:T(8,128)(2,1)S(1)}, u32[]{:S(2)}, u32[]{:S(2)}) collective-permute-start(bf16[24,3072]{1,0:T(8,128)(2,1)S(1)} %pad_maximum_fusion.5), channel_id=1, source_target_pairs={{0,3},{1,2},{2,1},{3,0},{4,7},{5,6},{6,5},{7,4},{8,11},{9,10},{10,... | collective-permute-start | bytes 442376 | tf_op jit(solution)/shard_map/ppermute | solution.py:685
  16.2 2.1 copy-done.8
  18.3 11.5 %pick_rows.1 = (bf16[1280,768]{1,0:T(8,128)(2,1)S(1)}, bf16[1280,768]{1,0:T(8,128)(2,1)S(1)}, bf16[1280,768]{1,0:T(8,128)(2,1)S(1)}, bf16[768,1280]{1,0:T(8,128)...) custom-call(s32[2,1,1280]{2,1,0:T(1,128)S(1)} %broadcast_in_dim.11.sel_ref, ...), custom_call_target="tpu_custom_call" | custom-call | flops 5033164800 | bytes 15728640 | tf_op jit(solution)/shard_map/pick_rows/pallas_call | solution.py:126
  31.2 1.3 copy-done.14
  34.4 1.4 copy-done.32
  37.5 1.7 collective-permute-start.3
  39.2 1.5 collective-permute-start.6
  41.3 9.1 %collective-permute-done.3 = bf16[4,24,1536]{2,1,0:T(8,128)(2,1)S(1)} collective-permute-done((bf16[4,24,1536]{2,1,0:T(8,128)(2,1)S(1)}, bf16[4,24,1536]{2,1,0:T(8,128)(2,1)S(1)}, u32[]{:S(2)}, u32[]{:S(2)}) %collective-permute-start.3) | collective-permute-done | bytes 294944 | tf_op jit(solution)/shard_map/ppermute | solution.py:685
  51.7 1.3 collective-permute-done.6
  54.5 9.3 %collective-permute-done.4 = bf16[2,4,24,1536]{3,2,1,0:T(8,128)(2,1)S(1)} collective-permute-done((bf16[2,4,24,1536]{3,2,1,0:T(8,128)(2,1)S(1)}, bf16[2,4,24,1536]{3,2,1,0:T(8,128)(2,1)S(1)}, u32[]{:S(2)}, u32[]{:S(2)}) %collective-permute-start.4) | collective-permute-done | bytes 589856 | tf_op jit(solution)/shard_map/ppermute | solution.py:685
  64.1 2.7 collective-permute-done.7
  68.1 1.6 copy.63
  70.0 1.7 maximum_select_fusion.1
  71.8 29.8 %attend_forward.1 = (bf16[1280,768]{1,0:T(8,128)(2,1)S(1)}, bf16[1280,768]{1,0:T(8,128)(2,1)S(1)}, bf16[1280,768]{1,0:T(8,128)(2,1)}, bf16[1280,768]{1,0:T(8,128)(2,1)}, f32[1280,128]{1,0:T(8,128)S(1)}) custom-call(bf16[1280,768]{1,0:T(8,128)(2,1)} %copy-done.33, bf16[768,1536]{1,0:T(8,128)(2,1)} %bitcast.241, bf16[768,1536]{1,0:T(8,128)(2,1)} %bitcast.237, ...), custom_call_target="tpu_custom_call" | custom-call | flops 14596177920 | bytes 11796480 | tf_op jit(solution)/shard_map/attend_forward/pallas_call | solution.py:208
  102.9 1.3 copy-done.37
  105.0 1.5 copy-done.5
  106.6 3.4 middle.1
  110.0 1.9 copy-done.10
  111.9 1.3 copy-done.25
  113.2 76.8 %mlp_all.1 = (f32[1280,768]{1,0:T(8,128)}, f32[1280,768]{1,0:T(8,128)}, bf16[2,4,4,96,768]{4,3,2,1,0:T(8,128)(2,1)}, bf16[2,4,4,96,768]{4,3,2,1,0:T(8,128)(2,1)}, f32[8,8,384]{2,1,0:T(8,128)}) custom-call(s32[3]{0:T(128)} %pad_add_fusion.me_ref, bf16[1280,768]{1,0:T(8,128)(2,1)} %copy-done.25, bf16[1280,768]{1,0:T(8,128)(2,1)} %copy-done.32, ...), custom_call_target="tpu_custom_call" | custom-call | flops 36238786560 | bytes 30670848 | tf_op jit(solution)/shard_map/mlp_all/pallas_call | solution.py:447
  190.2 2.0 slice.489
  192.5 18.2 %turn.1 = (bf16[1280,768]{1,0:T(8,128)(2,1)S(1)}, f32[1280,768]{1,0:T(8,128)}, bf16[1280,768]{1,0:T(8,128)(2,1)S(1)}, f32[768,768]{1,0:T(8,128)}, f32[8,768]{1,0:T(8,128)S(1)}) custom-call(bf16[1280,768]{1,0:T(8,128)(2,1)S(1)} %copy-done.4, bf16[1280,768]{1,0:T(8,128)(2,1)} %copy-done.14, f32[1280,768]{1,0:T(8,128)} %copy-done.10, ...), custom_call_target="tpu_custom_call" | custom-call | flops 3019898880 | bytes 25559040 | tf_op jit(solution)/shard_map/turn/pallas_call | solution.py:525
  212.0 2.2 copy-done.47
  214.2 1.7 fusion.1
  216.0 2.0 slice.491
  218.0 1.6 collective-permute-start.11
  219.9 1.6 collective-permute-start.10
  221.5 30.9 %attend_backward.2 = (bf16[1280,1536]{1,0:T(8,128)(2,1)}, bf16[16,24,2048]{2,1,0:T(8,128)(2,1)S(1)}, bf16[16,24,2048]{2,1,0:T(8,128)(2,1)}) custom-call(s32[3]{0:T(128)S(1)} %copy-done.22, bf16[768,1280]{1,0:T(8,128)(2,1)S(1)} %copy-done.30, bf16[1280,768]{1,0:T(8,128)(2,1)S(1)} %copy-done.35, bf16[1280,768]{1,0:T(8,128)(2,1)S(1)} %copy-done.38, ...), custom_call_target="tpu_custom_call" | custom-call | flops 19797114880 | bytes 13107200 | tf_op jit(solution)/shard_map/attend_backward/pallas_call | solution.py:314
  253.5 1.5 slice.537
  255.0 1.3 reshape.1039
  256.3 1.8 fusion.2
  258.1 1.3 collective-permute-start.13
  259.5 1.6 fusion.3
  261.1 1.5 collective-permute-start.12
  262.6 1.5 copy-done.36
  264.1 1.5 copy-done.39
  265.7 1.5 copy-done.41
  267.2 16.0 %attend_backward.3 = (bf16[1280,768]{1,0:T(8,128)(2,1)S(1)}, bf16[16,24,1024]{2,1,0:T(8,128)(2,1)S(1)}, bf16[16,24,1024]{2,1,0:T(8,128)(2,1)S(1)}) custom-call(s32[3]{0:T(128)S(1)} %copy-done.22, bf16[768,1280]{1,0:T(8,128)(2,1)S(1)} %copy-done.31, bf16[1280,768]{1,0:T(8,128)(2,1)S(1)} %copy-done.36, bf16[1280,768]{1,0:T(8,128)(2,1)S(1)} %copy-done.39, ...), custom_call_target="tpu_custom_call" | custom-call | flops 9898557440 | bytes 6553600 | tf_op jit(solution)/shard_map/attend_backward/pallas_call | solution.py:314
  284.6 2.8 fusion.10
  287.4 2.5 fusion.11
  290.6 1.4 collective-permute-start.20
  292.7 2.6 collective-permute-start.21
  296.5 2.3 fusion.4
  299.3 6.4 %place.1 = bf16[2,1280,768]{2,1,0:T(8,128)(2,1)} custom-call(bf16[1280,768]{1,0:T(8,128)(2,1)S(1)} %copy-done.13, s32[2,8,1280]{2,1,0:T(8,128)S(1)} %copy-done.20, bf16[2,1280,768]{2,1,0:T(8,128)(2,1)S(1)} %copy-done.9), custom_call_target="tpu_custom_call" | custom-call | flops 2516582400 | bytes 9830400 | tf_op jit(solution)/shard_map/place/pallas_call | solution.py:655
  307.8 2.1 copy-done.23
  309.9 2.1 copy-done.26
  312.0 1.5 copy-done.28
  313.6 11.9 %entry.1 = (bf16[1280,1536]{1,0:T(8,128)(2,1)S(1)}, f32[8,768]{1,0:T(8,128)S(1)}) custom-call(bf16[1280,1536]{1,0:T(8,128)(2,1)S(1)} %copy-done.26, bf16[1280,768]{1,0:T(8,128)(2,1)S(1)} %copy-done.28, bf16[768,1536]{1,0:T(8,128)(2,1)S(1)} %bitcast.242, bf16[768,1536]{1,0:T(8,128)(2,1)S(1)} %bitcast.240, bf16[1280,768]{1,0:T(8,128)(2,1)S(1)} %copy-done.4, ...), custom_call_target="tpu_custom_call" | custom-call | flops 4529848320 | bytes 23592960 | tf_op jit(solution)/shard_map/entry/pallas_call | solution.py:595
  326.7 1.3 collective-permute-start.19
  329.3 1.5 collective-permute-start.18
  330.7 11.6 %finish.1 = f32[2,1280,768]{2,1,0:T(8,128)} custom-call(bf16[1280,1536]{1,0:T(8,128)(2,1)S(1)} %get-tuple-element.147.grad_ref, s32[2,8,1280]{2,1,0:T(8,128)S(1)} %copy-done.20, bf16[2,1280,768]{2,1,0:T(8,128)(2,1)} %cot_ref.3), custom_call_target="tpu_custom_call" | custom-call | flops 5033164800 | bytes 17694720 | tf_op jit(solution)/shard_map/finish/pallas_call | solution.py:628
  343.6 1.5 fusion.27
  345.2 1.4 collective-permute-start.24
  346.7 2.2 collective-permute-start.25
  349.5 1.4 maximum_add_fusion
  352.8 5.5 %collective-permute-done.24 = bf16[24,3072]{1,0:T(8,128)(2,1)S(1)} collective-permute-done((bf16[24,3072]{1,0:T(8,128)(2,1)S(1)}, bf16[24,3072]{1,0:T(8,128)(2,1)S(1)}, u32[]{:S(2)}, u32[]{:S(2)}) %collective-permute-start.24) | collective-permute-done | bytes 147488 | tf_op jit(solution)/shard_map/ppermute | solution.py:685
  361.1 5.4 %stack.254 = f32[8]{0:T(128)S(1)} concatenate(f32[1]{0:T(128)} %bitcast.63, f32[1]{0:T(128)} %bitcast.64, f32[1]{0:T(128)} %bitcast.65, f32[1]{0:T(128)} %bitcast.66, f32[1]{0:T(128)} %bitcast.92, f32[1]{0:T(128)} %bitcast.93, f32[1]{0:T(128)} %bitcast.99, f32[1]{0:T(128)} %bitcast.103), dimensions={0} | concatenate | bytes 64 | tf_op jit(solution)/shard_map/stack | solution.py:862
  368.4 3.4 collective-permute-done.27
  372.6 3.3 collective-permute-done.28
  375.9 2.2 collective-permute-start.29
  378.1 1.9 collective-permute-done.29
  380.1 3.0 collective-permute-start.30
  383.1 1.9 collective-permute-done.30
  385.0 2.1 slice.582
  (275 shorter events, 44.6 us)
Async XLA Ops:
  7.2 9.0 %copy-start.86 = (s32[2,1280]{1,0:T(2,128)S(1)}, s32[2,1280]{1,0:T(2,128)}, u32[]{:S(2)}) copy-start(s32[2,1280]{1,0:T(2,128)} %param.23) | copy-start | bytes 30724
  7.2 9.0 %copy-start.87 = (s32[2,1280]{1,0:T(2,128)S(1)}, s32[2,1280]{1,0:T(2,128)}, u32[]{:S(2)}) copy-start(s32[2,1280]{1,0:T(2,128)} %param.24) | copy-start | bytes 30724
  7.2 9.0 %copy-start.16 = (f32[7,768]{1,0:T(8,128)S(1)}, f32[7,768]{1,0:T(8,128)}, u32[]{:S(2)}) copy-start(f32[7,768]{1,0:T(8,128)} %refs_6_.1) | copy-start | bytes 64516
  7.2 105.9 %all-gather.3.cloned.1.call-start = ((), (), s32[]{:S(2)}) async-start(), calls=%async_computation | async-start | bytes 9732096 | tf_op jit(solution)/shard_map/all_gather | solution.py:758
  10.4 26.6 %collective-permute-start.2 = (bf16[24,3072]{1,0:T(8,128)(2,1)S(1)}, bf16[24,3072]{1,0:T(8,128)(2,1)S(1)}, u32[]{:S(2)}, u32[]{:S(2)}) collective-permute-start(bf16[24,3072]{1,0:T(8,128)(2,1)S(1)} %pad_maximum_fusion.5), channel_id=1, source_target_pairs={{0,3},{1,2},{2,1},{3,0},{4,7},{5,6},{6,5},{7,4},{8,11},{9,10},{10,... | collective-permute-start | bytes 442376 | tf_op jit(solution)/shard_map/ppermute | solution.py:685
  15.5 21.5 %collective-permute-start.1 = (bf16[24,3072]{1,0:T(8,128)(2,1)S(1)}, bf16[24,3072]{1,0:T(8,128)(2,1)S(1)}, u32[]{:S(2)}, u32[]{:S(2)}) collective-permute-start(bf16[24,3072]{1,0:T(8,128)(2,1)S(1)} %pad_maximum_fusion.5), channel_id=1, source_target_pairs={{0,2},{1,3},{2,0},{3,1},{4,6},{5,7},{6,4},{7,5},{8,10},{9,11},{10,... | collective-permute-start | bytes 442376 | tf_op jit(solution)/shard_map/ppermute | solution.py:685
  15.5 21.5 %collective-permute-start = (bf16[24,3072]{1,0:T(8,128)(2,1)S(1)}, bf16[24,3072]{1,0:T(8,128)(2,1)S(1)}, u32[]{:S(2)}, u32[]{:S(2)}) collective-permute-start(bf16[24,3072]{1,0:T(8,128)(2,1)S(1)} %pad_maximum_fusion.5), channel_id=1, source_target_pairs={{0,1},{1,0},{2,3},{3,2},{4,5},{5,4},{6,7},{7,6},{8,9},{9,8},{10,11... | collective-permute-start | bytes 442376 | tf_op jit(solution)/shard_map/ppermute | solution.py:685
  37.5 12.9 %collective-permute-start.3 = (bf16[4,24,1536]{2,1,0:T(8,128)(2,1)S(1)}, bf16[4,24,1536]{2,1,0:T(8,128)(2,1)S(1)}, u32[]{:S(2)}, u32[]{:S(2)}) collective-permute-start(bf16[4,24,1536]{2,1,0:T(8,128)(2,1)S(1)} %get-tuple-element.204), channel_id=1, source_target_pairs={{0,8},{8,0},{16,24},{24,16},{1,9},{9,1},{17,25},{25,17},{2,10},{10... | collective-permute-start | bytes 884744 | tf_op jit(solution)/shard_map/ppermute | solution.py:685
  39.2 13.8 %collective-permute-start.6 = (bf16[4,24,1536]{2,1,0:T(8,128)(2,1)S(1)}, bf16[4,24,1536]{2,1,0:T(8,128)(2,1)S(1)}, u32[]{:S(2)}, u32[]{:S(2)}) collective-permute-start(bf16[4,24,1536]{2,1,0:T(8,128)(2,1)S(1)} %get-tuple-element.203), channel_id=1, source_target_pairs={{0,16},{8,24},{16,0},{24,8},{1,17},{9,25},{17,1},{25,9},{2,18},{10... | collective-permute-start | bytes 884744 | tf_op jit(solution)/shard_map/ppermute | solution.py:685
  50.5 13.3 %collective-permute-start.4 = (bf16[2,4,24,1536]{3,2,1,0:T(8,128)(2,1)S(1)}, bf16[2,4,24,1536]{3,2,1,0:T(8,128)(2,1)S(1)}, u32[]{:S(2)}, u32[]{:S(2)}) collective-permute-start(bf16[2,4,24,1536]{3,2,1,0:T(8,128)(2,1)S(1)} %maximum_select_fusion.6), channel_id=1, source_target_pairs={{0,16},{8,24},{16,0},{24,8},{1,17},{9,25},{17,1},{25,9},{2,18},{10... | collective-permute-start | bytes 1769480 | tf_op jit(solution)/shard_map/ppermute | solution.py:685
  53.1 13.7 %collective-permute-start.7 = (bf16[2,4,24,1536]{3,2,1,0:T(8,128)(2,1)S(1)}, bf16[2,4,24,1536]{3,2,1,0:T(8,128)(2,1)S(1)}, u32[]{:S(2)}, u32[]{:S(2)}) collective-permute-start(bf16[2,4,24,1536]{3,2,1,0:T(8,128)(2,1)S(1)} %maximum_select_fusion.8), channel_id=1, source_target_pairs={{0,8},{8,0},{16,24},{24,16},{1,9},{9,1},{17,25},{25,17},{2,10},{10... | collective-permute-start | bytes 1769480 | tf_op jit(solution)/shard_map/ppermute | solution.py:685
  64.0 3.7 collective-permute-start.5
  67.0 2.9 collective-permute-start.8
  71.8 33.3 %copy-start = (bf16[2,2,2,4,24,1536]{5,4,3,2,1,0:T(8,128)(2,1)S(1)}, bf16[2,2,2,4,24,1536]{5,4,3,2,1,0:T(8,128)(2,1)}, u32[]{:S(2)}) copy-start(bf16[2,2,2,4,24,1536]{5,4,3,2,1,0:T(8,128)(2,1)} %maximum_select_fusion.1) | copy-start | bytes 7077892
  71.8 33.3 %copy-start.3 = (bf16[1280,768]{1,0:T(8,128)(2,1)S(1)}, bf16[1280,768]{1,0:T(8,128)(2,1)}, u32[]{:S(2)}) copy-start(bf16[1280,768]{1,0:T(8,128)(2,1)} %copy-done.2) | copy-start | bytes 5898244
  190.0 22.0 %collective-permute-start.9 = (bf16[2,4,4,96,768]{4,3,2,1,0:T(8,128)(2,1)}, bf16[2,4,4,96,768]{4,3,2,1,0:T(8,128)(2,1)S(1)}, u32[]{:S(2)}, u32[]{:S(2)}) collective-permute-start(bf16[2,4,4,96,768]{4,3,2,1,0:T(8,128)(2,1)} %get-tuple-element.108), channel_id=1, source_target_pairs={{0,4},{4,0},{1,5},{5,1},{2,6},{6,2},{3,7},{7,3},{8,12},{12,8},{9,1... | collective-permute-start | bytes 14155784 | tf_op jit(solution)/shard_map/ppermute | solution.py:685
  192.2 27.4 %copy-start.45 = (bf16[1,4,4,96,768]{4,3,2,1,0:T(8,128)(2,1)}, bf16[1,4,4,96,768]{4,3,2,1,0:T(8,128)(2,1)S(1)}, u32[]{:S(2)}) copy-start(bf16[1,4,4,96,768]{4,3,2,1,0:T(8,128)(2,1)S(1)} %slice.489) | copy-start | bytes 7077892
  212.0 7.6 %copy-start.21 = (f32[8,768]{1,0:T(8,128)}, f32[8,768]{1,0:T(8,128)S(1)}, u32[]{:S(2)}) copy-start(f32[8,768]{1,0:T(8,128)S(1)} %get-tuple-element.152) | copy-start | bytes 73732
  218.0 34.5 %copy-start.46 = (bf16[1,4,4,96,768]{4,3,2,1,0:T(8,128)(2,1)}, bf16[1,4,4,96,768]{4,3,2,1,0:T(8,128)(2,1)S(1)}, u32[]{:S(2)}) copy-start(bf16[1,4,4,96,768]{4,3,2,1,0:T(8,128)(2,1)S(1)} %slice.491) | copy-start | bytes 7077892
  218.0 34.5 %collective-permute-start.11 = (bf16[2,4,96,768]{3,2,1,0:T(8,128)(2,1)S(1)}, bf16[2,4,96,768]{3,2,1,0:T(8,128)(2,1)}, u32[]{:S(2)}, u32[]{:S(2)}) collective-permute-start(bf16[2,4,96,768]{3,2,1,0:T(8,128)(2,1)S(1)} %fusion.1), channel_id=1, source_target_pairs={{0,16},{8,24},{16,0},{24,8},{1,17},{9,25},{17,1},{25,9},{2,18},{10... | collective-permute-start | bytes 3538952 | tf_op jit(solution)/shard_map/ppermute | solution.py:685
  219.9 32.6 %collective-permute-start.10 = (bf16[2,4,96,768]{3,2,1,0:T(8,128)(2,1)S(1)}, bf16[2,4,96,768]{3,2,1,0:T(8,128)(2,1)S(1)}, u32[]{:S(2)}, u32[]{:S(2)}) collective-permute-start(bf16[2,4,96,768]{3,2,1,0:T(8,128)(2,1)S(1)} %fusion), channel_id=1, source_target_pairs={{0,8},{8,0},{16,24},{24,16},{1,9},{9,1},{17,25},{25,17},{2,10},{10... | collective-permute-start | bytes 3538952 | tf_op jit(solution)/shard_map/ppermute | solution.py:685
  253.5 31.1 %collective-permute-start.14 = (bf16[16,24,2048]{2,1,0:T(8,128)(2,1)}, bf16[16,24,2048]{2,1,0:T(8,128)(2,1)}, u32[]{:S(2)}, u32[]{:S(2)}) collective-permute-start(bf16[16,24,2048]{2,1,0:T(8,128)(2,1)} %get-tuple-element.126), channel_id=1, source_target_pairs={{0,4},{4,0},{1,5},{5,1},{2,6},{6,2},{3,7},{7,3},{8,12},{12,8},{9,1... | collective-permute-start | bytes 4718600 | tf_op jit(solution)/shard_map/ppermute | solution.py:685
  258.1 26.4 %collective-permute-start.13 = (bf16[4,96,768]{2,1,0:T(8,128)(2,1)S(1)}, bf16[4,96,768]{2,1,0:T(8,128)(2,1)S(1)}, u32[]{:S(2)}, u32[]{:S(2)}) collective-permute-start(bf16[4,96,768]{2,1,0:T(8,128)(2,1)S(1)} %fusion.2), channel_id=1, source_target_pairs={{0,8},{8,0},{16,24},{24,16},{1,9},{9,1},{17,25},{25,17},{2,10},{10... | collective-permute-start | bytes 1769480 | tf_op jit(solution)/shard_map/ppermute | solution.py:685
  261.1 23.5 %collective-permute-start.12 = (bf16[4,96,768]{2,1,0:T(8,128)(2,1)S(1)}, bf16[4,96,768]{2,1,0:T(8,128)(2,1)S(1)}, u32[]{:S(2)}, u32[]{:S(2)}) collective-permute-start(bf16[4,96,768]{2,1,0:T(8,128)(2,1)S(1)} %fusion.3), channel_id=1, source_target_pairs={{0,16},{8,24},{16,0},{24,8},{1,17},{9,25},{17,1},{25,9},{2,18},{10... | collective-permute-start | bytes 1769480 | tf_op jit(solution)/shard_map/ppermute | solution.py:685
  284.5 41.0 %copy-start.15 = (bf16[16,24,1024]{2,1,0:T(8,128)(2,1)}, bf16[16,24,1024]{2,1,0:T(8,128)(2,1)S(1)}, u32[]{:S(2)}) copy-start(bf16[16,24,1024]{2,1,0:T(8,128)(2,1)S(1)} %get-tuple-element.138) | copy-start | bytes 2359300
  287.4 11.9 %copy-start.13 = (bf16[1280,768]{1,0:T(8,128)(2,1)S(1)}, bf16[1280,768]{1,0:T(8,128)(2,1)}, u32[]{:S(2)}) copy-start(bf16[1280,768]{1,0:T(8,128)(2,1)} %copy-done.12) | copy-start | bytes 5898244
  289.9 9.4 %copy-start.9 = (bf16[2,1280,768]{2,1,0:T(8,128)(2,1)S(1)}, bf16[2,1280,768]{2,1,0:T(8,128)(2,1)}, u32[]{:S(2)}) copy-start(bf16[2,1280,768]{2,1,0:T(8,128)(2,1)} %tok_ref.3) | copy-start | bytes 11796484
  290.6 51.8 %collective-permute-start.20 = (bf16[2,96,768]{2,1,0:T(8,128)(2,1)}, bf16[2,96,768]{2,1,0:T(8,128)(2,1)}, u32[]{:S(2)}, u32[]{:S(2)}) collective-permute-start(bf16[2,96,768]{2,1,0:T(8,128)(2,1)} %pad_maximum_fusion.2), channel_id=1, source_target_pairs={{0,1},{1,0},{2,3},{3,2},{4,5},{5,4},{6,7},{7,6},{8,9},{9,8},{10,11... | collective-permute-start | bytes 884744 | tf_op jit(solution)/shard_map/ppermute | solution.py:685
  292.7 49.7 %collective-permute-start.21 = (bf16[2,96,768]{2,1,0:T(8,128)(2,1)}, bf16[2,96,768]{2,1,0:T(8,128)(2,1)}, u32[]{:S(2)}, u32[]{:S(2)}) collective-permute-start(bf16[2,96,768]{2,1,0:T(8,128)(2,1)} %pad_maximum_fusion.3), channel_id=1, source_target_pairs={{0,2},{1,3},{2,0},{3,1},{4,6},{5,7},{6,4},{7,5},{8,10},{9,11},{10,... | collective-permute-start | bytes 884744 | tf_op jit(solution)/shard_map/ppermute | solution.py:685
  295.4 10.3 %collective-permute-start.15 = (bf16[16,24,1024]{2,1,0:T(8,128)(2,1)S(1)}, bf16[16,24,1024]{2,1,0:T(8,128)(2,1)}, u32[]{:S(2)}, u32[]{:S(2)}) collective-permute-start(bf16[16,24,1024]{2,1,0:T(8,128)(2,1)S(1)} %get-tuple-element.131), channel_id=1, source_target_pairs={{0,4},{4,0},{1,5},{5,1},{2,6},{6,2},{3,7},{7,3},{8,12},{12,8},{9,1... | collective-permute-start | bytes 2359304 | tf_op jit(solution)/shard_map/ppermute | solution.py:685
  296.1 46.3 %collective-permute-start.22 = (bf16[2,96,768]{2,1,0:T(8,128)(2,1)}, bf16[2,96,768]{2,1,0:T(8,128)(2,1)}, u32[]{:S(2)}, u32[]{:S(2)}) collective-permute-start(bf16[2,96,768]{2,1,0:T(8,128)(2,1)} %pad_maximum_fusion.4), channel_id=1, source_target_pairs={{0,3},{1,2},{2,1},{3,0},{4,7},{5,6},{6,5},{7,4},{8,11},{9,10},{10,... | collective-permute-start | bytes 884744 | tf_op jit(solution)/shard_map/ppermute | solution.py:685
  298.8 9.0 %copy-start.1 = (bf16[2,2,2,4,24,1536]{5,4,3,2,1,0:T(8,128)(2,1)S(1)}, bf16[2,2,2,4,24,1536]{5,4,3,2,1,0:T(8,128)(2,1)}, u32[]{:S(2)}) copy-start(bf16[2,2,2,4,24,1536]{5,4,3,2,1,0:T(8,128)(2,1)} %maximum_select_fusion.1) | copy-start | bytes 7077892
  298.8 9.0 %copy-start.11 = (bf16[2,2,2,4,24,1536]{5,4,3,2,1,0:T(8,128)(2,1)S(1)}, bf16[2,2,2,4,24,1536]{5,4,3,2,1,0:T(8,128)(2,1)}, u32[]{:S(2)}) copy-start(bf16[2,2,2,4,24,1536]{5,4,3,2,1,0:T(8,128)(2,1)} %copy.63) | copy-start | bytes 7077892
  298.8 9.0 %copy-start.17 = (f32[7,768]{1,0:T(8,128)S(1)}, f32[7,768]{1,0:T(8,128)}, u32[]{:S(2)}) copy-start(f32[7,768]{1,0:T(8,128)} %refs_6_.1) | copy-start | bytes 64516
  298.8 26.7 %collective-permute-start.16 = (bf16[2,4,24,2048]{3,2,1,0:T(8,128)(2,1)}, bf16[2,4,24,2048]{3,2,1,0:T(8,128)(2,1)}, u32[]{:S(2)}, u32[]{:S(2)}) collective-permute-start(bf16[2,4,24,2048]{3,2,1,0:T(8,128)(2,1)} %fusion.4), channel_id=1, source_target_pairs={{0,8},{8,0},{16,24},{24,16},{1,9},{9,1},{17,25},{25,17},{2,10},{10... | collective-permute-start | bytes 2359304 | tf_op jit(solution)/shard_map/ppermute | solution.py:685
  306.9 18.6 %collective-permute-start.17 = (bf16[2,4,24,1024]{3,2,1,0:T(8,128)(2,1)S(1)}, bf16[2,4,24,1024]{3,2,1,0:T(8,128)(2,1)S(1)}, u32[]{:S(2)}, u32[]{:S(2)}) collective-permute-start(bf16[2,4,24,1024]{3,2,1,0:T(8,128)(2,1)S(1)} %bitcast.269), channel_id=1, source_target_pairs={{0,16},{8,24},{16,0},{24,8},{1,17},{9,25},{17,1},{25,9},{2,18},{10... | collective-permute-start | bytes 1179656 | tf_op jit(solution)/shard_map/ppermute | solution.py:685
  325.5 16.9 %copy-start.64 = (bf16[2,4,24,1024]{3,2,1,0:T(8,128)(2,1)}, bf16[2,4,24,1024]{3,2,1,0:T(8,128)(2,1)S(1)}, u32[]{:S(2)}) copy-start(bf16[2,4,24,1024]{3,2,1,0:T(8,128)(2,1)S(1)} %collective-permute-done.17) | copy-start | bytes 1179652
  326.7 15.7 %collective-permute-start.19 = (bf16[4,24,1024]{2,1,0:T(8,128)(2,1)S(1)}, bf16[4,24,1024]{2,1,0:T(8,128)(2,1)S(1)}, u32[]{:S(2)}, u32[]{:S(2)}) collective-permute-start(bf16[4,24,1024]{2,1,0:T(8,128)(2,1)S(1)} %fusion.7), channel_id=1, source_target_pairs={{0,8},{8,0},{16,24},{24,16},{1,9},{9,1},{17,25},{25,17},{2,10},{10... | collective-permute-start | bytes 589832 | tf_op jit(solution)/shard_map/ppermute | solution.py:685
  329.3 13.2 %collective-permute-start.18 = (bf16[4,24,2048]{2,1,0:T(8,128)(2,1)S(1)}, bf16[4,24,2048]{2,1,0:T(8,128)(2,1)S(1)}, u32[]{:S(2)}, u32[]{:S(2)}) collective-permute-start(bf16[4,24,2048]{2,1,0:T(8,128)(2,1)S(1)} %fusion.5), channel_id=1, source_target_pairs={{0,16},{8,24},{16,0},{24,8},{1,17},{9,25},{17,1},{25,9},{2,18},{10... | collective-permute-start | bytes 1179656 | tf_op jit(solution)/shard_map/ppermute | solution.py:685
  345.2 13.1 %collective-permute-start.24 = (bf16[24,3072]{1,0:T(8,128)(2,1)S(1)}, bf16[24,3072]{1,0:T(8,128)(2,1)S(1)}, u32[]{:S(2)}, u32[]{:S(2)}) collective-permute-start(bf16[24,3072]{1,0:T(8,128)(2,1)S(1)} %pad_maximum_fusion.7), channel_id=1, source_target_pairs={{0,2},{1,3},{2,0},{3,1},{4,6},{5,7},{6,4},{7,5},{8,10},{9,11},{10,... | collective-permute-start | bytes 442376 | tf_op jit(solution)/shard_map/ppermute | solution.py:685
  346.7 11.7 %collective-permute-start.25 = (bf16[24,3072]{1,0:T(8,128)(2,1)S(1)}, bf16[24,3072]{1,0:T(8,128)(2,1)S(1)}, u32[]{:S(2)}, u32[]{:S(2)}) collective-permute-start(bf16[24,3072]{1,0:T(8,128)(2,1)S(1)} %pad_maximum_fusion.8), channel_id=1, source_target_pairs={{0,3},{1,2},{2,1},{3,0},{4,7},{5,6},{6,5},{7,4},{8,11},{9,10},{10,... | collective-permute-start | bytes 442376 | tf_op jit(solution)/shard_map/ppermute | solution.py:685
  348.8 10.0 %collective-permute-start.23 = (bf16[24,3072]{1,0:T(8,128)(2,1)S(1)}, bf16[24,3072]{1,0:T(8,128)(2,1)S(1)}, u32[]{:S(2)}, u32[]{:S(2)}) collective-permute-start(bf16[24,3072]{1,0:T(8,128)(2,1)S(1)} %pad_maximum_fusion.6), channel_id=1, source_target_pairs={{0,1},{1,0},{2,3},{3,2},{4,5},{5,4},{6,7},{7,6},{8,9},{9,8},{10,11... | collective-permute-start | bytes 442376 | tf_op jit(solution)/shard_map/ppermute | solution.py:685
  351.8 44.9 %copy-start.56 = (f32[768,96]{0,1:T(8,128)}, f32[768,96]{0,1:T(8,128)S(1)}, u32[]{:S(2)}) copy-start(f32[768,96]{0,1:T(8,128)S(1)} %get-tuple-element.175) | copy-start | bytes 884740
  351.8 44.9 %copy-start.57 = (f32[768,96]{0,1:T(8,128)}, f32[768,96]{0,1:T(8,128)S(1)}, u32[]{:S(2)}) copy-start(f32[768,96]{0,1:T(8,128)S(1)} %get-tuple-element.176) | copy-start | bytes 884740
  352.8 44.9 %copy-start.58 = (f32[96,768]{1,0:T(8,128)}, f32[96,768]{1,0:T(8,128)S(1)}, u32[]{:S(2)}) copy-start(f32[96,768]{1,0:T(8,128)S(1)} %get-tuple-element.177) | copy-start | bytes 884740
  352.8 44.9 %copy-start.59 = (f32[96,768]{1,0:T(8,128)}, f32[96,768]{1,0:T(8,128)S(1)}, u32[]{:S(2)}) copy-start(f32[96,768]{1,0:T(8,128)S(1)} %get-tuple-element.178) | copy-start | bytes 884740
  359.1 7.4 %copy-start.71 = (f32[3840]{0:T(1024)S(1)}, f32[3840]{0:T(1024)}, u32[]{:S(2)}) copy-start(f32[3840]{0:T(1024)} %reshape.1039) | copy-start | bytes 46084
  360.2 35.1 %copy-start.65 = (f32[24,768]{1,0:T(8,128)}, f32[24,768]{1,0:T(8,128)S(1)}, u32[]{:S(2)}) copy-start(f32[24,768]{1,0:T(8,128)S(1)} %get-tuple-element.179) | copy-start | bytes 221188
  360.2 35.1 %copy-start.66 = (f32[24,768]{1,0:T(8,128)}, f32[24,768]{1,0:T(8,128)S(1)}, u32[]{:S(2)}) copy-start(f32[24,768]{1,0:T(8,128)S(1)} %get-tuple-element.180) | copy-start | bytes 221188
  360.2 30.3 %copy-start.79 = (f32[3072]{0:T(1024)S(1)}, f32[3072]{0:T(1024)}, u32[]{:S(2)}) copy-start(f32[3072]{0:T(1024)} %param.38) | copy-start | bytes 36868
  360.2 33.6 %copy-start.18 = (f32[7,768]{1,0:T(8,128)S(1)}, f32[7,768]{1,0:T(8,128)}, u32[]{:S(2)}) copy-start(f32[7,768]{1,0:T(8,128)} %refs_6_.1) | copy-start | bytes 64516
  361.1 35.7 %copy-start.60 = (f32[24,2304]{1,0:T(8,128)}, f32[24,2304]{1,0:T(8,128)S(1)}, u32[]{:S(2)}) copy-start(f32[24,2304]{1,0:T(8,128)S(1)} %get-tuple-element.181) | copy-start | bytes 663556
  361.1 35.7 %copy-start.61 = (f32[24,2304]{1,0:T(8,128)}, f32[24,2304]{1,0:T(8,128)S(1)}, u32[]{:S(2)}) copy-start(f32[24,2304]{1,0:T(8,128)S(1)} %get-tuple-element.182) | copy-start | bytes 663556
  361.1 29.4 %copy-start.84 = (f32[3072]{0:T(1024)S(1)}, f32[3072]{0:T(1024)}, u32[]{:S(2)}) copy-start(f32[3072]{0:T(1024)} %param.39) | copy-start | bytes 36868
  361.1 29.4 %copy-start.85 = (f32[3072]{0:T(1024)S(1)}, f32[3072]{0:T(1024)}, u32[]{:S(2)}) copy-start(f32[3072]{0:T(1024)} %param.40) | copy-start | bytes 36868
  361.1 32.7 %copy-start.82 = (f32[7,768]{1,0:T(8,128)S(1)}, f32[7,768]{1,0:T(8,128)}, u32[]{:S(2)}) copy-start(f32[7,768]{1,0:T(8,128)} %param.42) | copy-start | bytes 64516
  361.1 32.7 %copy-start.83 = (f32[7,768]{1,0:T(8,128)S(1)}, f32[7,768]{1,0:T(8,128)}, u32[]{:S(2)}) copy-start(f32[7,768]{1,0:T(8,128)} %param.43) | copy-start | bytes 64516
  366.5 1.3 collective-permute-start.26
  367.8 4.0 collective-permute-start.27
  371.9 4.0 collective-permute-start.28
  375.9 4.1 %collective-permute-start.29 = (f32[67,128]{1,0:T(8,128)S(1)}, f32[67,128]{1,0:T(8,128)S(1)}, u32[]{:S(2)}, u32[]{:S(2)}) collective-permute-start(f32[67,128]{1,0:T(8,128)S(1)} %add.601), channel_id=1, source_target_pairs={{0,1},{1,0},{2,3},{3,2},{4,5},{5,4},{6,7},{7,6},{8,9},{9,8},{10,11... | collective-permute-start | bytes 102920 | tf_op jit(solution)/shard_map/ppermute | solution.py:685
  380.1 5.0 %collective-permute-start.30 = (f32[67,128]{1,0:T(8,128)S(1)}, f32[67,128]{1,0:T(8,128)S(1)}, u32[]{:S(2)}, u32[]{:S(2)}) collective-permute-start(f32[67,128]{1,0:T(8,128)S(1)} %add.602), channel_id=1, source_target_pairs={{0,2},{1,3},{2,0},{3,1},{4,6},{5,7},{6,4},{7,5},{8,10},{9,11},{10,... | collective-permute-start | bytes 102920 | tf_op jit(solution)/shard_map/ppermute | solution.py:685
  391.1 7.5 %copy-start.80 = (f32[3072]{0:T(1024)}, f32[3072]{0:T(1024)S(1)}, u32[]{:S(2)}) copy-start(f32[3072]{0:T(1024)S(1)} %get-tuple-element.173) | copy-start | bytes 36868
  391.1 7.5 %copy-start.81 = (f32[3072]{0:T(1024)}, f32[3072]{0:T(1024)S(1)}, u32[]{:S(2)}) copy-start(f32[3072]{0:T(1024)S(1)} %get-tuple-element.174) | copy-start | bytes 36868
  (56 other events, 178.0 us)
Sparse Core Ops, SparseCore 0:
  11.5 91.1 all-gather.2

commit v3 on v2

--- a/solution.py
+++ b/solution.py
@@ -41,6 +41,17 @@
 
 def params(mib, **more):
     return pltpu.CompilerParams(vmem_limit_bytes=mib << 20, **more)
+
+
+def hbm(shape, dtype):
+    return pltpu.HBM(shape, dtype)
+
+
+def pinned(*arrays):
+    return [
+        pltpu.with_memory_space_constraint(array, pltpu.HBM) if array.size >= 1 << 17 else array
+        for array in arrays
+    ]
 
 
 def cost(flops, nbytes, trans=0):
@@ -133,19 +144,19 @@
             pl.BlockSpec((1, 8, 128), lambda r: (r, 0, 0)),
         ],
         out_shape=[
-            jax.ShapeDtypeStruct((count, D), bf16),
-            jax.ShapeDtypeStruct((count, D), bf16),
-            jax.ShapeDtypeStruct((count, D), bf16),
-            jax.ShapeDtypeStruct((D, count), bf16),
-            jax.ShapeDtypeStruct((count, D), bf16),
-            jax.ShapeDtypeStruct((rows, 8, SEQ), jnp.int32),
-            jax.ShapeDtypeStruct((rows, 8, 128), jnp.int32),
+            hbm((count, D), bf16),
+            hbm((count, D), bf16),
+            hbm((count, D), bf16),
+            hbm((D, count), bf16),
+            hbm((count, D), bf16),
+            hbm((rows, 8, SEQ), jnp.int32),
+            hbm((rows, 8, 128), jnp.int32),
         ],
         scratch_shapes=[pltpu.VMEM((CAP, D), f32), pltpu.VMEM((CAP, D), f32)],
         compiler_params=params(40),
         cost_estimate=cost(4 * count * SEQ * D, 4 * rows * SEQ * D * 2),
         name="pick_rows",
-    )(sel[:, None, :], ids[:, None, :], tokens, cotangent, vectors)
+    )(*pinned(sel[:, None, :], ids[:, None, :], tokens, cotangent, vectors))
 
 
 def fill_bias(bias_scr, bounds_ref):
@@ -167,7 +178,7 @@
 
 
 def attend_kernel(
-    a_ref, wqk_ref, wv_ref, bounds_ref,
+    a_ref, w_ref, bounds_ref,
     q_ref, k_ref, v_ref, ctx_ref, lse_ref, bias_scr,
 ):
     group = pl.program_id(1)
@@ -178,9 +189,8 @@
         lse_ref[...] = jnp.zeros_like(lse_ref)
 
     a = a_ref[...]
-    q_ref[...] = dot_ab(a, wqk_ref[:, :GROUP]).astype(bf16)
-    k_ref[...] = dot_ab(a, wqk_ref[:, GROUP:]).astype(bf16)
-    v_ref[...] = dot_ab(a, wv_ref[...]).astype(bf16)
+    for part, ref in enumerate((q_ref, k_ref, v_ref)):
+        ref[...] = dot_ab(a, w_ref[:, part * GROUP : (part + 1) * GROUP]).astype(bf16)
     masks = half_masks()
     lane = lax.broadcasted_iota(jnp.int32, (1, 128), 1)
     for pair in range(GROUP // 128):
@@ -200,22 +210,21 @@
         ctx_ref[:, cols] = jnp.where(lane < HEAD_DIM, halves[0], halves[1]).astype(bf16)
 
 
-def attend_forward(a, w_qk, w_vo, bounds):
+def attend_forward(a, w_qkv, bounds):
     count = a.shape[0]
     rows = count // CAP
     piece = pl.BlockSpec((CAP, GROUP), lambda r, g: (r, g))
-    narrow = jax.ShapeDtypeStruct((count, D), bf16)
+    narrow = hbm((count, D), bf16)
     return pl.pallas_call(
         attend_kernel,
         grid=(rows, GROUPS),
         in_specs=[
             pl.BlockSpec((CAP, D), lambda r, g: (r, 0)),
-            pl.BlockSpec((D, 2 * GROUP), lambda r, g: (0, g)),
-            pl.BlockSpec((D, GROUP), lambda r, g: (0, g)),
+            pl.BlockSpec((D, 3 * GROUP), lambda r, g: (0, g)),
             pl.BlockSpec((1, 8, 128), lambda r, g: (r, 0, 0)),
         ],
         out_specs=[piece, piece, piece, piece, pl.BlockSpec((CAP, 128), lambda r, g: (r, 0))],
-        out_shape=[narrow, narrow, narrow, narrow, jax.ShapeDtypeStruct((count, 128), f32)],
+        out_shape=[narrow, narrow, narrow, narrow, hbm((count, 128), f32)],
         scratch_shapes=[pltpu.VMEM((CAP, CAP), f32)],
         compiler_params=params(48),
         cost_estimate=cost(
@@ -223,7 +232,7 @@
             rows * HEADS * CAP * CAP,
         ),
         name="attend_forward",
-    )(a, w_qk, w_vo, bounds)
+    )(*pinned(a, w_qkv, bounds))
 
 
 def attend_back_kernel(
@@ -287,16 +296,14 @@
         return
     blocks, core_bit = plan
     size = D // blocks
-    me = me_ref[0]
-    on_high = (me & core_bit) != 0
+    on_high = (me_ref[0] & core_bit) != 0
     for block in range(blocks):
         if block & core_bit:
             continue
         low = acc_scr[block * size : (block + 1) * size, :]
         other = block | core_bit
         high = acc_scr[other * size : (other + 1) * size, :]
-        place = me ^ block
-        slot = (place // (2 * core_bit)) * core_bit + place % core_bit
+        slot = (block // (2 * core_bit)) * core_bit + block % core_bit
         keep_ref[slot] = jnp.where(on_high, high, low).astype(bf16)
         send_ref[slot] = jnp.where(on_high, low, high).astype(bf16)
 
@@ -331,9 +338,9 @@
             scratch_shapes=[pltpu.VMEM((CAP, CAP), f32), pltpu.VMEM((D, width), f32)],
         ),
         out_shape=[
-            jax.ShapeDtypeStruct((count, groups * 3 * GROUP), bf16),
-            jax.ShapeDtypeStruct((half, size, groups * width), bf16),
-            jax.ShapeDtypeStruct((half, sent, groups * width), bf16),
+            hbm((count, groups * 3 * GROUP), bf16),
+            hbm((half, size, groups * width), bf16),
+            hbm((half, sent, groups * width), bf16),
         ],
         compiler_params=params(40),
         cost_estimate=cost(
@@ -342,7 +349,7 @@
             groups * (GROUP // HEAD_DIM) * count * CAP,
         ),
         name="attend_backward",
-    )(me, at, q, k, v, ctx, dctx, lse, bounds, gwo)
+    )(me, *pinned(at, q, k, v, ctx, dctx, lse, bounds, gwo))
 
 
 def middle_kernel(ctx_ref, wo_ref, x_ref, vec_ref, att_ref, c_ref):
@@ -352,7 +359,7 @@
     c_ref[...] = (normalized * vec_ref[2:3, :] + vec_ref[3:4, :]).astype(bf16)
 
 
-def middle(ctx, w_vo, x, vectors):
+def middle(ctx, w_o, x, vectors):
     count = ctx.shape[0]
     tile = 320
     wide = pl.BlockSpec((tile, D), lambda t: (t, 0))
@@ -360,18 +367,18 @@
         middle_kernel,
         grid=(count // tile,),
         in_specs=[
-            wide, pl.BlockSpec((D, D), lambda t: (0, 1)), wide,
+            wide, pl.BlockSpec((D, D), lambda t: (0, 0)), wide,
             pl.BlockSpec((7, D), lambda t: (0, 0)),
         ],
         out_specs=[wide, wide],
         out_shape=[
-            jax.ShapeDtypeStruct((count, D), f32),
-            jax.ShapeDtypeStruct((count, D), bf16),
+            hbm((count, D), f32),
+            hbm((count, D), bf16),
         ],
         compiler_params=params(32),
         cost_estimate=cost(2 * count * D * D, 10 * count * D),
         name="middle",
-    )(ctx, w_vo, x, vectors)
+    )(*pinned(ctx, w_o, x, vectors))
 
 
 ERF_P = 0.3275911 / math.sqrt(2.0)
@@ -422,7 +429,7 @@
         for block in range(0, blocks, 2):
             low = grad[block * size : (block + 1) * size]
             high = grad[(block + 1) * size : (block + 2) * size]
-            slot = (me_ref[2] ^ block) >> 1
+            slot = block // 2
             keep_ref[which, slot, 0] = jnp.where(on_high, high, low).astype(bf16)
             send_ref[which, slot, 0] = jnp.where(on_high, low, high).astype(bf16)
     if not split:
@@ -431,7 +438,8 @@
 
 def mlp_all(me, c, dm, weights, bias, split):
     count = c.shape[0]
-    blocks, mp, _, size, units = weights.shape
+    blocks, mp, _, units = weights.shape
+    size = D // blocks
     width = 384
     subs = units // width
     half = blocks // 2 if split else 1
@@ -441,7 +449,7 @@
 
     def weight_spec(which):
         return pl.BlockSpec(
-            (blocks, 1, 1, size, width), lambda j, s, me, which=which: (0, me[1] ^ j, which, 0, s)
+            (blocks, 1, size, width), lambda j, s, me, which=which: (0, me[1] ^ j, which, s)
         )
 
     return pl.pallas_call(
@@ -457,23 +465,23 @@
                 all_rows, all_rows,
                 pl.BlockSpec((2, half, 1, rows_out, width), lambda j, s, me: (0, 0, j, 0, s)),
                 pl.BlockSpec((2, half, 1, sent, width), lambda j, s, me: (0, 0, j, 0, s)),
-                pl.BlockSpec((1, 8, width), lambda j, s, me: ((me[1] ^ j) * subs + s, 0, 0)),
+                pl.BlockSpec((1, 8, width), lambda j, s, me: (me[1] ^ j, 0, s)),
             ],
             scratch_shapes=[pltpu.VMEM((D, count), bf16), pltpu.VMEM((D, count), bf16)],
         ),
         out_shape=[
-            jax.ShapeDtypeStruct((count, D), f32),
-            jax.ShapeDtypeStruct((count, D), f32),
-            jax.ShapeDtypeStruct((2, half, mp, rows_out, units), bf16),
-            jax.ShapeDtypeStruct((2, half, mp, sent, units), bf16),
-            jax.ShapeDtypeStruct((mp * subs, 8, width), f32),
+            hbm((count, D), f32),
+            hbm((count, D), f32),
+            hbm((2, half, mp, rows_out, units), bf16),
+            hbm((2, half, mp, sent, units), bf16),
+            hbm((mp, 8, units), f32),
         ],
         compiler_params=params(58),
         cost_estimate=cost(
             12 * count * D * mp * units, 12 * count * D + 8 * mp * units * D, 2 * count * mp * units
         ),
         name="mlp_all",
-    )(me, c, dm, weights, weights, bias.reshape(mp * subs, 1, width))
+    )(me, *pinned(c, dm, weights, weights, bias.reshape(mp * subs, 1, width)))
 
 
 def turn_kernel(
@@ -518,7 +526,7 @@
     gwo_ref[...] += dot_ab(ctx_ref[...], datt, 0, 0)
 
 
-def turn(x, dy, att, mlp, dc, ctx, w_vo, vectors):
+def turn(x, dy, att, mlp, dc, ctx, w_o, vectors):
     count = x.shape[0]
     tile = 320
     wide = pl.BlockSpec((tile, D), lambda t: (t, 0))
@@ -526,7 +534,7 @@
         turn_kernel,
         grid=(count // tile,),
         in_specs=[
-            wide, wide, wide, wide, wide, wide, pl.BlockSpec((D, D), lambda t: (0, 1)),
+            wide, wide, wide, wide, wide, wide, pl.BlockSpec((D, D), lambda t: (0, 0)),
             pl.BlockSpec((7, D), lambda t: (0, 0)),
         ],
         out_specs=[
@@ -534,17 +542,17 @@
             pl.BlockSpec((8, D), lambda t: (0, 0)),
         ],
         out_shape=[
-            jax.ShapeDtypeStruct((count, D), bf16),
-            jax.ShapeDtypeStruct((count, D), f32),
-            jax.ShapeDtypeStruct((count, D), bf16),
-            jax.ShapeDtypeStruct((D, D), f32),
-            jax.ShapeDtypeStruct((8, D), f32),
+            hbm((count, D), bf16),
+            hbm((count, D), f32),
+            hbm((count, D), bf16),
+            hbm((D, D), f32),
+            hbm((8, D), f32),
         ],
         scratch_shapes=[pltpu.VMEM((tile, D), bf16)],
         compiler_params=params(48),
         cost_estimate=cost(4 * count * D * D, 26 * count * D),
         name="turn",
-    )(x, dy, att, mlp, dc, ctx, w_vo, vectors)
+    )(*pinned(x, dy, att, mlp, dc, ctx, w_o, vectors))
 
 
 def entry_kernel(
@@ -552,7 +560,7 @@
 ):
     count = len(spans)
     grads = refs[:count]
-    wqk_ref, wv_ref, x_ref, part_ref, vec_ref, out_ref, gvec_ref, da_scr = refs[count:]
+    w_ref, x_ref, part_ref, vec_ref, out_ref, gvec_ref, da_scr = refs[count:]
 
     @pl.when(pl.program_id(0) == 0)
     def _():
@@ -560,16 +568,9 @@
 
     da = None
     for ref, (start, groups) in zip(grads, spans):
-        for at in range(groups):
-            group, left = start + at, at * 3 * GROUP
-            term = dot_ab(
-                ref[:, left : left + 2 * GROUP],
-                wqk_ref[:, group * 2 * GROUP : (group + 1) * 2 * GROUP], 1, 1,
-            ) + dot_ab(
-                ref[:, left + 2 * GROUP : left + 3 * GROUP],
-                wv_ref[:, group * GROUP : (group + 1) * GROUP], 1, 1,
-            )
-            da = term if da is None else da + term
+        left, right = start * 3 * GROUP, (start + groups) * 3 * GROUP
+        term = dot_ab(ref[...], w_ref[:, left:right], 1, 1)
+        da = term if da is None else da + term
     da_scr[...] = da
     tile = 64
 
@@ -588,7 +589,7 @@
     lax.fori_loop(0, x_ref.shape[0] // tile, body, 0)
 
 
-def entry(grads, spans, w_qk, w_vo, x, part, vectors):
+def entry(grads, spans, w_qkv, x, part, vectors):
     count = x.shape[0]
     tile = 320
     wide = pl.BlockSpec((tile, D), lambda r: (r, 0))
@@ -597,22 +598,21 @@
         grid=(count // tile,),
         in_specs=[pl.BlockSpec((tile, g.shape[1]), lambda r: (r, 0)) for g in grads]
         + [
-            pl.BlockSpec((D, 2 * D), lambda r: (0, 0)), pl.BlockSpec((D, D), lambda r: (0, 0)),
-            wide, wide, pl.BlockSpec((7, D), lambda r: (0, 0)),
+            pl.BlockSpec((D, 3 * D), lambda r: (0, 0)), wide, wide, pl.BlockSpec((7, D), lambda r: (0, 0)),
         ],
         out_specs=[
             pl.BlockSpec((tile, 2 * D), lambda r: (r, 0)),
             pl.BlockSpec((8, D), lambda r: (0, 0)),
         ],
         out_shape=[
-            jax.ShapeDtypeStruct((count, 2 * D), bf16),
-            jax.ShapeDtypeStruct((8, D), f32),
+            hbm((count, 2 * D), bf16),
+            hbm((8, D), f32),
         ],
         scratch_shapes=[pltpu.VMEM((tile, D), f32)],
         compiler_params=params(32),
         cost_estimate=cost(2 * count * D * 3 * D, 24 * count * D),
         name="entry",
-    )(*grads, w_qk, w_vo, x, part, vectors)
+    )(*pinned(*grads, w_qkv, x, part, vectors))
 
 
 def finish_kernel(grad_ref, rank_ref, cot_ref, out_ref, ext_scr):
@@ -634,12 +634,12 @@
             pl.BlockSpec((1, SEQ, D), lambda r: (r, 0, 0)),
         ],
         out_specs=pl.BlockSpec((1, SEQ, D), lambda r: (r, 0, 0)),
-        out_shape=jax.ShapeDtypeStruct((rows, SEQ, D), f32),
+        out_shape=hbm((rows, SEQ, D), f32),
         scratch_shapes=[pltpu.VMEM((CAP, 2 * D + 128), bf16)],
         compiler_params=params(48),
         cost_estimate=cost(4 * rows * CAP * SEQ * D, 18 * rows * CAP * D),
         name="finish",
-    )(grad, rank, cotangent)
+    )(*pinned(grad, rank, cotangent))
 
 
 def place_kernel(y_ref, rank_ref, tok_ref, out_ref, ext_scr):
@@ -661,12 +661,12 @@
             pl.BlockSpec((1, SEQ, D), lambda r: (r, 0, 0)),
         ],
         out_specs=pl.BlockSpec((1, SEQ, D), lambda r: (r, 0, 0)),
-        out_shape=jax.ShapeDtypeStruct((rows, SEQ, D), bf16),
+        out_shape=hbm((rows, SEQ, D), bf16),
         scratch_shapes=[pltpu.VMEM((CAP, D + 128), bf16)],
         compiler_params=params(48),
         cost_estimate=cost(2 * rows * CAP * SEQ * D, 10 * rows * CAP * D),
         name="place",
-    )(y, rank, tokens)
+    )(*pinned(y, rank, tokens))
 
 
 def lamb_moments(weight, gradient, first_mom, second_mom, decay):
@@ -679,6 +679,149 @@
         + decay * weight
     )
     return (first_new, second_new, update)
+
+
+def square_sum(value):
+    return jnp.sum(jnp.sum(value * value, 1, keepdims=True), 0, keepdims=True)
+
+
+def added(mine_ref, got_refs, place):
+    result = mine_ref[place]
+    for ref in got_refs:
+        result = result + ref[place].astype(f32)
+    return result
+
+
+def lanes_of(pairs):
+    lane = lax.broadcasted_iota(jnp.int32, (8, 128), 1)
+    result = jnp.zeros((8, 128), f32)
+    for place, value in pairs:
+        result = result + jnp.where(lane == place, value, 0.0)
+    return result
+
+
+def mlp_lamb_kernel(*refs, gots):
+    weights, (mine_ref, *rest) = refs[:6], refs[6:]
+    got_refs, outs = rest[:gots], rest[gots:]
+    pairs = []
+    for which in range(2):
+        weight_ref, first_ref, second_ref = weights[3 * which : 3 * which + 3]
+        grad = added(mine_ref, got_refs, which)
+        weight = weight_ref[...]
+        news = lamb_moments(weight, grad, first_ref[...], second_ref[...], decay_mat)
+        for ref, value in zip(outs[3 * which : 3 * which + 3], news):
+            ref[...] = value
+        pairs += [(2 + which, square_sum(weight)), (6 + which, square_sum(news[2]))]
+    outs[6][...] = lanes_of(pairs)
+
+
+def mlp_lamb(moments, mine, gots):
+    like = jax.ShapeDtypeStruct(moments[0].shape, f32)
+    return pl.pallas_call(
+        partial(mlp_lamb_kernel, gots=len(gots)),
+        out_shape=[like] * 6 + [jax.ShapeDtypeStruct((8, 128), f32)],
+        compiler_params=params(24),
+        cost_estimate=cost(40 * mine.size, 40 * mine.size),
+        name="mlp_lamb",
+    )(*moments, mine, *gots)
+
+
+def attn_lamb_kernel(*refs, gots):
+    moments, (mine_ref, *rest) = refs[:6], refs[6:]
+    got_refs, rest = rest[:gots], rest[gots:]
+    one_ref, two_ref, bias_ref, sq_ref, *outs = rest
+    sums = [jnp.zeros((1, 1), f32) for _ in range(4)]
+    for part in range(4):
+        tensor = part // 3
+        weight_ref, first_ref, second_ref = moments[3 * tensor : 3 * tensor + 3]
+        for group in range(GROUPS):
+            left = (group * 4 + part) * GROUP
+            grad = added(mine_ref, got_refs, (slice(None), slice(left, left + GROUP)))
+            left = (part % 3) * D + group * GROUP
+            cols = (slice(None), slice(left, left + GROUP))
+            weight = weight_ref[cols]
+            news = lamb_moments(weight, grad, first_ref[cols], second_ref[cols], decay_mat)
+            for ref, value in zip(outs[3 * tensor : 3 * tensor + 3], news):
+                ref[cols] = value
+            sums[tensor] += square_sum(weight)
+            sums[2 + tensor] += square_sum(news[2])
+    load_ref = outs[6]
+    load_ref[...] = jnp.zeros_like(load_ref)
+    load_ref[0:2, :] = one_ref[0:2, :]
+    load_ref[2:7, :] = two_ref[0:5, :]
+    for i in range(FF // D):
+        load_ref[7 + i : 8 + i, :] = bias_ref[i, 0:1, :]
+    squares = sq_ref[...] + lanes_of(list(zip((0, 1, 4, 5), sums)))
+    load_ref[LOAD_SQ : LOAD_SQ + 1, 0:128] = squares[0:1]
+
+
+LOAD_SQ = 7 + FF // D
+LOAD_ROWS = 16
+
+
+def attn_lamb(moments, mine, gots, gvec_one, gvec_two, gbias, squares):
+    qkv_like = jax.ShapeDtypeStruct(moments[0].shape, f32)
+    proj_like = jax.ShapeDtypeStruct(moments[3].shape, f32)
+    return pl.pallas_call(
+        partial(attn_lamb_kernel, gots=len(gots)),
+        out_shape=[qkv_like] * 3 + [proj_like] * 3
+        + [jax.ShapeDtypeStruct((LOAD_ROWS, D), f32)],
+        compiler_params=params(24),
+        cost_estimate=cost(40 * mine.size, 40 * mine.size),
+        name="attn_lamb",
+    )(*moments, mine, *gots, gvec_one, gvec_two, gbias, squares)
+
+
+def last_kernel(
+    load_ref, qkv_ref, proj_ref, up_ref, down_ref, qkv_upd, proj_upd, up_upd, down_upd,
+    bias_ref, bias_one, bias_two, vec_ref, vec_one, vec_two,
+    norms_ref, qkv_new, proj_new, up_new, down_new,
+    bias_new, bias_first, bias_second, vec_new, vec_first, vec_second, bias_scr,
+):
+    norms = jnp.sqrt(load_ref[LOAD_SQ : LOAD_SQ + 1, 0:128])
+    norms_ref[0:1, :] = norms[:, 0:4]
+    norms_ref[1:2, :] = norms[:, 4:8]
+    for i, (weight, upd, new) in enumerate(
+        (
+            (qkv_ref, qkv_upd, qkv_new), (proj_ref, proj_upd, proj_new),
+            (up_ref, up_upd, up_new), (down_ref, down_upd, down_new),
+        )
+    ):
+        ratio = norms[:, i : i + 1] / norms[:, 4 + i : 5 + i]
+        new[...] = weight[...] - rate_lamb * ratio * upd[...]
+    for i in range(FF // 128):
+        row, left = 7 + i // (D // 128), i % (D // 128) * 128
+        bias_scr[i : i + 1, :] = load_ref[row : row + 1, left : left + 128]
+    bias = bias_ref[...]
+    first, second, upd = lamb_moments(bias, bias_scr[...], bias_one[...], bias_two[...], 0.0)
+    bias_first[...] = first
+    bias_second[...] = second
+    bias_new[...] = bias - rate_lamb * (
+        jnp.sqrt(square_sum(bias)) / jnp.sqrt(square_sum(upd))
+    ) * upd
+    vec = vec_ref[...]
+    first, second, upd = lamb_moments(vec, load_ref[0:7, :], vec_one[...], vec_two[...], 0.0)
+    vec_first[...] = first
+    vec_second[...] = second
+    ratio = jnp.sqrt(jnp.sum(vec * vec, -1, keepdims=True)) / jnp.sqrt(
+        jnp.sum(upd * upd, -1, keepdims=True)
+    )
+    vec_new[...] = vec - rate_lamb * ratio * upd
+
+
+def last(load, weights, upds, bias, vecs):
+    def like(value):
+        return jax.ShapeDtypeStruct(value.shape, f32)
+
+    return pl.pallas_call(
+        last_kernel,
+        out_shape=[jax.ShapeDtypeStruct((2, 4), f32)] + [like(w) for w in weights]
+        + [like(b) for b in bias] + [like(v) for v in vecs],
+        scratch_shapes=[pltpu.VMEM((FF // 128, 128), f32)],
+        compiler_params=params(24),
+        cost_estimate=cost(1 << 20, 4 << 20),
+        name="last",
+    )(load, *weights, *upds, *bias, *vecs)
 
 
 def swap(value, axis, size, bit):
@@ -726,196 +869,187 @@
     def merge(held, came, high, axis):
         return jnp.where(high, jnp.stack([came, held], axis), jnp.stack([held, came], axis))
 
-    narrow = qkv_weight.astype(bf16)
     size = D // world
-    low_qk = narrow[:, : 2 * D].reshape(size, 2, GROUPS, GROUP).transpose(0, 2, 1, 3)
-    low_qk = low_qk.reshape(size, 2 * D)
-    low_vo = jnp.concatenate([narrow[:, 2 * D :], proj_weight.astype(bf16)], 1)
-    mlp_low = jnp.stack([up_weight.astype(bf16), down_weight.astype(bf16).T])
+    low_qkv = qkv_weight.astype(bf16).reshape(size, 3, GROUPS, GROUP).transpose(0, 2, 1, 3)
+    low_qkv = low_qkv.reshape(size, 3 * D)
+    proj_low = proj_weight.astype(bf16)
+    mlp_low = jnp.concatenate([up_weight.astype(bf16), down_weight.astype(bf16).T], 0)
     picked = pick_rows(selected, image_ids, tokens, cotangent, vectors)
     if fast:
-        low_both = jnp.concatenate([low_qk, low_vo], 1)
-        held = [low_both] + [swap_mp(low_both, k) for k in range(1, mp)]
+        held = [low_qkv] + [swap_mp(low_qkv, k) for k in range(1, mp)]
         held, picked = tie(held, picked)
-        held = jnp.stack(held).reshape((2,) * (mp.bit_length() - 1) + (size, 4 * D))
+        held = jnp.stack(held).reshape((2,) * (mp.bit_length() - 1) + (size, 3 * D))
         for axis in range(mp.bit_length() - 1):
             flip = ((mp_at >> (mp.bit_length() - 2 - axis)) & 1) != 0
             held = jnp.where(flip, jnp.flip(held, axis), held)
-        held = held.reshape(mp, size, 4 * D)
+        held = held.reshape(mp, size, 3 * D)
         halves = []
         for half, order in enumerate((ups, downs)):
-            value = held[:, :, half * 2 * D : (half + 1) * 2 * D]
+            value = held[:, :, half * D * 3 // 2 : (half + 1) * D * 3 // 2]
             done = []
             for bit in order + (1,):
                 axis = sum(other > bit for other in done)
                 done.append(bit)
                 value = merge(value, swap_dp(value, bit), (dp_at & bit) != 0, axis)
-            halves.append(value.reshape(D, 2 * D))
-        w_qk, w_vo = halves
+            halves.append(value.reshape(D, 3 * D // 2))
+        w_qkv = jnp.concatenate(halves, 1)
+        mlp_mat = lax.all_gather(
+            jnp.concatenate([mlp_low, proj_low], 0), everyone, axis=0, tiled=True
+        )
+        mlp_mat = mlp_mat.reshape(dp, mp, mlp_low.shape[0] + size, FF // mp)
+        w_o = mlp_mat[:, :, mlp_low.shape[0] :].reshape(D, D)
     else:
-        w_qk = lax.all_gather(low_qk, everyone, axis=0, tiled=True)
-        w_vo = lax.all_gather(low_vo, everyone, axis=0, tiled=True)
-    mlp_mat = lax.all_gather(mlp_low[None], everyone, axis=0, tiled=True)
-    mlp_mat = mlp_mat.reshape(dp, mp, 2, D // dp, FF // mp)
-    if not fast:
-        mlp_mat = mlp_mat.transpose(1, 2, 0, 3, 4).reshape(1, mp, 2, D, FF // mp)
-
-    def stage(terms, left, bit):
-        axis = left.index(bit)
-        give = total([lax.index_in_dim(t, 1, axis, False) for t in terms]).astype(bf16)
-        terms = [lax.index_in_dim(t, 0, axis, False) for t in terms]
-        return terms + [swap_dp(give, bit)], [b for b in left if b != bit]
-
-    def as_bits(value):
-        return value.reshape((2,) * len(bits) + (mp,) + value.shape[-2:])
+        w_qkv = lax.all_gather(low_qkv, everyone, axis=0, tiled=True)
+        w_o = lax.all_gather(proj_low, everyone, axis=0, tiled=True)
+        mlp_mat = lax.all_gather(mlp_low, everyone, axis=0, tiled=True)
+        mlp_mat = mlp_mat.reshape(dp, mp, 2, D // dp, FF // mp).transpose(1, 2, 0, 3, 4)
+        mlp_mat = mlp_mat.reshape(1, mp, 2 * D, FF // mp)
+
+    def view(term, **more):
+        array, names, fixed = term
+        fixed = {**fixed, **more}
+        start = [fixed.get(name, 0) for name in names] + [0, 0]
+        extent = [1 if name in fixed else n for name, n in zip(names, array.shape)]
+        kept = [n for name, n in zip(names, array.shape) if name not in fixed]
+        out = lax.dynamic_slice(array, start, tuple(extent) + array.shape[-2:])
+        return out.reshape(tuple(kept) + array.shape[-2:])
+
+    def name_of(bit):
+        return f"b{bit}"
+
+    def opened(array, which=None):
+        names = [name_of(bit) for bit in reversed(bits)] + ["mp"]
+        fixed = {}
+        shape = (2,) * len(bits) + (mp,) + array.shape[-2:]
+        if which is not None:
+            names, shape, fixed = ["which"] + names, (2,) + shape, {"which": which}
+        return (array.reshape(shape), names, fixed)
+
+    def step(chains):
+        for chain in chains:
+            terms, order = chain
+            bit = order.pop(0)
+            name, mine = name_of(bit), (dp_at // bit) & 1
+            give = total([view(term, **{name: 1 - mine}) for term in terms]).astype(bf16)
+            left = [n for n in terms[0][1] if n not in terms[0][2] and n != name]
+            chain[0] = [(t[0], t[1], {**t[2], name: mine}) for t in terms]
+            chain[0].append((swap_dp(give, bit), left, {}))
+
+    def newest(chains):
+        return [chain[0][-1][0] for chain in chains]
+
+    def renew(chains, arrays):
+        for chain, array in zip(chains, arrays):
+            chain[0][-1] = (array,) + chain[0][-1][1:]
 
     x, dy, a, at, dm, rank, bounds = picked
-    q, k, v, ctx, lse = attend_forward(a, w_qk, w_vo, bounds)
-    att, c = middle(ctx, w_vo, x, vectors)
-    mlp, dc, mlp_keep, mlp_send, bias_rows = mlp_all(me, c, dm, mlp_mat, up_bias, fast)
+    q, k, v, ctx, lse = attend_forward(a, w_qkv, bounds)
+    att, c = middle(ctx, w_o, x, vectors)
+    mlp, dc, mlp_keep, mlp_send, gbias = mlp_all(me, c, dm, mlp_mat, up_bias, fast)
     plan = (world, mp) if fast else None
     spans = ((0, GROUPS - 1), (GROUPS - 1, 1))
     back = partial(attend_backward, me, at, q, k, v, ctx)
     if fast:
         mlp_came = swap_dp(mlp_send, 1)
-    y, part, dctx, gwo, gvec_two = turn(x, dy, att, mlp, dc, ctx, w_vo, vectors)
+    y, part, dctx, gwo, gvec_two = turn(x, dy, att, mlp, dc, ctx, w_o, vectors)
     if fast:
         mlp_came, dctx = tie(mlp_came, dctx)
-        chains = []
-        for which, order in enumerate((ups, downs)):
-            terms = [as_bits(mlp_keep[which]), as_bits(mlp_came[which])]
-            chains.append([terms, list(reversed(bits)), list(order)])
-
-        def step(chains):
-            for chain in chains:
-                chain[0], chain[1] = stage(chain[0], chain[1], chain[2].pop(0))
-
+        chains = [
+            [[opened(mlp_keep, which), opened(mlp_came, which)], list(order)]
+            for which, order in enumerate((ups, downs))
+        ]
         step(chains)
         d_one, keep_one, send_one = back(dctx, lse, bounds, gwo, plan, *spans[0])
-        (chains[0][0][-1], chains[1][0][-1]), d_one, send_one, dctx = tie(
-            (chains[0][0][-1], chains[1][0][-1]), d_one, send_one, dctx
-        )
-        while chains[0][2]:
+        arrays, d_one, send_one, dctx = tie(newest(chains), d_one, send_one, dctx)
+        renew(chains, arrays)
+        while chains[0][1]:
             step(chains)
         came_one = swap_dp(send_one, 1)
         d_two, keep_two, send_two = back(dctx, lse, bounds, gwo, plan, *spans[1])
-        (chains[0][0][-1], chains[1][0][-1]), came_one, send_two, d_two, y = tie(
-            (chains[0][0][-1], chains[1][0][-1]), came_one, send_two, d_two, y
-        )
+        arrays, came_one, send_two, d_two, y = tie(newest(chains), came_one, send_two, d_two, y)
+        renew(chains, arrays)
         mlp_sent = []
         for k_at in range(1, mp):
-            give = jnp.stack([total([t[k_at] for t in chain[0]]) for chain in chains])
+            give = jnp.stack([total([view(t, mp=k_at) for t in chain[0]]) for chain in chains])
             mlp_sent.append(swap_mp(give.astype(bf16), k_at))
-        mlp_mine = jnp.stack([total([t[0] for t in chain[0]]) for chain in chains])
-        one = [[as_bits(keep_one), as_bits(came_one)], list(reversed(bits)), list(ups)]
+        mlp_mine = jnp.stack([total([view(t, mp=0) for t in chain[0]]) for chain in chains])
+        one = [[opened(keep_one), opened(came_one)], list(ups)]
         came_two = swap_dp(send_two, 1)
         step([one])
         block_output = place(y, rank, tokens)
         came_two, block_output, d_one = tie(came_two, block_output, d_one)
-        two = [[as_bits(keep_two), as_bits(came_two)], list(reversed(bits)), list(downs)]
+        two = [[opened(keep_two), opened(came_two)], list(downs)]
         step([two])
-        grad, gvec_one = entry((d_one, d_two), spans, w_qk, w_vo, x, part, vectors)
-        one[0][-1], two[0][-1], grad, gvec_one = tie(one[0][-1], two[0][-1], grad, gvec_one)
-        while one[2]:
+        grad, gvec_one = entry((d_one, d_two), spans, w_qkv, x, part, vectors)
+        arrays, grad, gvec_one = tie(newest([one, two]), grad, gvec_one)
+        renew([one, two], arrays)
+        while one[1]:
             step([one, two])
         input_grad = finish(grad, rank, cotangent)
-        one[0][-1], two[0][-1], input_grad, mlp_sent = tie(
-            one[0][-1], two[0][-1], input_grad, mlp_sent
-        )
+        arrays, input_grad, mlp_sent = tie(newest([one, two]), input_grad, mlp_sent)
+        renew([one, two], arrays)
         attn_sent = []
         for k_at in range(1, mp):
-            give = [total([t[k_at] for t in chain[0]]).astype(bf16) for chain in (one, two)]
+            give = [
+                total([view(t, mp=mp_at ^ k_at) for t in chain[0]]).astype(bf16)
+                for chain in (one, two)
+            ]
             attn_sent.append(swap_mp(jnp.concatenate(give, 1), k_at))
-        mlp_sum = mlp_mine + total(mlp_sent)
-        attn_sum = jnp.concatenate(
-            [total([t[0] for t in chain[0]]) for chain in (one, two)], 1
-        ) + total(attn_sent)
+        attn_mine = jnp.concatenate(
+            [total([view(t, mp=mp_at) for t in chain[0]]) for chain in (one, two)], 1
+        )
     else:
         d_all, attn_keep, _ = back(dctx, lse, bounds, gwo, plan, 0, GROUPS)
         block_output = place(y, rank, tokens)
-        grad, gvec_one = entry((d_all,), ((0, GROUPS),), w_qk, w_vo, x, part, vectors)
+        grad, gvec_one = entry((d_all,), ((0, GROUPS),), w_qkv, x, part, vectors)
         input_grad = finish(grad, rank, cotangent)
         shaped = mlp_keep[:, 0].reshape(2, mp, dp, D // dp, FF // mp)
         shaped = jnp.take(shaped, mp_at ^ jnp.arange(mp), axis=1)
         shaped = shaped.transpose(2, 1, 0, 3, 4).reshape(world, 2, D // dp, FF // mp)
-        mlp_sum = lax.psum_scatter(shaped, everyone, scatter_dimension=0, tiled=True)[0]
-        mlp_sum = mlp_sum.astype(f32)
-        attn_sum = lax.psum_scatter(attn_keep[0], everyone, scatter_dimension=0, tiled=True)
-        attn_sum = attn_sum.astype(f32)
-    attn_sum = attn_sum.reshape(size, GROUPS, 4, GROUP).transpose(0, 2, 1, 3)
-    attn_sum = attn_sum.reshape(size, 4 * D)
-    qkv_sum, proj_sum = attn_sum[:, : 3 * D], attn_sum[:, 3 * D :]
-    up_sum, down_sum = mlp_sum[0], mlp_sum[1].T
-
-    qkv_first_new, qkv_second_new, qkv_upd = lamb_moments(
-        qkv_weight, qkv_sum, qkv_first, qkv_second, decay_mat
+        mlp_mine = lax.psum_scatter(shaped, everyone, scatter_dimension=0, tiled=True)[0]
+        mlp_mine = mlp_mine.astype(f32)
+        attn_mine = lax.psum_scatter(attn_keep[0], everyone, scatter_dimension=0, tiled=True)
+        attn_mine = attn_mine.astype(f32)
+        mlp_sent, attn_sent = [], []
+
+    *mlp_news, squares = mlp_lamb(
+        (up_weight, up_first, up_second, down_weight.T, down_first.T, down_second.T),
+        mlp_mine, mlp_sent,
     )
-    proj_first_new, proj_second_new, proj_upd = lamb_moments(
-        proj_weight, proj_sum, proj_first, proj_second, decay_mat
+    *attn_news, load = attn_lamb(
+        (qkv_weight, qkv_first, qkv_second, proj_weight, proj_first, proj_second),
+        attn_mine, attn_sent, gvec_one, gvec_two, gbias, squares,
     )
-    up_first_new, up_second_new, up_upd = lamb_moments(
-        up_weight, up_sum, up_first, up_second, decay_mat
-    )
-    down_first_new, down_second_new, down_upd = lamb_moments(
-        down_weight, down_sum, down_first, down_second, decay_mat
-    )
-    squares = jnp.stack(
-        [
-            jnp.sum(value * value)
-            for value in (
-                qkv_weight, proj_weight, up_weight, down_weight,
-                qkv_upd, proj_upd, up_upd, down_upd,
-            )
-        ]
-    )
-    small = jnp.concatenate(
-        [
-            gvec_one[0:2].reshape(-1),
-            gvec_two[0:5].reshape(-1),
-            bias_rows[:, 0, :].reshape(-1),
-            jnp.pad(squares, (0, 120)),
-        ]
-    ).reshape(-1, 128)
     if fast:
         bit = 1
         while bit < dp:
-            small = small + swap_dp(small, bit)
+            load = load + swap_dp(load, bit)
             bit *= 2
         bit = 1
         while bit < mp:
-            small = small + swap_mp(small, bit)
+            load = load + swap_mp(load, bit)
             bit *= 2
     else:
-        small = lax.psum(small, everyone)
-    small = small.reshape(-1)
-    vector_sum = small[: 7 * D].reshape(7, D)
-    bias_sum = small[7 * D : 7 * D + FF]
-    weight_norms = jnp.sqrt(small[7 * D + FF : 7 * D + FF + 8]).reshape(2, 4)
-    ratios = weight_norms[0] / weight_norms[1]
-    qkv_new = qkv_weight - rate_lamb * ratios[0] * qkv_upd
-    proj_new = proj_weight - rate_lamb * ratios[1] * proj_upd
-    up_new = up_weight - rate_lamb * ratios[2] * up_upd
-    down_new = down_weight - rate_lamb * ratios[3] * down_upd
-    bias_first_new, bias_second_new, bias_upd = lamb_moments(
-        up_bias, bias_sum, bias_first, bias_second, 0.0
+        load = lax.psum(load, everyone)
+    square = (FF // 128, 128)
+    (
+        weight_norms, qkv_new, proj_new, up_new, down_new,
+        bias_new, bias_first_new, bias_second_new, *vector_news,
+    ) = last(
+        load,
+        (qkv_weight, proj_weight, up_weight, down_weight.T),
+        (attn_news[2], attn_news[5], mlp_news[2], mlp_news[5]),
+        [value.reshape(square) for value in (up_bias, bias_first, bias_second)],
+        (vectors, vector_first, vector_second),
     )
-    bias_ratio = jnp.sqrt(jnp.sum(up_bias * up_bias)) / jnp.sqrt(jnp.sum(bias_upd * bias_upd))
-    bias_new = up_bias - rate_lamb * bias_ratio * bias_upd
-    vector_first_new, vector_second_new, vector_upd = lamb_moments(
-        vectors, vector_sum, vector_first, vector_second, 0.0
-    )
-    vector_ratio = jnp.sqrt(jnp.sum(vectors * vectors, -1, keepdims=True)) / jnp.sqrt(
-        jnp.sum(vector_upd * vector_upd, -1, keepdims=True)
-    )
-    vectors_new = vectors - rate_lamb * vector_ratio * vector_upd
     return (
         block_output, input_grad, weight_norms,
-        qkv_new, qkv_first_new, qkv_second_new,
-        proj_new, proj_first_new, proj_second_new,
-        up_new, up_first_new, up_second_new,
-        down_new, down_first_new, down_second_new,
-        bias_new, bias_first_new, bias_second_new,
-        vectors_new, vector_first_new, vector_second_new,
+        qkv_new, attn_news[0], attn_news[1],
+        proj_new, attn_news[3], attn_news[4],
+        up_new, mlp_news[0], mlp_news[1],
+        down_new.T, mlp_news[3].T, mlp_news[4].T,
+        bias_new.reshape(FF), bias_first_new.reshape(FF), bias_second_new.reshape(FF),
+        *vector_news,
     )
 
 

time: 409 us -> 363 us (0.89)
  local copies, waits for them, and re-layouts: 53 us -> 4.19 us
  other arithmetic: 39 us -> 17.2 us
  waiting for transfers between devices: 40.6 us -> 60.9 us
  Pallas kernels: 217 us -> 229 us
  starting transfers between devices: 37.3 us -> 32.8 us
  between operations: 19.2 us -> 15.1 us
    unnamed x176 -> x64, local copies, waits for them, and re-layouts: 34.2 us -> 1.21 us
    all_gather x1, waiting for transfers between devices: 0.01 us -> 14.5 us  [on_device(): lax.all_gather(jnp.concatenate([mlp_low, proj_low], 0), everyone, axis=0,...]
    pallas_call x1, Pallas kernels: 76.8 us -> 63 us  [mlp_all(): pl.pallas_call(partial(mlp_kernel, blocks=blocks, split=split), grid_spec...]
    pallas_call x2, Pallas kernels: 47 us -> 57.8 us  [attend_backward(): pl.pallas_call(partial(attend_back_kernel, plan=plan, start=start), grid_...]
    ppermute x31, waiting for transfers between devices: 40.5 us -> 46.3 us  [swap(): return lax.ppermute(value, axis, [(i, i ^ bit) for i in range(size)])]
    slice x9 -> x1, local copies, waits for them, and re-layouts: 8.18 us -> 2.4 us  [on_device(): w_o = mlp_mat[:, :, mlp_low.shape[0]:].reshape(D, D)]
    convert_element_type x12, other arithmetic: 14 us -> 8.24 us  [the longest x7 5.97 us: step(): total([view(term, **{name: 1 - mine}) for term in terms]).astype(bf16)]
    another operation x1 -> x0, local copies, waits for them, and re-layouts: 5.43 us -> none  [on_device(): jnp.stack([jnp.sum(value * value) for value in (qkv_weight, proj_weight,...]
  transfers between devices with their start and end apart: 32 -> 32, of which waited for: 12 -> 13; matrix products, arithmetic and copies ran while one was open for 6% -> 3% of each run, Pallas kernels for 34% -> 44%
where the time goes in v3:
time: 363 us; the launch traced here: 359 us
  Pallas kernels  229 us (63%)
  waiting for transfers between devices  60.9 us (17%)
  starting transfers between devices  32.8 us (9%)
  other arithmetic  17.2 us (5%)
  between operations  15.1 us (4%)
  local copies, waits for them, and re-layouts  4.19 us (1%)
    pallas_call x1, Pallas kernels, mlp_all(): pl.pallas_call(partial(mlp_kernel, blocks=blocks, split=split), grid_spec...  63 us
    pallas_call x2, Pallas kernels, attend_backward(): pl.pallas_call(partial(attend_back_kernel, plan=plan, start=start), grid_...  57.8 us
    ppermute x31, waiting for transfers between devices, swap(): return lax.ppermute(value, axis, [(i, i ^ bit) for i in range(size)])  46.3 us
    ppermute x31, starting transfers between devices, swap(): return lax.ppermute(value, axis, [(i, i ^ bit) for i in range(size)])  32.8 us
    pallas_call x1, Pallas kernels, attend_forward(): pl.pallas_call(attend_kernel, grid=(rows, GROUPS), in_specs=[pl.BlockSpec...  29.2 us
    pallas_call x1, Pallas kernels, turn(): pl.pallas_call(turn_kernel, grid=(count // tile,), in_specs=[wide, wide,...  18.1 us
    pallas_call x1, Pallas kernels, entry(): pl.pallas_call(partial(entry_kernel, spans=spans), grid=(count // tile,),...  15.8 us
    all_gather x1, waiting for transfers between devices, on_device(): lax.all_gather(jnp.concatenate([mlp_low, proj_low], 0), everyone, axis=0,...  14.5 us
  transfers between devices with their start and end apart: 32, of which 13 were waited for; matrix products, arithmetic and copies ran while one was open for 3% of the time, Pallas kernels for 44%

profile of v3, /device:TPU:0, one launch (start us, length us, event | category | flops | bytes accessed | tf_op | source)
XLA Modules:
  0.0 359.1 jit_solution(7949156100415743122)
XLA Ops:
  7.3 1.0 convert_bitcast_fusion
  8.3 1.0 convert_element_type.630
  9.3 0.9 convert_element_type.632
  10.2 0.7 pad_maximum_fusion.3
  11.3 3.1 collective-permute-start
  14.4 2.6 collective-permute-start.1
  17.0 14.0 %pick_rows.1 = (bf16[1280,768]{1,0:T(8,128)(2,1)}, bf16[1280,768]{1,0:T(8,128)(2,1)}, bf16[1280,768]{1,0:T(8,128)(2,1)}, bf16[768,1280]{1,0:T(8,128)(2,1)}, bf16...) custom-call(s32[2,1,1280]{2,1,0:T(1,128)S(1)} %broadcast_in_dim.6.sel_ref, ...), custom_call_target="tpu_custom_call" | custom-call | flops 5033164800 | bytes 15728640 | tf_op jit(solution)/shard_map/pick_rows/pallas_call | solution.py:137
  31.4 1.8 collective-permute-start.3
  33.1 0.6 pad_add_fusion.me_ref
  33.7 1.5 collective-permute-start.6
  35.2 2.8 collective-permute-done.3
  38.1 1.6 collective-permute-start.4
  39.7 0.7 collective-permute-done.6
  40.5 0.9 collective-permute-start.7
  41.6 12.5 %collective-permute-done.4 = bf16[2,4,24,1152]{3,2,1,0:T(8,128)(2,1)S(1)} collective-permute-done((bf16[2,4,24,1152]{3,2,1,0:T(8,128)(2,1)S(1)}, bf16[2,4,24,1152]{3,2,1,0:T(8,128)(2,1)S(1)}, u32[]{:S(2)}, u32[]{:S(2)}) %collective-permute-start.4) | collective-permute-done | bytes 442400 | tf_op jit(solution)/shard_map/ppermute | solution.py:828
  54.3 5.1 %collective-permute-done.7 = bf16[2,4,24,1152]{3,2,1,0:T(8,128)(2,1)S(1)} collective-permute-done((bf16[2,4,24,1152]{3,2,1,0:T(8,128)(2,1)S(1)}, bf16[2,4,24,1152]{3,2,1,0:T(8,128)(2,1)S(1)}, u32[]{:S(2)}, u32[]{:S(2)}) %collective-permute-start.7) | collective-permute-done | bytes 442400 | tf_op jit(solution)/shard_map/ppermute | solution.py:828
  60.0 0.3 maximum_select_fusion
  60.5 1.5 collective-permute-done.8
  62.1 0.3 maximum_select_fusion.1
  62.4 2.1 pad_maximum_fusion.w_ref.refs_2_
  64.5 29.2 %attend_forward.1 = (bf16[1280,768]{1,0:T(8,128)(2,1)}, bf16[1280,768]{1,0:T(8,128)(2,1)}, bf16[1280,768]{1,0:T(8,128)(2,1)}, bf16[1280,768]{1,0:T(8,128)(2,1)}, f32[1280,128]{1,0:T(8,128)}) custom-call(bf16[1280,768]{1,0:T(8,128)(2,1)} %get-tuple-element.122.a_ref, bf16[768,2304]{1,0:T(8,128)(2,1)} %pad_maximum_fusion.w_ref.refs_2_, s32[2,8,128]{2,1,0:T(8,128)S(1)} %copy-done.23), custom_call_target="tpu_custom_call" | custom-call | flops 14596177920 | bytes 11796480 | tf_op jit(solution)/shard_map/attend_forward/pallas_call | solution.py:218
  93.7 14.5 %all-gather.2.cloned.1.call-done = bf16[6912,768]{1,0:T(8,128)(2,1)} async-done(((bf16[216,768]{1,0:T(8,128)(2,1)}), bf16[6912,768]{1,0:T(8,128)(2,1)}) %all-gather.2.cloned.1.call-update) | async-done | bytes 10616848 | tf_op jit(solution)/shard_map/all_gather | solution.py:896
  108.3 2.4 slice.14
  110.7 6.4 %middle.1 = (f32[1280,768]{1,0:T(8,128)}, bf16[1280,768]{1,0:T(8,128)(2,1)}) custom-call(bf16[1280,768]{1,0:T(8,128)(2,1)} %get-tuple-element.128.ctx_ref, bf16[768,768]{1,0:T(8,128)(2,1)} %bitcast.213, bf16[1280,768]{1,0:T(8,128)(2,1)} %get-tuple-element.129.x_ref.refs_3_, f32[7,768]{1,0:T(8,128)S(1)} %copy-done.10), custom_call_target="tpu_custom_call" | custom-call | flops 1509949440 | bytes 9830400 | tf_op jit(solution)/shard_map/middle/pallas_call | solution.py:366
  117.1 63.0 %mlp_all.1 = (f32[1280,768]{1,0:T(8,128)}, f32[1280,768]{1,0:T(8,128)}, bf16[2,4,4,96,768]{4,3,2,1,0:T(8,128)(2,1)}, bf16[2,4,4,96,768]{4,3,2,1,0:T(8,128)(2,1)}, f32[4,8,768]{2,1,0:T(8,128)}) custom-call(s32[3]{0:T(128)} %pad_add_fusion.me_ref, bf16[1280,768]{1,0:T(8,128)(2,1)} %get-tuple-element.130.c_ref, bf16[1280,768]{1,0:T(8,128)(2,1)} %get-tuple-element.131.dm_ref, ...), custom_call_target="tpu_custom_call" | custom-call | flops 36238786560 | bytes 30670848 | tf_op jit(solution)/shard_map/mlp_all/pallas_call | solution.py:455
  180.1 0.3 collective-permute-start.9
  180.4 18.1 %turn.1 = (bf16[1280,768]{1,0:T(8,128)(2,1)}, f32[1280,768]{1,0:T(8,128)}, bf16[1280,768]{1,0:T(8,128)(2,1)}, f32[768,768]{1,0:T(8,128)}, f32[8,768]{1,0:T(8,128)}) custom-call(bf16[1280,768]{1,0:T(8,128)(2,1)} %get-tuple-element.129.x_ref.refs_3_, bf16[1280,768]{1,0:T(8,128)(2,1)} %get-tuple-element.134.dy_ref, f32[1280,768]{1,0:T(8,128)} %get-tuple-element.135.att_ref, ...), custom_call_target="tpu_custom_call" | custom-call | flops 3019898880 | bytes 25559040 | tf_op jit(solution)/shard_map/turn/pallas_call | solution.py:533
  198.5 1.6 fusion.1
  200.1 1.6 collective-permute-start.11
  201.7 1.5 fusion
  203.2 0.6 collective-permute-start.10
  203.8 31.3 %attend_backward.2 = (bf16[1280,1536]{1,0:T(8,128)(2,1)}, bf16[16,24,2048]{2,1,0:T(8,128)(2,1)}, bf16[16,24,2048]{2,1,0:T(8,128)(2,1)}) custom-call(s32[3]{0:T(128)S(1)} %copy-done.22, bf16[768,1280]{1,0:T(8,128)(2,1)} %get-tuple-element.140.at_ref, bf16[1280,768]{1,0:T(8,128)(2,1)} %get-tuple-element.141.q_ref, bf16[1280,768]{1,0:T(8,128)(2,1)} %get-tuple-element.142.k_ref, ...), custom_call_target="tpu_custom_call" | custom-call | flops 19797114880 | bytes 13107200 | tf_op jit(solution)/shard_map/attend_backward/pallas_call | solution.py:321
  235.2 1.0 copy-done.26
  236.2 2.2 fusion.2
  238.5 1.5 collective-permute-start.12
  240.0 0.6 collective-permute-start.13
  240.6 26.5 %attend_backward.3 = (bf16[1280,768]{1,0:T(8,128)(2,1)}, bf16[16,24,1024]{2,1,0:T(8,128)(2,1)}, bf16[16,24,1024]{2,1,0:T(8,128)(2,1)}) custom-call(s32[3]{0:T(128)S(1)} %copy-done.22, bf16[768,1280]{1,0:T(8,128)(2,1)} %get-tuple-element.140.at_ref, bf16[1280,768]{1,0:T(8,128)(2,1)} %get-tuple-element.141.q_ref, bf16[1280,768]{1,0:T(8,128)(2,1)} %get-tuple-element.142.k_ref, ...), custom_call_target="tpu_custom_call" | custom-call | flops 9898557440 | bytes 6553600 | tf_op jit(solution)/shard_map/attend_backward/pallas_call | solution.py:321
  267.1 2.4 fusion.10
  269.6 1.8 collective-permute-start.22
  271.4 1.0 collective-permute-start.21
  272.5 1.7 collective-permute-start.20
  274.2 0.3 fusion.4
  274.5 1.5 collective-permute-start.16
  276.0 8.3 %place.1 = bf16[2,1280,768]{2,1,0:T(8,128)(2,1)} custom-call(bf16[1280,768]{1,0:T(8,128)(2,1)} %get-tuple-element.157.y_ref, s32[2,8,1280]{2,1,0:T(8,128)S(1)} %copy-done.12, bf16[2,1280,768]{2,1,0:T(8,128)(2,1)} %tok_ref.3), custom_call_target="tpu_custom_call" | custom-call | flops 2516582400 | bytes 9830400 | tf_op jit(solution)/shard_map/place/pallas_call | solution.py:655
  284.5 0.7 collective-permute-start.17
  285.2 15.8 %entry.1 = (bf16[1280,1536]{1,0:T(8,128)(2,1)}, f32[8,768]{1,0:T(8,128)}) custom-call(bf16[1280,1536]{1,0:T(8,128)(2,1)} %get-tuple-element.165.refs_0_, bf16[1280,768]{1,0:T(8,128)(2,1)} %get-tuple-element.166.refs_1_, bf16[768,2304]{1,0:T(8,128)(2,1)} %pad_maximum_fusion.w_ref.refs_2_, bf16[1280,768]{1,0:T(8,128)(2,1)} %get-tuple-element.129.x_ref.refs_3_, ...), custom_call_target="tpu_custom_call" | custom-call | flops 4529848320 | bytes 23592960 | tf_op jit(solution)/shard_map/entry/pallas_call | solution.py:596
  301.0 1.5 collective-permute-start.19
  302.7 0.6 collective-permute-start.18
  303.4 12.4 %finish.1 = f32[2,1280,768]{2,1,0:T(8,128)} custom-call(bf16[1280,1536]{1,0:T(8,128)(2,1)} %get-tuple-element.172.grad_ref, s32[2,8,1280]{2,1,0:T(8,128)S(1)} %copy-done.12, bf16[2,1280,768]{2,1,0:T(8,128)(2,1)} %cot_ref.3), custom_call_target="tpu_custom_call" | custom-call | flops 5033164800 | bytes 17694720 | tf_op jit(solution)/shard_map/finish/pallas_call | solution.py:628
  316.3 1.8 collective-permute-start.25
  318.3 2.6 collective-permute-start.23
  321.1 1.6 mlp_lamb.1
  322.7 2.2 collective-permute-done.25.refs_9_
  324.9 5.8 %collective-permute-done.24.refs_8_ = bf16[24,3072]{1,0:T(8,128)(2,1)S(1)} collective-permute-done((bf16[24,3072]{1,0:T(8,128)(2,1)S(1)}, bf16[24,3072]{1,0:T(8,128)(2,1)S(1)}, u32[]{:S(2)}, u32[]{:S(2)}) %collective-permute-start.24) | collective-permute-done | bytes 147488 | tf_op jit(solution)/shard_map/ppermute | solution.py:828
  330.8 1.1 attn_lamb.1
  331.9 1.2 collective-permute-done.26
  333.2 1.3 collective-permute-start.27
  334.5 2.8 collective-permute-done.27
  337.3 1.4 collective-permute-start.28
  338.7 2.8 collective-permute-done.28
  341.6 4.1 %collective-permute-done.29 = f32[16,768]{1,0:T(8,128)S(1)} collective-permute-done((f32[16,768]{1,0:T(8,128)S(1)}, f32[16,768]{1,0:T(8,128)S(1)}, u32[]{:S(2)}, u32[]{:S(2)}) %collective-permute-start.29) | collective-permute-done | bytes 49184 | tf_op jit(solution)/shard_map/ppermute | solution.py:828
  345.7 0.4 collective-permute-start.30
  346.0 4.8 %collective-permute-done.30 = f32[16,768]{1,0:T(8,128)S(1)} collective-permute-done((f32[16,768]{1,0:T(8,128)S(1)}, f32[16,768]{1,0:T(8,128)S(1)}, u32[]{:S(2)}, u32[]{:S(2)}) %collective-permute-start.30) | collective-permute-done | bytes 49184 | tf_op jit(solution)/shard_map/ppermute | solution.py:828
  350.9 1.1 last.1
  (132 shorter events, 3.5 us)
Async XLA Ops:
  7.2 3.8 %copy-start.2 = (f32[24,2304]{1,0:T(8,128)S(1)}, f32[24,2304]{1,0:T(8,128)}, u32[]{:S(2)}) copy-start(f32[24,2304]{1,0:T(8,128)} %qkv_ref.1) | copy-start | bytes 663556
  7.2 9.7 %copy-start.29 = (s32[2,1280]{1,0:T(2,128)S(1)}, s32[2,1280]{1,0:T(2,128)}, u32[]{:S(2)}) copy-start(s32[2,1280]{1,0:T(2,128)} %param.24) | copy-start | bytes 30724
  7.2 9.8 %copy-start.30 = (s32[2,1280]{1,0:T(2,128)S(1)}, s32[2,1280]{1,0:T(2,128)}, u32[]{:S(2)}) copy-start(s32[2,1280]{1,0:T(2,128)} %param.23) | copy-start | bytes 30724
  7.2 9.8 %copy-start.10 = (f32[7,768]{1,0:T(8,128)S(1)}, f32[7,768]{1,0:T(8,128)}, u32[]{:S(2)}) copy-start(f32[7,768]{1,0:T(8,128)} %vec_ref.7) | copy-start | bytes 64516
  7.2 101.0 %all-gather.2.cloned.1.call-start = ((), (), s32[]{:S(2)}) async-start(), calls=%async_computation | async-start | bytes 10948608 | tf_op jit(solution)/shard_map/all_gather | solution.py:896
  11.3 19.7 %collective-permute-start = (bf16[24,2304]{1,0:T(8,128)(2,1)S(1)}, bf16[24,2304]{1,0:T(8,128)(2,1)S(1)}, u32[]{:S(2)}, u32[]{:S(2)}) collective-permute-start(bf16[24,2304]{1,0:T(8,128)(2,1)S(1)} %reshape.968), channel_id=1, source_target_pairs={{0,1},{1,0},{2,3},{3,2},{4,5},{5,4},{6,7},{7,6},{8,9},{9,8},{10,11... | collective-permute-start | bytes 331784 | tf_op jit(solution)/shard_map/ppermute | solution.py:828
  14.4 16.7 %collective-permute-start.1 = (bf16[24,2304]{1,0:T(8,128)(2,1)S(1)}, bf16[24,2304]{1,0:T(8,128)(2,1)S(1)}, u32[]{:S(2)}, u32[]{:S(2)}) collective-permute-start(bf16[24,2304]{1,0:T(8,128)(2,1)S(1)} %reshape.968), channel_id=1, source_target_pairs={{0,2},{1,3},{2,0},{3,1},{4,6},{5,7},{6,4},{7,5},{8,10},{9,11},{10,... | collective-permute-start | bytes 331784 | tf_op jit(solution)/shard_map/ppermute | solution.py:828
  16.9 14.1 %collective-permute-start.2 = (bf16[24,2304]{1,0:T(8,128)(2,1)S(1)}, bf16[24,2304]{1,0:T(8,128)(2,1)S(1)}, u32[]{:S(2)}, u32[]{:S(2)}) collective-permute-start(bf16[24,2304]{1,0:T(8,128)(2,1)S(1)} %reshape.968), channel_id=1, source_target_pairs={{0,3},{1,2},{2,1},{3,0},{4,7},{5,6},{6,5},{7,4},{8,11},{9,10},{10,... | collective-permute-start | bytes 331784 | tf_op jit(solution)/shard_map/ppermute | solution.py:828
  31.4 6.7 %collective-permute-start.3 = (bf16[4,24,1152]{2,1,0:T(8,128)(2,1)S(1)}, bf16[4,24,1152]{2,1,0:T(8,128)(2,1)S(1)}, u32[]{:S(2)}, u32[]{:S(2)}) collective-permute-start(bf16[4,24,1152]{2,1,0:T(8,128)(2,1)S(1)} %get-tuple-element.236), channel_id=1, source_target_pairs={{0,8},{8,0},{16,24},{24,16},{1,9},{9,1},{17,25},{25,17},{2,10},{10... | collective-permute-start | bytes 663560 | tf_op jit(solution)/shard_map/ppermute | solution.py:828
  33.7 6.6 %collective-permute-start.6 = (bf16[4,24,1152]{2,1,0:T(8,128)(2,1)S(1)}, bf16[4,24,1152]{2,1,0:T(8,128)(2,1)S(1)}, u32[]{:S(2)}, u32[]{:S(2)}) collective-permute-start(bf16[4,24,1152]{2,1,0:T(8,128)(2,1)S(1)} %get-tuple-element.235), channel_id=1, source_target_pairs={{0,16},{8,24},{16,0},{24,8},{1,17},{9,25},{17,1},{25,9},{2,18},{10... | collective-permute-start | bytes 663560 | tf_op jit(solution)/shard_map/ppermute | solution.py:828
  38.1 15.9 %collective-permute-start.4 = (bf16[2,4,24,1152]{3,2,1,0:T(8,128)(2,1)S(1)}, bf16[2,4,24,1152]{3,2,1,0:T(8,128)(2,1)S(1)}, u32[]{:S(2)}, u32[]{:S(2)}) collective-permute-start(bf16[2,4,24,1152]{3,2,1,0:T(8,128)(2,1)S(1)} %maximum_select_fusion.6), channel_id=1, source_target_pairs={{0,16},{8,24},{16,0},{24,8},{1,17},{9,25},{17,1},{25,9},{2,18},{10... | collective-permute-start | bytes 1327112 | tf_op jit(solution)/shard_map/ppermute | solution.py:828
  40.5 18.9 %collective-permute-start.7 = (bf16[2,4,24,1152]{3,2,1,0:T(8,128)(2,1)S(1)}, bf16[2,4,24,1152]{3,2,1,0:T(8,128)(2,1)S(1)}, u32[]{:S(2)}, u32[]{:S(2)}) collective-permute-start(bf16[2,4,24,1152]{3,2,1,0:T(8,128)(2,1)S(1)} %maximum_select_fusion.8), channel_id=1, source_target_pairs={{0,8},{8,0},{16,24},{24,16},{1,9},{9,1},{17,25},{25,17},{2,10},{10... | collective-permute-start | bytes 1327112 | tf_op jit(solution)/shard_map/ppermute | solution.py:828
  54.2 5.8 %collective-permute-start.5 = (bf16[2,2,4,24,1152]{4,3,2,1,0:T(8,128)(2,1)S(1)}, bf16[2,2,4,24,1152]{4,3,2,1,0:T(8,128)(2,1)S(1)}, u32[]{:S(2)}, u32[]{:S(2)}) collective-permute-start(bf16[2,2,4,24,1152]{4,3,2,1,0:T(8,128)(2,1)S(1)} %maximum_select_fusion.2), channel_id=1, source_target_pairs={{0,4},{4,0},{1,5},{5,1},{2,6},{6,2},{3,7},{7,3},{8,12},{12,8},{9,1... | collective-permute-start | bytes 2654216 | tf_op jit(solution)/shard_map/ppermute | solution.py:828
  59.5 2.5 collective-permute-start.8
  62.4 2.1 copy-start.23
  180.1 18.4 %collective-permute-start.9 = (bf16[2,4,4,96,768]{4,3,2,1,0:T(8,128)(2,1)}, bf16[2,4,4,96,768]{4,3,2,1,0:T(8,128)(2,1)}, u32[]{:S(2)}, u32[]{:S(2)}) collective-permute-start(bf16[2,4,4,96,768]{4,3,2,1,0:T(8,128)(2,1)} %get-tuple-element.133), channel_id=1, source_target_pairs={{0,4},{4,0},{1,5},{5,1},{2,6},{6,2},{3,7},{7,3},{8,12},{12,8},{9,1... | collective-permute-start | bytes 14155784 | tf_op jit(solution)/shard_map/ppermute | solution.py:828
  180.4 18.1 %copy-start.24 = (bf16[2,4,4,96,768]{4,3,2,1,0:T(8,128)(2,1)S(1)}, bf16[2,4,4,96,768]{4,3,2,1,0:T(8,128)(2,1)}, u32[]{:S(2)}) copy-start(bf16[2,4,4,96,768]{4,3,2,1,0:T(8,128)(2,1)} %get-tuple-element.132) | copy-start | bytes 14155780
  200.1 3.7 %copy-start.22 = (s32[3]{0:T(128)S(1)}, s32[3]{0:T(128)}, u32[]{:S(2)}) copy-start(s32[3]{0:T(128)} %pad_add_fusion.me_ref) | copy-start | bytes 40
  200.1 35.1 %collective-permute-start.11 = (bf16[2,4,96,768]{3,2,1,0:T(8,128)(2,1)S(1)}, bf16[2,4,96,768]{3,2,1,0:T(8,128)(2,1)S(1)}, u32[]{:S(2)}, u32[]{:S(2)}) collective-permute-start(bf16[2,4,96,768]{3,2,1,0:T(8,128)(2,1)S(1)} %fusion.1), channel_id=1, source_target_pairs={{0,16},{8,24},{16,0},{24,8},{1,17},{9,25},{17,1},{25,9},{2,18},{10... | collective-permute-start | bytes 3538952 | tf_op jit(solution)/shard_map/ppermute | solution.py:828
  203.2 32.0 %collective-permute-start.10 = (bf16[2,4,96,768]{3,2,1,0:T(8,128)(2,1)S(1)}, bf16[2,4,96,768]{3,2,1,0:T(8,128)(2,1)S(1)}, u32[]{:S(2)}, u32[]{:S(2)}) collective-permute-start(bf16[2,4,96,768]{3,2,1,0:T(8,128)(2,1)S(1)} %fusion), channel_id=1, source_target_pairs={{0,8},{8,0},{16,24},{24,16},{1,9},{9,1},{17,25},{25,17},{2,10},{10... | collective-permute-start | bytes 3538952 | tf_op jit(solution)/shard_map/ppermute | solution.py:828
  235.2 1.1 copy-start.26
  236.2 30.9 %collective-permute-start.14 = (bf16[16,24,2048]{2,1,0:T(8,128)(2,1)}, bf16[16,24,2048]{2,1,0:T(8,128)(2,1)S(1)}, u32[]{:S(2)}, u32[]{:S(2)}) collective-permute-start(bf16[16,24,2048]{2,1,0:T(8,128)(2,1)} %get-tuple-element.151), channel_id=1, source_target_pairs={{0,4},{4,0},{1,5},{5,1},{2,6},{6,2},{3,7},{7,3},{8,12},{12,8},{9,1... | collective-permute-start | bytes 4718600 | tf_op jit(solution)/shard_map/ppermute | solution.py:828
  238.5 28.6 %collective-permute-start.12 = (bf16[4,96,768]{2,1,0:T(8,128)(2,1)S(1)}, bf16[4,96,768]{2,1,0:T(8,128)(2,1)S(1)}, u32[]{:S(2)}, u32[]{:S(2)}) collective-permute-start(bf16[4,96,768]{2,1,0:T(8,128)(2,1)S(1)} %get-tuple-element.222), channel_id=1, source_target_pairs={{0,16},{8,24},{16,0},{24,8},{1,17},{9,25},{17,1},{25,9},{2,18},{10... | collective-permute-start | bytes 1769480 | tf_op jit(solution)/shard_map/ppermute | solution.py:828
  239.9 27.2 %copy-start.27 = (bf16[2,4,96,768]{3,2,1,0:T(8,128)(2,1)S(1)}, bf16[2,4,96,768]{3,2,1,0:T(8,128)(2,1)}, u32[]{:S(2)}) copy-start(bf16[2,4,96,768]{3,2,1,0:T(8,128)(2,1)} %copy-done.26) | copy-start | bytes 3538948
  240.0 27.1 %collective-permute-start.13 = (bf16[4,96,768]{2,1,0:T(8,128)(2,1)S(1)}, bf16[4,96,768]{2,1,0:T(8,128)(2,1)S(1)}, u32[]{:S(2)}, u32[]{:S(2)}) collective-permute-start(bf16[4,96,768]{2,1,0:T(8,128)(2,1)S(1)} %get-tuple-element.221), channel_id=1, source_target_pairs={{0,8},{8,0},{16,24},{24,16},{1,9},{9,1},{17,25},{25,17},{2,10},{10... | collective-permute-start | bytes 1769480 | tf_op jit(solution)/shard_map/ppermute | solution.py:828
  267.1 4.3 %copy-start.31 = (bf16[16,24,1024]{2,1,0:T(8,128)(2,1)S(1)}, bf16[16,24,1024]{2,1,0:T(8,128)(2,1)}, u32[]{:S(2)}) copy-start(bf16[16,24,1024]{2,1,0:T(8,128)(2,1)} %get-tuple-element.156) | copy-start | bytes 2359300
  269.5 4.7 %copy-start.25 = (bf16[16,24,2048]{2,1,0:T(8,128)(2,1)S(1)}, bf16[16,24,2048]{2,1,0:T(8,128)(2,1)}, u32[]{:S(2)}) copy-start(bf16[16,24,2048]{2,1,0:T(8,128)(2,1)} %get-tuple-element.161) | copy-start | bytes 4718596
  269.6 46.2 %collective-permute-start.22 = (bf16[2,96,768]{2,1,0:T(8,128)(2,1)S(1)}, bf16[2,96,768]{2,1,0:T(8,128)(2,1)S(1)}, u32[]{:S(2)}, u32[]{:S(2)}) collective-permute-start(bf16[2,96,768]{2,1,0:T(8,128)(2,1)S(1)} %pad_maximum_fusion.6), channel_id=1, source_target_pairs={{0,3},{1,2},{2,1},{3,0},{4,7},{5,6},{6,5},{7,4},{8,11},{9,10},{10,... | collective-permute-start | bytes 884744 | tf_op jit(solution)/shard_map/ppermute | solution.py:828
  271.4 13.0 %collective-permute-start.15 = (bf16[16,24,1024]{2,1,0:T(8,128)(2,1)S(1)}, bf16[16,24,1024]{2,1,0:T(8,128)(2,1)S(1)}, u32[]{:S(2)}, u32[]{:S(2)}) collective-permute-start(bf16[16,24,1024]{2,1,0:T(8,128)(2,1)S(1)} %copy-done.31), channel_id=1, source_target_pairs={{0,4},{4,0},{1,5},{5,1},{2,6},{6,2},{3,7},{7,3},{8,12},{12,8},{9,1... | collective-permute-start | bytes 2359304 | tf_op jit(solution)/shard_map/ppermute | solution.py:828
  271.4 44.4 %collective-permute-start.21 = (bf16[2,96,768]{2,1,0:T(8,128)(2,1)S(1)}, bf16[2,96,768]{2,1,0:T(8,128)(2,1)S(1)}, u32[]{:S(2)}, u32[]{:S(2)}) collective-permute-start(bf16[2,96,768]{2,1,0:T(8,128)(2,1)S(1)} %pad_maximum_fusion.5), channel_id=1, source_target_pairs={{0,2},{1,3},{2,0},{3,1},{4,6},{5,7},{6,4},{7,5},{8,10},{9,11},{10,... | collective-permute-start | bytes 884744 | tf_op jit(solution)/shard_map/ppermute | solution.py:828
  272.5 43.3 %collective-permute-start.20 = (bf16[2,96,768]{2,1,0:T(8,128)(2,1)S(1)}, bf16[2,96,768]{2,1,0:T(8,128)(2,1)S(1)}, u32[]{:S(2)}, u32[]{:S(2)}) collective-permute-start(bf16[2,96,768]{2,1,0:T(8,128)(2,1)S(1)} %pad_maximum_fusion.4), channel_id=1, source_target_pairs={{0,1},{1,0},{2,3},{3,2},{4,5},{5,4},{6,7},{7,6},{8,9},{9,8},{10,11... | collective-permute-start | bytes 884744 | tf_op jit(solution)/shard_map/ppermute | solution.py:828
  274.2 1.8 copy-start.12
  274.5 26.5 %collective-permute-start.16 = (bf16[2,4,24,2048]{3,2,1,0:T(8,128)(2,1)S(1)}, bf16[2,4,24,2048]{3,2,1,0:T(8,128)(2,1)S(1)}, u32[]{:S(2)}, u32[]{:S(2)}) collective-permute-start(bf16[2,4,24,2048]{3,2,1,0:T(8,128)(2,1)S(1)} %fusion.4), channel_id=1, source_target_pairs={{0,8},{8,0},{16,24},{24,16},{1,9},{9,1},{17,25},{25,17},{2,10},{10... | collective-permute-start | bytes 2359304 | tf_op jit(solution)/shard_map/ppermute | solution.py:828
  276.0 8.3 %copy-start.28 = (bf16[16,24,1024]{2,1,0:T(8,128)(2,1)S(1)}, bf16[16,24,1024]{2,1,0:T(8,128)(2,1)}, u32[]{:S(2)}) copy-start(bf16[16,24,1024]{2,1,0:T(8,128)(2,1)} %get-tuple-element.163) | copy-start | bytes 2359300
  284.5 16.4 %collective-permute-start.17 = (bf16[2,4,24,1024]{3,2,1,0:T(8,128)(2,1)S(1)}, bf16[2,4,24,1024]{3,2,1,0:T(8,128)(2,1)S(1)}, u32[]{:S(2)}, u32[]{:S(2)}) collective-permute-start(bf16[2,4,24,1024]{3,2,1,0:T(8,128)(2,1)S(1)} %fusion.7), channel_id=1, source_target_pairs={{0,16},{8,24},{16,0},{24,8},{1,17},{9,25},{17,1},{25,9},{2,18},{10... | collective-permute-start | bytes 1179656 | tf_op jit(solution)/shard_map/ppermute | solution.py:828
  301.0 14.8 %collective-permute-start.19 = (bf16[4,24,1024]{2,1,0:T(8,128)(2,1)S(1)}, bf16[4,24,1024]{2,1,0:T(8,128)(2,1)S(1)}, u32[]{:S(2)}, u32[]{:S(2)}) collective-permute-start(bf16[4,24,1024]{2,1,0:T(8,128)(2,1)S(1)} %fusion.8), channel_id=1, source_target_pairs={{0,8},{8,0},{16,24},{24,16},{1,9},{9,1},{17,25},{25,17},{2,10},{10... | collective-permute-start | bytes 589832 | tf_op jit(solution)/shard_map/ppermute | solution.py:828
  302.7 13.1 %collective-permute-start.18 = (bf16[4,24,2048]{2,1,0:T(8,128)(2,1)S(1)}, bf16[4,24,2048]{2,1,0:T(8,128)(2,1)S(1)}, u32[]{:S(2)}, u32[]{:S(2)}) collective-permute-start(bf16[4,24,2048]{2,1,0:T(8,128)(2,1)S(1)} %fusion.5), channel_id=1, source_target_pairs={{0,16},{8,24},{16,0},{24,8},{1,17},{9,25},{17,1},{25,9},{2,18},{10... | collective-permute-start | bytes 1179656 | tf_op jit(solution)/shard_map/ppermute | solution.py:828
  316.1 5.0 %copy-start = (f32[768,96]{0,1:T(8,128)S(1)}, f32[768,96]{0,1:T(8,128)}, u32[]{:S(2)}) copy-start(f32[768,96]{0,1:T(8,128)} %param.35) | copy-start | bytes 884740
  316.1 5.0 %copy-start.1 = (f32[96,768]{1,0:T(8,128)S(1)}, f32[96,768]{1,0:T(8,128)}, u32[]{:S(2)}) copy-start(f32[96,768]{1,0:T(8,128)} %up_ref.1) | copy-start | bytes 884740
  316.1 5.0 %copy-start.4 = (f32[96,768]{1,0:T(8,128)S(1)}, f32[96,768]{1,0:T(8,128)}, u32[]{:S(2)}) copy-start(f32[96,768]{1,0:T(8,128)} %refs_1_.2) | copy-start | bytes 884740
  316.1 5.0 %copy-start.5 = (f32[96,768]{1,0:T(8,128)S(1)}, f32[96,768]{1,0:T(8,128)}, u32[]{:S(2)}) copy-start(f32[96,768]{1,0:T(8,128)} %refs_2_.2) | copy-start | bytes 884740
  316.1 5.0 %copy-start.6 = (f32[768,96]{0,1:T(8,128)S(1)}, f32[768,96]{0,1:T(8,128)}, u32[]{:S(2)}) copy-start(f32[768,96]{0,1:T(8,128)} %param.36) | copy-start | bytes 884740
  316.1 5.0 %copy-start.7 = (f32[768,96]{0,1:T(8,128)S(1)}, f32[768,96]{0,1:T(8,128)}, u32[]{:S(2)}) copy-start(f32[768,96]{0,1:T(8,128)} %param.37) | copy-start | bytes 884740
  316.3 8.6 %collective-permute-start.25 = (bf16[24,3072]{1,0:T(8,128)(2,1)S(1)}, bf16[24,3072]{1,0:T(8,128)(2,1)S(1)}, u32[]{:S(2)}, u32[]{:S(2)}) collective-permute-start(bf16[24,3072]{1,0:T(8,128)(2,1)S(1)} %pad_maximum_fusion.10), channel_id=1, source_target_pairs={{0,3},{1,2},{2,1},{3,0},{4,7},{5,6},{6,5},{7,4},{8,11},{9,10},{10,... | collective-permute-start | bytes 442376 | tf_op jit(solution)/shard_map/ppermute | solution.py:828
  318.1 12.6 %collective-permute-start.24 = (bf16[24,3072]{1,0:T(8,128)(2,1)S(1)}, bf16[24,3072]{1,0:T(8,128)(2,1)S(1)}, u32[]{:S(2)}, u32[]{:S(2)}) collective-permute-start(bf16[24,3072]{1,0:T(8,128)(2,1)S(1)} %pad_maximum_fusion.9), channel_id=1, source_target_pairs={{0,2},{1,3},{2,0},{3,1},{4,6},{5,7},{6,4},{7,5},{8,10},{9,11},{10,... | collective-permute-start | bytes 442376 | tf_op jit(solution)/shard_map/ppermute | solution.py:828
  318.3 12.5 %collective-permute-start.23 = (bf16[24,3072]{1,0:T(8,128)(2,1)S(1)}, bf16[24,3072]{1,0:T(8,128)(2,1)S(1)}, u32[]{:S(2)}, u32[]{:S(2)}) collective-permute-start(bf16[24,3072]{1,0:T(8,128)(2,1)S(1)} %pad_maximum_fusion.8), channel_id=1, source_target_pairs={{0,1},{1,0},{2,3},{3,2},{4,5},{5,4},{6,7},{7,6},{8,9},{9,8},{10,11... | collective-permute-start | bytes 442376 | tf_op jit(solution)/shard_map/ppermute | solution.py:828
  320.9 9.8 %copy-start.3 = (f32[24,768]{1,0:T(8,128)S(1)}, f32[24,768]{1,0:T(8,128)}, u32[]{:S(2)}) copy-start(f32[24,768]{1,0:T(8,128)} %proj_ref.1) | copy-start | bytes 221188
  320.9 9.8 %copy-start.8 = (f32[24,2304]{1,0:T(8,128)S(1)}, f32[24,2304]{1,0:T(8,128)}, u32[]{:S(2)}) copy-start(f32[24,2304]{1,0:T(8,128)} %refs_1_.3) | copy-start | bytes 663556
  321.0 9.8 %copy-start.9 = (f32[24,2304]{1,0:T(8,128)S(1)}, f32[24,2304]{1,0:T(8,128)}, u32[]{:S(2)}) copy-start(f32[24,2304]{1,0:T(8,128)} %refs_2_.3) | copy-start | bytes 663556
  321.0 9.8 %copy-start.11 = (f32[4,8,768]{2,1,0:T(8,128)S(1)}, f32[4,8,768]{2,1,0:T(8,128)}, u32[]{:S(2)}) copy-start(f32[4,8,768]{2,1,0:T(8,128)} %get-tuple-element.180.refs_12_) | copy-start | bytes 294916
  321.0 9.8 %copy-start.13 = (f32[24,768]{1,0:T(8,128)S(1)}, f32[24,768]{1,0:T(8,128)}, u32[]{:S(2)}) copy-start(f32[24,768]{1,0:T(8,128)} %refs_4_.1) | copy-start | bytes 221188
  321.0 9.8 %copy-start.14 = (f32[24,768]{1,0:T(8,128)S(1)}, f32[24,768]{1,0:T(8,128)}, u32[]{:S(2)}) copy-start(f32[24,768]{1,0:T(8,128)} %refs_5_.3) | copy-start | bytes 221188
  321.0 9.8 %copy-start.17 = (f32[8,768]{1,0:T(8,128)S(1)}, f32[8,768]{1,0:T(8,128)}, u32[]{:S(2)}) copy-start(f32[8,768]{1,0:T(8,128)} %get-tuple-element.179.refs_11_) | copy-start | bytes 73732
  321.0 9.8 %copy-start.18 = (f32[8,768]{1,0:T(8,128)S(1)}, f32[8,768]{1,0:T(8,128)}, u32[]{:S(2)}) copy-start(f32[8,768]{1,0:T(8,128)} %get-tuple-element.178.refs_10_) | copy-start | bytes 73732
  322.7 28.2 %copy-start.15 = (f32[7,768]{1,0:T(8,128)S(1)}, f32[7,768]{1,0:T(8,128)}, u32[]{:S(2)}) copy-start(f32[7,768]{1,0:T(8,128)} %vec_one.1) | copy-start | bytes 64516
  322.7 28.2 %copy-start.16 = (f32[7,768]{1,0:T(8,128)S(1)}, f32[7,768]{1,0:T(8,128)}, u32[]{:S(2)}) copy-start(f32[7,768]{1,0:T(8,128)} %vec_two.1) | copy-start | bytes 64516
  322.7 28.2 %copy-start.19 = (f32[3072]{0:T(1024)S(1)}, f32[3072]{0:T(1024)}, u32[]{:S(2)}) copy-start(f32[3072]{0:T(1024)} %param.38) | copy-start | bytes 36868
  322.7 28.2 %copy-start.20 = (f32[3072]{0:T(1024)S(1)}, f32[3072]{0:T(1024)}, u32[]{:S(2)}) copy-start(f32[3072]{0:T(1024)} %param.39) | copy-start | bytes 36868
  322.7 28.2 %copy-start.21 = (f32[3072]{0:T(1024)S(1)}, f32[3072]{0:T(1024)}, u32[]{:S(2)}) copy-start(f32[3072]{0:T(1024)} %param.40) | copy-start | bytes 36868
  331.9 1.2 collective-permute-start.26
  333.2 4.2 %collective-permute-start.27 = (f32[16,768]{1,0:T(8,128)S(1)}, f32[16,768]{1,0:T(8,128)S(1)}, u32[]{:S(2)}, u32[]{:S(2)}) collective-permute-start(f32[16,768]{1,0:T(8,128)S(1)} %add.635), channel_id=1, source_target_pairs={{0,8},{8,0},{16,24},{24,16},{1,9},{9,1},{17,25},{25,17},{2,10},{10... | collective-permute-start | bytes 147464 | tf_op jit(solution)/shard_map/ppermute | solution.py:828
  337.3 4.1 %collective-permute-start.28 = (f32[16,768]{1,0:T(8,128)S(1)}, f32[16,768]{1,0:T(8,128)S(1)}, u32[]{:S(2)}, u32[]{:S(2)}) collective-permute-start(f32[16,768]{1,0:T(8,128)S(1)} %add.636), channel_id=1, source_target_pairs={{0,16},{8,24},{16,0},{24,8},{1,17},{9,25},{17,1},{25,9},{2,18},{10... | collective-permute-start | bytes 147464 | tf_op jit(solution)/shard_map/ppermute | solution.py:828
  341.5 4.2 %collective-permute-start.29 = (f32[16,768]{1,0:T(8,128)S(1)}, f32[16,768]{1,0:T(8,128)S(1)}, u32[]{:S(2)}, u32[]{:S(2)}) collective-permute-start(f32[16,768]{1,0:T(8,128)S(1)} %add.637), channel_id=1, source_target_pairs={{0,1},{1,0},{2,3},{3,2},{4,5},{5,4},{6,7},{7,6},{8,9},{9,8},{10,11... | collective-permute-start | bytes 147464 | tf_op jit(solution)/shard_map/ppermute | solution.py:828
  345.7 5.2 %collective-permute-start.30 = (f32[16,768]{1,0:T(8,128)S(1)}, f32[16,768]{1,0:T(8,128)S(1)}, u32[]{:S(2)}, u32[]{:S(2)}) collective-permute-start(f32[16,768]{1,0:T(8,128)S(1)} %add.638), channel_id=1, source_target_pairs={{0,2},{1,3},{2,0},{3,1},{4,6},{5,7},{6,4},{7,5},{8,10},{9,11},{10,... | collective-permute-start | bytes 147464 | tf_op jit(solution)/shard_map/ppermute | solution.py:828
Sparse Core Ops, SparseCore 0:
  11.4 96.7 all-gather.1
